TPU v7x, 128 devices: a whole 4x4x4 slice. The times are simulated.
128 devices in a mesh: section: 8 (over z, x_lo), tp: 16 (over y, x_hi, core).
Axes of the slice: x: 4 (x_hi: 2, x_lo: 2; x = x_hi * 2 + x_lo), y: 4, z: 4, core: 2. Of those that a mesh axis runs over, the one named last changes fastest.
Arguments:
- teacher_rows: bfloat16 [8, 256, 8192], P('section', 'tp'), may hold values from -72 to 72
- norm_gain: float32 [8, 8192], P('section'), may hold values from 0.1 to 1.9
- query_weight: bfloat16 [8, 8192, 8192], P('section', None, 'tp'), may hold values from -2.762136 to 2.762136
- keys_values: bfloat16 [8, 2, 8192, 1024], P('section', None, None, 'tp'), may hold values from -0.071815532 to 0.071815532
- output_weight: bfloat16 [8, 8192, 8192], P('section', 'tp'), may hold values from -0.5 to 0.5
- doc_start: int32 [8], P('section'), may hold values from 1 to 255
- student_rows: bfloat16 [8, 256, 4096], P('section', 'tp'), may hold values from -30 to 30
- projector: bfloat16 [4096, 8192], P('tp', 'section'), may hold values from -1 to 2
Outputs:
- teacher_next: bfloat16 [8, 256, 8192], P('section', 'tp')
- distill_loss: float32 [], replicated
- grad_student: float32 [8, 256, 4096], P('section', 'tp')
- grad_projector: float32 [4096, 8192], P('tp', 'section')
All inputs are finite; a program needn't handle non-finite values.
Results may differ from a plain program's by a relative error of at most 0.02.
Values may be sent and summed in bfloat16 or wider, within the bound.
No kernel may reach another device: no remote copies, remote signals or barrier semaphores. Data moves between devices by JAX's collectives and lax.ppermute only.
A program may use at most 128 MiB of HBM per device.

v0:
```python
import math

import jax
import jax.numpy as jnp
from jax import lax
from jax.sharding import PartitionSpec as P

HD = 128


LOSS_WEIGHT = 64.0
NORM_EPS = 1e-05
COS_EPS = 1e-06


def partner(value, axis, apart):
    mask = 2**apart
    pairs = [(source, source ^ mask) for source in range(lax.axis_size(axis))]
    return lax.ppermute(value, axis, pairs)


def from_everyone(value, axis):
    copies = jnp.broadcast_to(value, (lax.axis_size(axis), *value.shape))
    return lax.all_to_all(copies, axis, split_axis=0, concat_axis=0, tiled=True)


def laid_out(pieces, dim):
    pieces = jnp.moveaxis(pieces, 0, dim)
    shape = pieces.shape
    return pieces.reshape(*shape[:dim], shape[dim] * shape[dim + 1], *shape[dim + 2 :])


def collect(value, axis, dim):
    pieces = from_everyone(value, axis)
    return laid_out(pieces, dim)


def taken_together(value, axis):
    everything = from_everyone(value, axis)
    return jnp.sum(everything, axis=0)


def packed_total(arrays, axis):
    ends = [0]
    for a in arrays:
        ends.append(ends[-1] + a.size)
    subtotal = taken_together(jnp.concatenate([a.ravel() for a in arrays]), axis)
    return tuple((subtotal[b:e].reshape(a.shape) for a, b, e in zip(arrays, ends, ends[1:])))


def cut_along(value, dim, length):
    shape = value.shape
    pieces = value.reshape(*shape[:dim], length, shape[dim] // length, *shape[dim + 1 :])
    return jnp.moveaxis(pieces, dim, 0)


def sent_and_summed(value, axis, dim):
    pieces = cut_along(value, dim, lax.axis_size(axis))
    arrived = lax.all_to_all(pieces, axis, split_axis=0, concat_axis=0, tiled=True)
    return arrived.astype(jnp.float32).sum(axis=0)


def round_bf16(values):
    return lax.optimization_barrier(values.astype(jnp.bfloat16)).astype(jnp.float32)


def join_halves(mine, other, low_side):
    return jnp.where(
        low_side, jnp.concatenate([mine, other], axis=1), jnp.concatenate([other, mine], axis=1)
    )


def cosine_step(inner, own_sq, target_sq, student_proj, target):
    inv_own = lax.rsqrt(own_sq + COS_EPS)
    inv_target = lax.rsqrt(target_sq + COS_EPS)
    cosine = inner * inv_own * inv_target
    slope = LOSS_WEIGHT * (
        (inner * inv_target * inv_own * inv_own * inv_own)[:, None] * student_proj
        - target * (inv_own * inv_target)[:, None]
    )
    return (cosine, slope.astype(jnp.bfloat16))


def attend(queries, keys_full, values_full, first_new):
    row_total = queries.shape[0]
    kv_heads = keys_full.shape[1] // HD
    group = queries.shape[1] // HD // kv_heads
    query_heads = queries.reshape(row_total, kv_heads, group, HD)
    key_heads = keys_full.reshape(row_total, kv_heads, HD)
    value_heads = values_full.reshape(row_total, kv_heads, HD)
    scale = 1.0 / math.sqrt(HD)
    scores = (
        jnp.einsum("qegd,ked->egqk", query_heads, key_heads, preferred_element_type=jnp.float32)
        * scale
    )
    positions = jnp.arange(row_total, dtype=jnp.int32)
    after_start = positions >= first_new
    visible = (positions[None, :] <= positions[:, None]) & (
        after_start[None, :] == after_start[:, None]
    )
    scores = jnp.where(visible, scores, -1e30)
    row_max = jnp.max(scores, axis=-1, keepdims=True)
    expo = jnp.where(visible, jnp.exp(scores - row_max), 0.0)
    weights = (expo / jnp.sum(expo, axis=-1, keepdims=True)).astype(jnp.bfloat16)
    mixed = jnp.einsum("egqk,ked->qegd", weights, value_heads, preferred_element_type=jnp.float32)
    return mixed.astype(jnp.bfloat16).reshape(row_total, queries.shape[1])


def shards(
    teacher_rows,
    norm_gain,
    query_weight,
    keys_values,
    output_weight,
    doc_start,
    student_rows,
    projector,
):
    span_rows = teacher_rows[0]
    tp_count = lax.axis_size("tp")
    tp_position = lax.axis_index("tp")
    rows_float = span_rows.astype(jnp.float32)
    mean_square = jnp.mean(rows_float * rows_float, axis=1, keepdims=True)
    normed = (rows_float * lax.rsqrt(mean_square + NORM_EPS) * norm_gain[0][None, :]).astype(
        jnp.bfloat16
    )
    query_local = query_weight[0]
    key_local = keys_values[0, 0]
    value_local = keys_values[0, 1]
    query_cols = query_local.shape[1]
    key_cols = key_local.shape[1]
    block_rows = lax.all_gather(normed, "tp", axis=0, tiled=True)
    query_part = jnp.dot(block_rows, query_local, preferred_element_type=jnp.float32).astype(
        jnp.bfloat16
    )
    key_part = jnp.dot(block_rows, key_local, preferred_element_type=jnp.float32).astype(
        jnp.bfloat16
    )
    value_part = jnp.dot(block_rows, value_local, preferred_element_type=jnp.float32).astype(
        jnp.bfloat16
    )
    projected = jnp.concatenate([query_part, key_part, value_part], axis=1)
    queries = projected[:, :query_cols]
    keys_full = projected[:, query_cols : query_cols + key_cols]
    values_full = projected[:, query_cols + key_cols :]
    other_key, other_value = partner((keys_full, values_full), "tp", 0)
    low_side = tp_position // 2**0 % 2 == 0
    keys_full = join_halves(keys_full, other_key, low_side)
    values_full = join_halves(values_full, other_value, low_side)
    mixed_heads = attend(queries, keys_full, values_full, doc_start[0])
    out_local = output_weight[0]
    block = mixed_heads
    attn_sum = lax.psum_scatter(
        round_bf16(jnp.dot(block, out_local, preferred_element_type=jnp.float32)).astype(
            jnp.bfloat16
        ),
        "tp",
        scatter_dimension=0,
        tiled=True,
    ).astype(jnp.float32)
    teacher_next = (rows_float + attn_sum).astype(jnp.bfloat16)
    contract_last = (((1,), (1,)), ((), ()))
    contract_pair = (((0, 1), (0, 1)), ((), ()))
    gathered = collect(student_rows, "section", 0)
    token_count = gathered.shape[0] * gathered.shape[1]
    token_rows = gathered.reshape(token_count, gathered.shape[2])
    arrived = lax.all_to_all(teacher_next[None], "section", split_axis=2, concat_axis=0, tiled=True)
    target = arrived.reshape(token_count, arrived.shape[2]).astype(jnp.float32)
    proj_block = lax.all_gather(projector, "tp", axis=0, tiled=True)
    student_proj = jnp.dot(token_rows, proj_block, preferred_element_type=jnp.float32)
    inner, own_sq, target_sq = packed_total(
        (
            jnp.sum(student_proj * target, axis=1),
            jnp.sum(student_proj * student_proj, axis=1),
            jnp.sum(target * target, axis=1),
        ),
        "section",
    )
    cosine, slope = cosine_step(inner, own_sq, target_sq, student_proj, target)
    loss_total = taken_together(jnp.sum(1.0 - cosine), "tp")
    distill_loss = loss_total / (token_count * tp_count)
    block = slope
    grad_local = sent_and_summed(
        lax.dot_general(
            block, proj_block, contract_last, preferred_element_type=jnp.float32
        ).astype(jnp.bfloat16),
        "section",
        0,
    )
    by_column = lax.all_to_all(gathered, "tp", split_axis=2, concat_axis=1, tiled=True)
    slope_stacked = slope.reshape(gathered.shape[0], gathered.shape[1], slope.shape[1])
    block = by_column
    grad_proj = lax.dot_general(
        block,
        lax.all_gather(slope_stacked, "tp", axis=1, tiled=True),
        contract_pair,
        preferred_element_type=jnp.float32,
    )
    return (teacher_next[None], distill_loss, grad_local[None], grad_proj)


def solution(mesh):
    placed = (
        P("section", "tp", None),
        P("section", None),
        P("section", None, "tp"),
        P("section", None, None, "tp"),
        P("section", "tp", None),
        P("section"),
        P("section", "tp", None),
        P("tp", "section"),
    )
    return jax.shard_map(
        shards,
        mesh=mesh,
        in_specs=placed,
        out_specs=(P("section", "tp", None), P(), P("section", "tp", None), P("tp", "section")),
        check_vma=False,
    )
```

profile of v0, /device:TPU:1, one launch (start us, length us, event | category | flops | bytes accessed | tf_op | source)
XLA Modules:
  0.0 376.0 jit_solution(13403994111314197012)
XLA Ops:
  11.2 58.2 %all-gather.4.cloned.1.call-done = bf16[256,8192]{1,0:T(8,128)(2,1)} async-done(((bf16[16,8192]{1,0:T(8,128)(2,1)}), bf16[256,8192]{1,0:T(8,128)(2,1)}) %all-gather.4.cloned.1.call-update) | async-done | bytes 4194320 | tf_op jit(solution)/shard_map/all_gather | solution.py:132
  69.4 4.0 %convolution_convert_fusion.3 = bf16[256,64]{0,1:T(8,128)(2,1)S(1)} fusion(bf16[256,8192]{1,0:T(8,128)(2,1)} %all-gather.4.cloned.1.call-done, bf16[1,2,8192,64]{2,3,1,0:T(8,128)(2,1)} %param.11), kind=kOutput, calls=%fused_computation.13 | convolution fusion | flops 268451840 | bytes 5275648 | tf_op jit(solution)/shard_map/dot_general | solution.py:136
  75.5 5.8 %fusion.8 = bf16[32,4,8,128]{3,2,1,0:T(8,128)(2,1)S(1)} fusion(bf16[256,8192]{1,0:T(8,128)(2,1)S(1)} %copy-done, bf16[1,8192,512]{2,1,0:T(8,128)(2,1)} %param.10), kind=kOutput, calls=%fused_computation.12 | convolution fusion | flops 2147614720 | bytes 12845056 | tf_op jit(solution)/shard_map/dot_general | solution.py:133
  82.4 4.5 %convolution_convert_fusion = bf16[256,8192]{1,0:T(8,128)(2,1)} fusion(bf16[256,512]{0,1:T(8,128)(2,1)S(1)} %bitcast.115, bf16[1,512,8192]{2,1,0:T(8,128)(2,1)S(1)} %bitcast.111), kind=kOutput, calls=%fused_computation | convolution fusion | flops 2149580800 | bytes 12845056 | tf_op jit(solution)/shard_map/dot_general | solution.py:154
  87.6 76.1 %reduce-scatter.2.cloned.1.call-done = bf16[16,8192]{1,0:T(8,128)(2,1)} async-done(((bf16[256,8192]{1,0:T(8,128)(2,1)}), bf16[16,8192]{1,0:T(8,128)(2,1)}) %reduce-scatter.2.cloned.1.call-update) | async-done | bytes 262160 | tf_op jit(solution)/shard_map/reduce_scatter | solution.py:153
  164.7 6.8 %copy.48 = bf16[1,16,8192]{1,0,2:T(2,128)(2,1)} copy(bf16[1,16,8192]{2,1,0:T(8,128)(2,1)S(1)} %fusion.26) | data formatting | bytes 524288 | tf_op jit(solution)/shard_map/broadcast_in_dim | solution.py:199
  172.0 45.2 %reduce.8 = bf16[8192,16]{1,0:T(8,128)(2,1)S(1)} reduce(bf16[8192,1,16]{2,1,0:T(2,128)(2,1)} %bitcast.106, bf16[]{:T(256)} %broadcast.68), dimensions={1}, to_apply=%bitcast.82.reduce_sub_computation | reduce | bytes 524290
  219.5 10.6 %all_to_all.49 = bf16[8,2,8192]{2,1,0:T(2,128)(2,1)S(1)} all-to-all(bf16[8,2,8192]{2,1,0:T(2,128)(2,1)S(1)} %reshape.123), channel_id=1, replica_groups=mesh['section'=8,'tp'=16] {'section'}, dimensions={0} | all-to-all | bytes 524288 | tf_op jit(solution)/shard_map/all_to_all | solution.py:167
  231.2 3.6 all-to-all-start
  234.8 5.1 %reshape.124 = bf16[8192,1,16]{2,1,0:T(2,128)(2,1)} reshape(bf16[8,2,8192]{2,1,0:T(2,128)(2,1)S(1)} %all_to_all.49) | data formatting | bytes 524288
  239.9 8.5 %convert_multiply_fusion.2 = f32[1,16,8192]{1,0,2:T(1,128)} fusion(bf16[8192,1,16]{2,1,0:T(2,128)(2,1)} %reshape.124), kind=kLoop, calls=%fused_computation.68 | loop fusion | flops 262144 | bytes 786432 | tf_op jit(solution)/shard_map/mul | solution.py:175
  250.9 8.5 %bitcast_convert_fusion = f32[1,16,8192]{1,0,2:T(1,128)} fusion(bf16[8192,1,16]{2,1,0:T(2,128)(2,1)} %reshape.124), kind=kLoop, calls=%fused_computation.72 | loop fusion | flops 131072 | bytes 786432 | tf_op jit(solution)/shard_map/convert_element_type | solution.py:168
  259.4 2.8 copy.49
  262.2 4.7 %fusion.20 = (f32[128]{0:T(128)S(1)}, f32[128]{0:T(128)S(1)}, f32[128,1024]{1,0:T(8,128)S(1)}) fusion(f32[1,16,8,1024]{3,1,2,0:T(8,128)S(1)} %copy.49, bf16[128,4096]{1,0:T(8,128)(2,1)S(1)} %bitcast.108, bf16[4096,1024]{1,0:T(8,128)(2,1)} %all-gather.6.cloned.1.call-done), kind=kOutput, calls=%fused_computation.31 | convolution fusion | flops 1074265856 | bytes 10486784 | tf_op jit(solution)/shard_map/dot_general | solution.py:170
  267.0 9.9 %all_to_all.50 = f32[8,1,384]{2,1,0:T(1,128)S(1)} all-to-all(f32[8,1,384]{2,1,0:T(1,128)S(1)} %broadcast_in_dim.42), channel_id=1, replica_groups=mesh['section'=8,'tp'=16] {'section'}, dimensions={0} | all-to-all | bytes 24576 | tf_op jit(solution)/shard_map/all_to_all | solution.py:24
  278.3 7.3 %copy.54 = bf16[8,16,4096]{1,0,2:T(8,128)(2,1)} copy(bf16[8,16,4096]{2,1,0:T(8,128)(2,1)S(1)} %bitcast.109) | data formatting | bytes 2097152 | tf_op jit(solution)/shard_map/reshape | solution.py:30
  285.7 10.5 %reshape.125 = bf16[16,2,16384]{2,1,0:T(2,128)(2,1)S(1)} reshape(bf16[4096,8,16]{2,1,0:T(8,128)(2,1)} %bitcast.103) | data formatting | bytes 2097152
  296.2 31.7 %all_to_all.51 = bf16[16,2,16384]{2,1,0:T(2,128)(2,1)S(1)} all-to-all(bf16[16,2,16384]{2,1,0:T(2,128)(2,1)S(1)} %reshape.125), channel_id=1, replica_groups=mesh['section'=8,'tp'=16] {'tp'}, dimensions={0} | all-to-all | bytes 2097152 | tf_op jit(solution)/shard_map/all_to_all | solution.py:190
  329.1 5.7 %all-to-all-start.3 = ((f32[16,1,1]{2,1,0:T(1,128)}), f32[16,1,1]{2,1,0:T(1,128)S(1)}, u32[]{:S(2)}, u32[]{:S(2)}) async-start(f32[16,1,1]{2,1,0:T(1,128)} %broadcast_in_dim.43), calls=%async_computation.4 | async-start | bytes 16384 | tf_op jit(solution)/shard_map/all_to_all | solution.py:24
  334.8 7.2 %convolution_convert_fusion.1 = bf16[128,4096]{1,0:T(8,128)(2,1)} fusion(bf16[128,1024]{1,0:T(8,128)(2,1)S(1)} %copy-done.2, bf16[4096,1024]{1,0:T(8,128)(2,1)} %all-gather.6.cloned.1.call-done), kind=kOutput, calls=%fused_computation.4 | convolution fusion | flops 1074266112 | bytes 9699328 | tf_op jit(solution)/shard_map/dot_general | solution.py:184
  342.0 3.6 all-to-all-start.4
  345.6 7.5 %reshape.126 = bf16[4096,8,16]{2,1,0:T(8,128)(2,1)} reshape(bf16[16,2,16384]{2,1,0:T(2,128)(2,1)S(1)} %all_to_all.51) | data formatting | bytes 2097152
  353.1 8.3 %copy.56 = bf16[8,16,16,256]{3,2,1,0:T(8,128)(2,1)S(1)} copy(bf16[8,16,16,256]{2,0,3,1:T(8,128)(2,1)} %bitcast.104) | data formatting | bytes 2097152 | tf_op jit(solution)/shard_map/all_to_all | solution.py:190
  363.5 3.5 convolution_bitcast_fusion
  (58 shorter events, 20.0 us)
Async XLA Ops:
  7.2 66.6 %copy-start.3 = (bf16[1,2,8192,64]{2,3,1,0:T(8,128)(2,1)S(1)}, bf16[1,2,8192,64]{2,3,1,0:T(8,128)(2,1)}, u32[]{:S(2)}) copy-start(bf16[1,2,8192,64]{2,3,1,0:T(8,128)(2,1)} %param.11) | copy-start | bytes 6291460
  7.2 62.2 %all-gather.4.cloned.1.call-start = ((), (), s32[]{:S(2)}) async-start(), calls=%async_computation.7 | async-start | bytes 4456448 | tf_op jit(solution)/shard_map/all_gather | solution.py:132
  10.3 153.4 %reduce-scatter.2.cloned.1.call-start = ((), (), s32[]{:S(2)}) async-start(), calls=%async_computation.8 | async-start | bytes 4456448 | tf_op jit(solution)/shard_map/reduce_scatter | solution.py:153
  69.4 4.4 %copy-start = (bf16[256,8192]{1,0:T(8,128)(2,1)S(1)}, bf16[256,8192]{1,0:T(8,128)(2,1)}, u32[]{:S(2)}) copy-start(bf16[256,8192]{1,0:T(8,128)(2,1)} %all-gather.4.cloned.1.call-done) | copy-start | bytes 12582916
  73.4 7.9 %collective-permute-start.1 = (bf16[256,64]{0,1:T(8,128)(2,1)S(1)}, bf16[256,64]{0,1:T(8,128)(2,1)S(1)}, u32[]{:S(2)}, u32[]{:S(2)}) collective-permute-start(bf16[256,64]{0,1:T(8,128)(2,1)S(1)} %convolution_convert_fusion.3), channel_id=1, source_target_pairs={{0,1},{1,0},{2,3},{3,2},{4,5},{5,4},{6,7},{7,6},{8,9},{9,8},{10,11... | collective-permute-start | bytes 98312 | tf_op jit(solution)/shard_map/ppermute | solution.py:19
  73.8 8.6 %slice-start = ((s8[8388608]{0:T(1024)(128)(4,1)}), s8[4194304]{0:T(1024)(128)(4,1)S(1)}, s32[]{:S(2)}) async-start(s8[8388608]{0:T(1024)(128)(4,1)} %bitcast.110), calls=%async_computation.11 | async-start | bytes 8388608
  75.2 7.2 %slice-start.1 = ((s8[8388608]{0:T(1024)(128)(4,1)}), s8[4194304]{0:T(1024)(128)(4,1)S(1)}, s32[]{:S(2)}) async-start(s8[8388608]{0:T(1024)(128)(4,1)} %bitcast.110), calls=%async_computation.12 | async-start | bytes 8388608
  75.2 6.8 %collective-permute-start = (bf16[256,64]{0,1:T(8,128)(2,1)S(1)}, bf16[256,64]{0,1:T(8,128)(2,1)S(1)}, u32[]{:S(2)}, u32[]{:S(2)}) collective-permute-start(bf16[256,64]{0,1:T(8,128)(2,1)S(1)} %convolution_convert_fusion.4), channel_id=1, source_target_pairs={{0,1},{1,0},{2,3},{3,2},{4,5},{5,4},{6,7},{7,6},{8,9},{9,8},{10,11... | collective-permute-start | bytes 98312 | tf_op jit(solution)/shard_map/ppermute | solution.py:19
  86.9 76.8 %copy-start.1 = (bf16[1,16,8192]{2,1,0:T(8,128)(2,1)S(1)}, bf16[1,16,8192]{2,1,0:T(8,128)(2,1)}, u32[]{:S(2)}) copy-start(bf16[1,16,8192]{2,1,0:T(8,128)(2,1)} %param.8) | copy-start | bytes 786436
  86.9 175.3 %all-gather.6.cloned.1.call-start = ((), (), s32[]{:S(2)}) async-start(), calls=%async_computation.9 | async-start | bytes 8912896 | tf_op jit(solution)/shard_map/all_gather | solution.py:169
  164.7 52.5 %copy-start.4 = (bf16[1,16,8192]{2,1,0:T(8,128)(2,1)}, bf16[1,16,8192]{2,1,0:T(8,128)(2,1)S(1)}, u32[]{:S(2)}) copy-start(bf16[1,16,8192]{2,1,0:T(8,128)(2,1)S(1)} %fusion.26) | copy-start | bytes 786436
  172.0 58.1 %copy-start.5 = (bf16[1,16,4096]{2,1,0:T(8,128)(2,1)S(1)}, bf16[1,16,4096]{2,1,0:T(8,128)(2,1)}, u32[]{:S(2)}) copy-start(bf16[1,16,4096]{2,1,0:T(8,128)(2,1)} %param.14) | copy-start | bytes 393220
  231.2 31.0 %all-to-all-start = ((bf16[8,1,16,4096]{3,2,1,0:T(8,128)(2,1)}), bf16[8,1,16,4096]{3,2,1,0:T(8,128)(2,1)S(1)}, u32[]{:S(2)}, u32[]{:S(2)}) async-start(bf16[8,1,16,4096]{3,2,1,0:T(8,128)(2,1)} %broadcast_in_dim.41), calls=%async_computation.1 | async-start | bytes 2097152 | tf_op jit(solution)/shard_map/all_to_all | solution.py:24
  234.7 128.8 %all-gather.8.cloned.1.call-start = ((), (), s32[]{:S(2)}) async-start(), calls=%async_computation.10 | async-start | bytes 4456448 | tf_op jit(solution)/shard_map/all_gather | solution.py:195
  285.7 49.1 %copy-start.2 = (bf16[128,1024]{1,0:T(8,128)(2,1)S(1)}, bf16[128,1024]{1,0:T(8,128)(2,1)}, u32[]{:S(2)}) copy-start(bf16[128,1024]{1,0:T(8,128)(2,1)} %fusion.23) | copy-start | bytes 786436
  329.1 12.9 %all-to-all-start.3 = ((f32[16,1,1]{2,1,0:T(1,128)}), f32[16,1,1]{2,1,0:T(1,128)S(1)}, u32[]{:S(2)}, u32[]{:S(2)}) async-start(f32[16,1,1]{2,1,0:T(1,128)} %broadcast_in_dim.43), calls=%async_computation.4 | async-start | bytes 16384 | tf_op jit(solution)/shard_map/all_to_all | solution.py:24
  342.0 20.7 %all-to-all-start.4 = ((bf16[8,16,4096]{2,1,0:T(8,128)(2,1)}), bf16[8,16,4096]{2,1,0:T(8,128)(2,1)S(1)}, u32[]{:S(2)}, u32[]{:S(2)}) async-start(bf16[8,16,4096]{2,1,0:T(8,128)(2,1)} %bitcast.25), calls=%async_computation.5 | async-start | bytes 2097152 | tf_op jit(solution)/shard_map/all_to_all | solution.py:59
Sparse Core Ops, SparseCore 0:
  11.0 58.3 all-gather.3
  87.0 76.6 reduce-scatter.1
  166.2 73.9 all-gather.5
  278.5 63.0 all-gather.7
where the time goes:
time: 377 us; the launch traced here: 376 us
  waiting for transfers between devices  135 us (36%)
  other arithmetic  72 us (19%)
  local copies, waits for them, and re-layouts  54.7 us (15%)
  blocking collectives  52.1 us (14%)
  matrix products  32 us (8%)
  between operations  16.4 us (4%)
  starting transfers between devices  13.8 us (4%)
    reduce_scatter x1, waiting for transfers between devices, shards(): lax.psum_scatter(round_bf16(jnp.dot(block, out_local, preferred_element_t...  76.1 us
    all_gather x1, waiting for transfers between devices, shards(): block_rows = lax.all_gather(normed, 'tp', axis=0, tiled=True)  58.2 us
    unnamed x2, other arithmetic  45.3 us
    all_to_all x1, blocking collectives, shards(): lax.all_to_all(gathered, 'tp', split_axis=2, concat_axis=1, tiled=True)  31.7 us
    unnamed x22, local copies, waits for them, and re-layouts  27.2 us
    all_to_all x1, blocking collectives, shards(): lax.all_to_all(teacher_next[None], 'section', split_axis=2, concat_axis=0...  10.6 us
    all_to_all x1, blocking collectives, from_everyone(): return lax.all_to_all(copies, axis, split_axis=0, concat_axis=0, tiled=True)  9.85 us
    all_to_all x2, starting transfers between devices, from_everyone(): return lax.all_to_all(copies, axis, split_axis=0, concat_axis=0, tiled=True)  9.24 us
  transfers between devices with their start and end apart: 9, of which 2 were waited for; matrix products, arithmetic and copies ran while one was open for 36% of the time, Pallas kernels for 0%

commit v1 on v0

v1 whole, which is shorter than its diff:
```python
import functools
import math

import jax
import jax.numpy as jnp
from jax import lax
from jax.experimental import pallas as pl
from jax.experimental.pallas import tpu as pltpu
from jax.sharding import Mesh
from jax.sharding import PartitionSpec as P

HD = 128
LOSS_WEIGHT = 64.0
NORM_EPS = 1e-05
COS_EPS = 1e-06
CARRY = 128
SEC = ("z", "xl")
TP = ("y", "xh", "c")

VM = pl.BlockSpec(memory_space=pltpu.VMEM)
SM = pl.BlockSpec(memory_space=pltpu.SMEM)
FAR = pl.BlockSpec(memory_space=pltpu.HBM)


def exchange(pieces, axes):
    return lax.all_to_all(pieces, axes, split_axis=0, concat_axis=0, tiled=True)


def swap(value, axis, apart=1):
    count = lax.axis_size(axis)
    return lax.ppermute(value, axis, [(i, i ^ apart) for i in range(count)])


def f32(value):
    return value.astype(jnp.float32)


def kernel_params(mib):
    return pltpu.CompilerParams(vmem_limit_bytes=mib * 2**20)


def far(value):
    return pltpu.with_memory_space_constraint(value, pltpu.HBM)


def fetched(sources, targets, sems):
    copies = [
        pltpu.make_async_copy(s, t, sems.at[i]) for i, (s, t) in enumerate(zip(sources, targets))
    ]
    for copy in copies:
        copy.start()
    return copies


def norm_kernel(x_ref, gain_ref, o_ref):
    x = f32(x_ref[...])
    mean_square = jnp.mean(x * x, axis=1, keepdims=True)
    o_ref[...] = (x * lax.rsqrt(mean_square + NORM_EPS) * gain_ref[...]).astype(jnp.bfloat16)


def normalize(x, gain):
    return pl.pallas_call(
        norm_kernel,
        out_shape=jax.ShapeDtypeStruct(x.shape, jnp.bfloat16),
        in_specs=[VM, VM],
        out_specs=VM,
        compiler_params=kernel_params(4),
        cost_estimate=pl.CostEstimate(
            flops=20 * x.size, bytes_accessed=320 * x.size, transcendentals=x.shape[0]
        ),
        name="normalize",
    )(x, gain)


def attention_kernel(n_shards, chunk, sc_ref, *refs):
    shard_refs = refs[:n_shards]
    wq_hbm, kva_hbm, kvb_hbm, o_ref, q_acc, kv_acc, wq_ref, kva_ref, kvb_ref, sems = refs[n_shards:]
    per, depth = shard_refs[0].shape
    rows = n_shards * per
    half = rows // 2
    dh = kva_ref.shape[1]
    steps = depth // chunk

    def fetch(step):
        cut = pl.ds(pl.multiple_of(step * chunk, chunk), chunk)
        return (
            pltpu.make_async_copy(wq_hbm.at[cut, :], wq_ref.at[cut, :], sems.at[0, step]),
            pltpu.make_async_copy(kva_hbm.at[:, :, cut], kva_ref.at[:, :, cut], sems.at[1, step]),
            pltpu.make_async_copy(kvb_hbm.at[:, :, cut], kvb_ref.at[:, :, cut], sems.at[2, step]),
        )

    for step in range(steps):
        for copy in fetch(step):
            copy.start()
    q_acc[...] = jnp.zeros_like(q_acc)
    kv_acc[...] = jnp.zeros_like(kv_acc)

    @pl.loop(0, steps)
    def _(step):
        for copy in fetch(step):
            copy.wait()
        cut = pl.ds(pl.multiple_of(step * chunk, chunk), chunk)
        x = jnp.concatenate([r[:, cut] for r in shard_refs], axis=0)
        wkv = jnp.concatenate(
            [kva_ref[0, :, cut], kvb_ref[0, :, cut], kva_ref[1, :, cut], kvb_ref[1, :, cut]],
            axis=0,
        )
        q_acc[...] += jnp.dot(x, wq_ref[cut, :], preferred_element_type=jnp.float32)
        kv_acc[...] += lax.dot_general(
            x, wkv, (((1,), (1,)), ((), ())), preferred_element_type=jnp.float32
        )

    core, xh, y, first_new = sc_ref[0], sc_ref[1], sc_ref[2], sc_ref[3]
    low = core == 0
    keys = kv_acc[:, :HD]
    values = kv_acc[:, HD:]
    keys = jnp.where(low, keys, pltpu.roll(keys, dh, axis=1)).astype(jnp.bfloat16)
    values = jnp.where(low, values, pltpu.roll(values, dh, axis=1)).astype(jnp.bfloat16)

    def place(shape, dim):
        i = lax.broadcasted_iota(jnp.int32, shape, dim)
        side = jnp.where(i < half, 1 - core, core)
        chip_x = ((i >> 6) & 1) ^ xh
        chip_y = ((i >> 4) & 3) ^ y
        return (chip_y * 4 + chip_x * 2 + side) * per + (i & (per - 1))

    row, col = place((rows, rows), 0), place((rows, rows), 1)
    visible = (col <= row) & ((col >= first_new) == (row >= first_new))
    scale = 1.0 / math.sqrt(HD)
    for h in range(q_acc.shape[1] // HD):
        head = slice(h * HD, (h + 1) * HD)
        q = q_acc[:, head].astype(jnp.bfloat16)
        scores = (
            lax.dot_general(q, keys, (((1,), (1,)), ((), ())), preferred_element_type=jnp.float32)
            * scale
        )
        scores = jnp.where(visible, scores, -1e30)
        top = jnp.max(scores, axis=1, keepdims=True)
        expo = jnp.where(visible, jnp.exp(scores - top), 0.0)
        weights = (expo / jnp.sum(expo, axis=1, keepdims=True)).astype(jnp.bfloat16)
        mixed = jnp.dot(weights, values, preferred_element_type=jnp.float32)
        o_ref[:, head] = mixed.astype(jnp.bfloat16)


def attention(scalars, shards_in, wq, kv_mine, kv_other, chunk=1024):
    per, depth = shards_in[0].shape
    n_shards = len(shards_in)
    rows = per * n_shards
    cols = wq.shape[1]
    dh = kv_mine.shape[1]
    return pl.pallas_call(
        functools.partial(attention_kernel, n_shards, chunk),
        out_shape=jax.ShapeDtypeStruct((rows, cols), jnp.bfloat16),
        in_specs=[SM] + [VM] * n_shards + [FAR] * 3,
        out_specs=VM,
        scratch_shapes=[
            pltpu.VMEM((rows, cols), jnp.float32),
            pltpu.VMEM((rows, 4 * dh), jnp.float32),
            pltpu.VMEM(wq.shape, jnp.bfloat16),
            pltpu.VMEM(kv_mine.shape, jnp.bfloat16),
            pltpu.VMEM(kv_other.shape, jnp.bfloat16),
            pltpu.SemaphoreType.DMA((3, depth // chunk)),
        ],
        compiler_params=kernel_params(20),
        cost_estimate=pl.CostEstimate(
            flops=2 * rows * depth * (cols + 4 * dh),
            bytes_accessed=2 * (rows * depth + depth * (cols + 4 * dh)),
            transcendentals=4 * rows * rows,
        ),
        name="attention",
    )(scalars, *shards_in, far(wq), far(kv_mine), far(kv_other))


def project_kernel(base, chunk, m_ref, w_hbm, other_ref, own_ref, w_ref, sems):
    half, cols = other_ref.shape
    copies = []
    for step in range(cols // chunk):
        copies.append(
            pltpu.make_async_copy(
                w_hbm.at[:, base + step * chunk : base + (step + 1) * chunk],
                w_ref.at[:, step * chunk : (step + 1) * chunk],
                sems.at[step],
            )
        )
        copies[-1].start()
    for step, copy in enumerate(copies):
        copy.wait()
        cut = slice(step * chunk, (step + 1) * chunk)
        y = jnp.dot(m_ref[...], w_ref[:, cut], preferred_element_type=jnp.float32)
        other_ref[:, cut] = y[:half].astype(jnp.bfloat16)
        own_ref[:, cut] = y[half:].astype(jnp.bfloat16)


def project(mixed, w, base, cols, chunk=512):
    rows, depth = mixed.shape
    out = jax.ShapeDtypeStruct((rows // 2, cols), jnp.bfloat16)
    return pl.pallas_call(
        functools.partial(project_kernel, base, chunk),
        out_shape=(out, out),
        in_specs=[VM, FAR],
        out_specs=(VM, VM),
        scratch_shapes=[
            pltpu.VMEM((depth, cols), jnp.bfloat16),
            pltpu.SemaphoreType.DMA((cols // chunk,)),
        ],
        compiler_params=kernel_params(12),
        cost_estimate=pl.CostEstimate(
            flops=2 * rows * depth * cols,
            bytes_accessed=2 * (rows * depth + depth * cols + rows * cols),
            transcendentals=0,
        ),
        name="project",
    )(mixed, far(w))


def add_kernel(n, *refs):
    outs = refs[2 * n :]
    per = outs[0].shape[0]
    width = refs[0].shape[1]
    for i, out in enumerate(outs):
        cut = slice(i * per, (i + 1) * per)
        for j in range(n):
            total = f32(refs[j][cut, :]) + f32(refs[n + j][cut, :])
            out[:, j * width : (j + 1) * width] = total.astype(jnp.bfloat16)


def add_pieces(kept, arrived, count):
    rows, cols = kept[0].shape
    out = jax.ShapeDtypeStruct((rows // count, cols * len(kept)), jnp.bfloat16)
    return pl.pallas_call(
        functools.partial(add_kernel, len(kept)),
        out_shape=(out,) * count,
        in_specs=[VM] * (2 * len(kept)),
        out_specs=(VM,) * count,
        compiler_params=kernel_params(4),
        name="add_pieces",
    )(*kept, *arrived)


def sum_kernel(*refs):
    total = f32(refs[0][...])
    for r in refs[1:-1]:
        total += f32(r[...])
    refs[-1][...] = total.astype(refs[-1].dtype)


def sum_of(arrays, dtype):
    return pl.pallas_call(
        sum_kernel,
        out_shape=jax.ShapeDtypeStruct(arrays[0].shape, dtype),
        in_specs=[VM] * len(arrays),
        out_specs=VM,
        compiler_params=kernel_params(4),
        name="sum_of",
    )(*arrays)


def slope_kernel(*refs):
    parts = refs[:-4]
    x_ref, sp_ref, next_ref, slope_ref = refs[-4:]
    blocks, rows, width = sp_ref.shape
    inner = jnp.zeros((rows, 1), jnp.float32)
    own_sq = jnp.zeros((rows, 1), jnp.float32)
    target_sq = jnp.zeros((rows, 1), jnp.float32)
    for j in range(blocks):
        cols = slice(j * width, (j + 1) * width)
        total = f32(parts[0][:, cols])
        for p in parts[1:]:
            total += f32(p[:, cols])
        new = (f32(x_ref[:, cols]) + total).astype(jnp.bfloat16)
        next_ref[:, cols] = new
        target = f32(new)
        sp = sp_ref[j]
        inner += jnp.sum(sp * target, axis=1, keepdims=True)
        own_sq += jnp.sum(sp * sp, axis=1, keepdims=True)
        target_sq += jnp.sum(target * target, axis=1, keepdims=True)
    inv_own = lax.rsqrt(own_sq + COS_EPS)
    inv_target = lax.rsqrt(target_sq + COS_EPS)
    cosine = inner * inv_own * inv_target
    toward = inner * inv_target * inv_own * inv_own * inv_own
    away = inv_own * inv_target
    for j in range(blocks):
        cols = slice(j * width, (j + 1) * width)
        slope = LOSS_WEIGHT * (toward * sp_ref[j] - f32(next_ref[:, cols]) * away)
        slope_ref[j, :, :width] = slope.astype(jnp.bfloat16)
    distance = jnp.broadcast_to(1.0 - cosine, (rows, CARRY))
    high = f32(distance.astype(jnp.bfloat16))
    middle = f32((distance - high).astype(jnp.bfloat16))
    low = distance - high - middle
    lane = lax.broadcasted_iota(jnp.int32, (rows, CARRY), 1)
    carried = jnp.where(lane == 0, high, jnp.where(lane == 1, middle, low))
    carried = jnp.where(lane < 3, carried, 0.0).astype(jnp.bfloat16)
    for j in range(blocks):
        slope_ref[j, :, width:] = carried


def slopes(parts, x, sp):
    return pl.pallas_call(
        slope_kernel,
        out_shape=(
            jax.ShapeDtypeStruct(x.shape, jnp.bfloat16),
            jax.ShapeDtypeStruct((*sp.shape[:2], sp.shape[2] + CARRY), jnp.bfloat16),
        ),
        in_specs=[VM] * (len(parts) + 2),
        out_specs=(VM, VM),
        compiler_params=kernel_params(6),
        name="slopes",
    )(*parts, x, sp)


def stacked(refs, all_ref):
    for k, r in enumerate(refs):
        all_ref[:, k] = r[:, :, : all_ref.shape[3]]
    n_sec, n_y, rows, width = all_ref.shape
    return all_ref[...].reshape(n_sec * n_y * rows, width)


def blocks_of(sc_ref, size):
    core, xh = sc_ref[0], sc_ref[1]
    for at_x, at_c in ((xh, core), (xh, 1 - core), (1 - xh, core), (1 - xh, 1 - core)):
        yield pl.ds(pl.multiple_of((at_x * 2 + at_c) * size, size), size)


def student_proj_kernel(n_sends, sc_ref, *refs):
    distant, keep_ref, send_refs = refs[:5], refs[5], refs[6 : 6 + n_sends]
    near, sems = refs[6 + n_sends : -1], refs[-1]
    copies = fetched(distant, near, sems)
    tokens_ref, proj_refs = near[0], near[1:]
    size = proj_refs[0].shape[0]
    total = None
    copies[0].wait()
    for cut, p, copy in zip(blocks_of(sc_ref, size), proj_refs, copies[1:]):
        copy.wait()
        y = jnp.dot(tokens_ref[:, cut], p[...], preferred_element_type=jnp.float32)
        total = y if total is None else total + y
    n_sec, rows, block = keep_ref.shape
    total = total.reshape(n_sec, 1 + n_sends, rows, block)
    keep_ref[...] = total[:, 0]
    for k, out in enumerate(send_refs):
        out[...] = total[:, k + 1].astype(jnp.bfloat16)


def student_proj_part(scalars, tokens, proj, n_sec, n_y):
    n_tok, feats = tokens.shape
    rows, block = n_tok // (n_sec * n_y), proj[0].shape[1]
    keep = jax.ShapeDtypeStruct((n_sec, rows, block), jnp.float32)
    send = jax.ShapeDtypeStruct((n_sec, rows, block), jnp.bfloat16)
    inputs = (tokens, *proj)
    return pl.pallas_call(
        functools.partial(student_proj_kernel, n_y - 1),
        out_shape=(keep,) + (send,) * (n_y - 1),
        in_specs=[SM] + [FAR] * len(inputs),
        out_specs=(VM,) * n_y,
        scratch_shapes=[pltpu.VMEM(v.shape, v.dtype) for v in inputs]
        + [pltpu.SemaphoreType.DMA((len(inputs),))],
        compiler_params=kernel_params(14),
        cost_estimate=pl.CostEstimate(
            flops=2 * n_tok * feats * block,
            bytes_accessed=2 * (n_tok * feats + feats * block + n_tok * block),
            transcendentals=0,
        ),
        name="student_proj_part",
    )(scalars, *map(far, inputs))


def gradients_kernel(n_y, sc_ref, *refs):
    slope_refs, distant = refs[:n_y], refs[n_y : n_y + 5]
    gs_ref, loss_ref, away_far, away_near, stay_far, stay_near = refs[n_y + 5 : n_y + 11]
    all_ref, near, sems = refs[n_y + 11], refs[n_y + 12 : -1], refs[-1]
    copies = fetched(distant, near, sems)
    tokens_ref, proj_refs = near[0], near[1:]
    slope = stacked(slope_refs, all_ref)
    width, size = proj_refs[0].shape
    core, xh = sc_ref[0], sc_ref[1]
    copies[0].wait()
    for out, at_x, at_c in (
        (away_far, 1 - xh, 1 - core),
        (away_near, xh, 1 - core),
        (stay_far, 1 - xh, core),
        (stay_near, xh, core),
    ):
        cut = pl.ds(pl.multiple_of((at_x * 2 + at_c) * size, size), size)
        y = jnp.dot(tokens_ref[cut, :], slope, preferred_element_type=jnp.float32)
        out[...] = y.astype(out.dtype)
    for cut, p, copy in zip(blocks_of(sc_ref, size), proj_refs, copies[1:]):
        copy.wait()
        y = jnp.dot(slope, p[...], preferred_element_type=jnp.float32)
        gs_ref[:, :, :, cut] = y.astype(jnp.bfloat16).reshape(*gs_ref.shape[:3], size)
    loss = None
    for r in slope_refs:
        part = jnp.sum(f32(r[:, :, width:]), axis=(0, 1), keepdims=True)
        loss = part if loss is None else loss + part
    loss = jnp.sum(loss[0], axis=1, keepdims=True)
    loss_ref[...] = jnp.broadcast_to(loss, loss_ref.shape)


def gradients(scalars, slope, tokens_t, proj_t):
    n_y = len(slope)
    n_sec, rows = slope[0].shape[:2]
    width, size = proj_t[0].shape
    low = jax.ShapeDtypeStruct((size, width), jnp.bfloat16)
    high = jax.ShapeDtypeStruct((size, width), jnp.float32)
    inputs = (tokens_t, *proj_t)
    return pl.pallas_call(
        functools.partial(gradients_kernel, n_y),
        out_shape=(
            jax.ShapeDtypeStruct((n_sec, n_y, rows, size * len(proj_t)), jnp.bfloat16),
            jax.ShapeDtypeStruct((8, 128), jnp.float32),
            low,
            low,
            high,
            high,
        ),
        in_specs=[SM] + [VM] * n_y + [FAR] * len(inputs),
        out_specs=(VM,) * 6,
        scratch_shapes=[pltpu.VMEM((n_sec, n_y, rows, width), jnp.bfloat16)]
        + [pltpu.VMEM(v.shape, v.dtype) for v in inputs]
        + [pltpu.SemaphoreType.DMA((len(inputs),))],
        compiler_params=kernel_params(14),
        name="gradients",
    )(scalars, *slope, *map(far, inputs))


def section_sum_kernel(g_ref, *outs):
    for k, out in enumerate(outs):
        total = f32(g_ref[0, k])
        for s in range(1, g_ref.shape[0]):
            total += f32(g_ref[s, k])
        out[...] = total.astype(out.dtype)


def section_sum(g):
    _, n_y, rows, feats = g.shape
    first = jax.ShapeDtypeStruct((rows, feats), jnp.float32)
    rest = jax.ShapeDtypeStruct((rows, feats), jnp.bfloat16)
    return pl.pallas_call(
        section_sum_kernel,
        out_shape=(first,) + (rest,) * (n_y - 1),
        in_specs=[VM],
        out_specs=(VM,) * n_y,
        compiler_params=kernel_params(6),
        name="section_sum",
    )(g)


def place_kernel(sc_ref, *refs):
    o_ref = refs[-1]
    feats = refs[0].shape[1]
    for k, r in enumerate(refs[:-1]):
        cut = pl.ds(pl.multiple_of((sc_ref[2] ^ k) * feats, feats), feats)
        o_ref[:, cut] = f32(r[...])


def placed_feats(scalars, pieces):
    rows, feats = pieces[0].shape
    return pl.pallas_call(
        place_kernel,
        out_shape=jax.ShapeDtypeStruct((rows, feats * len(pieces)), jnp.float32),
        in_specs=[SM] + [VM] * len(pieces),
        out_specs=VM,
        compiler_params=kernel_params(4),
        name="placed_feats",
    )(scalars, *pieces)


def tied(*values):
    return lax.optimization_barrier(values)


def to_columns(value, n_y):
    return [value] + [swap(value, "y", k) for k in range(1, n_y)]


def step(
    teacher_rows,
    norm_gain,
    query_weight,
    keys_values,
    output_weight,
    doc_start,
    student_rows,
    projector,
):
    core = lax.axis_index("c").astype(jnp.int32)
    xh = lax.axis_index("xh").astype(jnp.int32)
    y = lax.axis_index("y").astype(jnp.int32)
    n_sec = lax.axis_size(SEC)
    n_y = lax.axis_size("y")
    n_tp = lax.axis_size(TP)
    x = teacher_rows[0]
    rows, width = x.shape
    scalars = jnp.stack([core, xh, y, doc_start[0]])

    feats = student_rows.shape[2] // n_y
    picked = [
        lax.dynamic_slice_in_dim(student_rows[0], (y ^ k) * feats, feats, axis=1)
        for k in range(n_y)
    ]
    picked = [picked[0]] + [swap(picked[k], "y", k) for k in range(1, n_y)]
    proj = [projector, swap(projector, "c", 1), swap(projector, "xh", 1)]

    normed = normalize(x, norm_gain)
    y1, y3 = swap(normed, "y", 1), swap(normed, "y", 3)
    across = swap(normed, "xh", 1)
    y2 = swap(normed, "y", 2)
    own = [normed, y1, y2, y3]
    own += [across, swap(across, "y", 1), swap(y2, "xh", 1), swap(across, "y", 3)]
    other = [swap(v, "c", 1) for v in own]
    kv_mine = jnp.swapaxes(keys_values[0], 1, 2)
    kv_other = swap(kv_mine, "c", 1)

    mine, _ = tied(jnp.stack(picked), normed)
    tokens = exchange(jnp.broadcast_to(mine, (n_sec, *mine.shape)), SEC)
    n_tok = n_sec * n_y * rows
    tokens = tokens.reshape(n_tok, feats)

    mixed = attention(scalars, other + own, query_weight[0], kv_mine, kv_other)

    proj[2], mixed = tied(proj[2], mixed)
    proj.append(swap(proj[2], "c", 1))
    half = width // 2
    to_other, kept = project(mixed, output_weight[0], 0, half)
    sides = [(kept, to_other, swap(to_other, "c", 1))]

    tokens, _ = tied(tokens, kept)
    keep, *sends = student_proj_part(scalars, tokens, proj, n_sec, n_y)
    mixed, keep = tied(mixed, keep)
    got = [swap(sends[k - 1], "y", k) for k in range(1, n_y)]
    to_other, kept = project(mixed, output_weight[0], half, half)
    sides.append((kept, to_other, swap(to_other, "c", 1)))

    pieces = add_pieces([s[0] for s in sides], [s[2] for s in sides], 2 * n_y)
    near, away = list(pieces[:n_y]), list(pieces[n_y:])
    late = tied(pieces[0], tokens, *proj)
    tokens_t = late[1].T
    proj_t = [p.T for p in late[2:]]
    relayed = swap(away[2], "xh", 1)
    away = sum_of((away[0], swap(away[1], "y", 1), swap(away[3], "y", 3)), jnp.bfloat16)
    away = swap(away, "xh", 1)
    relayed = swap(sum_of((near[2], relayed), jnp.bfloat16), "y", 2)
    parts = (near[0], swap(near[1], "y", 1), swap(near[3], "y", 3), relayed, away)

    sp = sum_of((keep, *got), jnp.float32)
    sp = exchange(sp, SEC)
    sp, tokens_t, *proj_t = tied(sp, tokens_t, *proj_t)
    teacher_next, slope = slopes(parts, x, sp)

    slope = exchange(slope, SEC)
    slope = to_columns(slope, n_y)
    grad_s, loss, away_far, away_near, stay_far, stay_near = gradients(
        scalars, slope, tokens_t, proj_t
    )
    grad_s = exchange(grad_s, SEC)
    loss = loss + swap(loss, "c", 1)
    away_far = swap(away_far, "c", 1)
    away_near = swap(away_near, "c", 1)
    loss = loss + swap(loss, "xh", 1)
    across = swap(sum_of((stay_far, away_far), jnp.bfloat16), "xh", 1)
    grad_projector = sum_of((stay_near, away_near, across), jnp.float32)
    pieces = section_sum(grad_s)
    pieces = [pieces[0]] + [swap(pieces[k], "y", k) for k in range(1, n_y)]
    pieces[3], grad_projector, loss = tied(pieces[3], grad_projector, loss)
    grad_student = placed_feats(scalars, pieces)
    loss = loss[0, 0] / (n_sec * n_tp * rows)
    return (teacher_next[None], loss, grad_student[None], grad_projector)


def solution(mesh):
    fine = Mesh(mesh.devices.reshape(4, 2, 4, 2, 2), ("z", "xl", "y", "xh", "c"))
    placed = (
        P(SEC, TP, None),
        P(SEC, None),
        P(SEC, None, TP),
        P(SEC, None, None, TP),
        P(SEC, TP, None),
        P(SEC),
        P(SEC, TP, None),
        P(TP, SEC),
    )
    return jax.shard_map(
        step,
        mesh=fine,
        in_specs=placed,
        out_specs=(P(SEC, TP, None), P(), P(SEC, TP, None), P(TP, SEC)),
        check_vma=False,
    )
```

time: 377 us -> 192 us (0.51)
  waiting for transfers between devices: 135 us -> 52.4 us
  other arithmetic: 72 us -> 0.1 us
  starting transfers between devices: 13.8 us -> 69.6 us
  blocking collectives: 52.1 us -> 10.9 us
  local copies, waits for them, and re-layouts: 54.7 us -> 18.8 us
  Pallas kernels: 0 us -> 35.9 us
  matrix products: 32 us -> 0 us
  between operations: 16.4 us -> 3.3 us
    reduce_scatter x1 -> x0, waiting for transfers between devices: 76.1 us -> none  [shards(): lax.psum_scatter(round_bf16(jnp.dot(block, out_local, preferred_element_t...]
    all_gather x3 -> x0, waiting for transfers between devices: 58.3 us -> none  [the longest x1 58.2 us: shards(): block_rows = lax.all_gather(normed, 'tp', axis=0, tiled=True)]
    ppermute x2 -> x45, starting transfers between devices: 0.67 us -> 56.5 us  [swap(): return lax.ppermute(value, axis, [(i, i ^ apart) for i in range(count)])]
    unnamed x2 -> x0, other arithmetic: 45.3 us -> none
    ppermute x2 -> x45, waiting for transfers between devices: 0.01 us -> 42 us  [swap(): return lax.ppermute(value, axis, [(i, i ^ apart) for i in range(count)])]
    all_to_all x3 -> x1, blocking collectives: 52.1 us -> 10.9 us  [exchange(): return lax.all_to_all(pieces, axes, split_axis=0, concat_axis=0, tiled=True)]
    pallas_call x0 -> x15, Pallas kernels: none -> 35.9 us  [the longest x1 8.56 us: attention(): pl.pallas_call(functools.partial(attention_kernel, n_shards, chunk), out_...]
    dot_general x9 -> x0, matrix products: 32 us -> none  [the longest x1 7.24 us: shards(): lax.dot_general(block, proj_block, contract_last, preferred_element_type=...]
  transfers between devices with their start and end apart: 9 -> 48, of which waited for: 2 -> 15; matrix products, arithmetic and copies ran while one was open for 36% -> 7% of each run, Pallas kernels for 0% -> 14%
where the time goes in v1:
time: 192 us; the launch traced here: 191 us
  starting transfers between devices  69.6 us (36%)
  waiting for transfers between devices  52.4 us (27%)
  Pallas kernels  35.9 us (19%)
  local copies, waits for them, and re-layouts  18.8 us (10%)
  blocking collectives  10.9 us (6%)
  between operations  3.3 us (2%)
    ppermute x45, starting transfers between devices, swap(): return lax.ppermute(value, axis, [(i, i ^ apart) for i in range(count)])  56.5 us
    ppermute x45, waiting for transfers between devices, swap(): return lax.ppermute(value, axis, [(i, i ^ apart) for i in range(count)])  42 us
    all_to_all x3, starting transfers between devices, exchange(): return lax.all_to_all(pieces, axes, split_axis=0, concat_axis=0, tiled=True)  13.1 us
    all_to_all x1, blocking collectives, exchange(): return lax.all_to_all(pieces, axes, split_axis=0, concat_axis=0, tiled=True)  10.9 us
    all_to_all x3, waiting for transfers between devices, exchange(): return lax.all_to_all(pieces, axes, split_axis=0, concat_axis=0, tiled=True)  10.4 us
    pallas_call x1, Pallas kernels, attention(): pl.pallas_call(functools.partial(attention_kernel, n_shards, chunk), out_...  8.56 us
    pallas_call x2, Pallas kernels, project(): pl.pallas_call(functools.partial(project_kernel, base, chunk), out_shape=...  8.08 us
    unnamed x19, local copies, waits for them, and re-layouts  6.91 us
  transfers between devices with their start and end apart: 48, of which 15 were waited for; matrix products, arithmetic and copies ran while one was open for 7% of the time, Pallas kernels for 14%

profile of v1, /device:TPU:1, one launch (start us, length us, event | category | flops | bytes accessed | tf_op | source)
XLA Modules:
  0.0 191.0 jit_solution(6810831934827241829)
XLA Ops:
  8.2 2.8 %collective-permute-start.8 = (bf16[16,8192]{1,0:T(8,128)(2,1)S(1)}, bf16[16,8192]{1,0:T(8,128)(2,1)S(1)}, u32[]{:S(2)}, u32[]{:S(2)}) collective-permute-start(bf16[16,8192]{1,0:T(8,128)(2,1)S(1)} %normalize.1.refs_8_), channel_id=1, source_target_pairs={{0,2},{2,0},{1,3},{3,1},{4,6},{6,4},{5,7},{7,5},{8,10},{10,8},{9,1... | collective-permute-start | bytes 786440 | tf_op jit(solution)/shard_map/ppermute | solution.py:31
  14.8 6.0 %collective-permute-done.18 = bf16[16,1024]{1,0:T(8,128)(2,1)S(1)} collective-permute-done((bf16[16,1024]{1,0:T(8,128)(2,1)S(1)}, bf16[16,1024]{1,0:T(8,128)(2,1)S(1)}, u32[]{:S(2)}, u32[]{:S(2)}) %collective-permute-start.18) | collective-permute-done | bytes 32800 | tf_op jit(solution)/shard_map/ppermute | solution.py:31
  22.9 2.9 %collective-permute-done.6.refs_11_ = bf16[16,8192]{1,0:T(8,128)(2,1)S(1)} collective-permute-done((bf16[16,8192]{1,0:T(8,128)(2,1)S(1)}, bf16[16,8192]{1,0:T(8,128)(2,1)S(1)}, u32[]{:S(2)}, u32[]{:S(2)}) %collective-permute-start.6) | collective-permute-done | bytes 262176 | tf_op jit(solution)/shard_map/ppermute | solution.py:31
  26.7 3.0 %collective-permute-start.9 = (bf16[16,8192]{1,0:T(8,128)(2,1)S(1)}, bf16[16,8192]{1,0:T(8,128)(2,1)S(1)}, u32[]{:S(2)}, u32[]{:S(2)}) collective-permute-start(bf16[16,8192]{1,0:T(8,128)(2,1)S(1)} %collective-permute-done.8.refs_12_), channel_id=1, source_target_pairs={{0,1},{1,0},{2,3},{3,2},{4,5},{5,4},{6,7},{7,6},{8,9},{9,8},{10,11... | collective-permute-start | bytes 786440 | tf_op jit(solution)/shard_map/ppermute | solution.py:31
  29.7 3.6 %collective-permute-done.14.refs_15_ = bf16[16,8192]{1,0:T(8,128)(2,1)S(1)} collective-permute-done((bf16[16,8192]{1,0:T(8,128)(2,1)S(1)}, bf16[16,8192]{1,0:T(8,128)(2,1)S(1)}, u32[]{:S(2)}, u32[]{:S(2)}) %collective-permute-start.14) | collective-permute-done | bytes 262176 | tf_op jit(solution)/shard_map/ppermute | solution.py:31
  33.5 2.7 %collective-permute-start.5 = (bf16[16,8192]{1,0:T(8,128)(2,1)S(1)}, bf16[16,8192]{1,0:T(8,128)(2,1)S(1)}, u32[]{:S(2)}, u32[]{:S(2)}) collective-permute-start(bf16[16,8192]{1,0:T(8,128)(2,1)S(1)} %collective-permute-done.4.refs_10_), channel_id=1, source_target_pairs={{0,1},{1,0},{2,3},{3,2},{4,5},{5,4},{6,7},{7,6},{8,9},{9,8},{10,11... | collective-permute-start | bytes 786440 | tf_op jit(solution)/shard_map/ppermute | solution.py:31
  36.7 3.3 %collective-permute-done.12.refs_14_ = bf16[16,8192]{1,0:T(8,128)(2,1)S(1)} collective-permute-done((bf16[16,8192]{1,0:T(8,128)(2,1)S(1)}, bf16[16,8192]{1,0:T(8,128)(2,1)S(1)}, u32[]{:S(2)}, u32[]{:S(2)}) %collective-permute-start.12) | collective-permute-done | bytes 262176 | tf_op jit(solution)/shard_map/ppermute | solution.py:31
  40.0 3.6 %collective-permute-start.11 = (bf16[16,8192]{1,0:T(8,128)(2,1)S(1)}, bf16[16,8192]{1,0:T(8,128)(2,1)}, u32[]{:S(2)}, u32[]{:S(2)}) collective-permute-start(bf16[16,8192]{1,0:T(8,128)(2,1)S(1)} %collective-permute-done.10.refs_13_), channel_id=1, source_target_pairs={{0,1},{1,0},{2,3},{3,2},{4,5},{5,4},{6,7},{7,6},{8,9},{9,8},{10,11... | collective-permute-start | bytes 786440 | tf_op jit(solution)/shard_map/ppermute | solution.py:31
  47.6 6.0 %all-to-all-start = ((bf16[8,4,16,1024]{3,2,1,0:T(8,128)(2,1)}), bf16[8,4,16,1024]{3,2,1,0:T(8,128)(2,1)}, u32[]{:S(2)}, u32[]{:S(2)}) async-start(bf16[8,4,16,1024]{3,2,1,0:T(8,128)(2,1)} %broadcast_in_dim.9), calls=%async_computation | async-start | bytes 2097152 | tf_op jit(solution)/shard_map/all_to_all | solution.py:26
  55.7 8.6 %attention.1.m_ref = bf16[256,512]{1,0:T(8,128)(2,1)S(1)} custom-call(s32[4]{0:T(128)S(1)} %pad_add_fusion.sc_ref, bf16[16,8192]{1,0:T(8,128)(2,1)S(1)} %collective-permute-done.1.refs_0_, bf16[16,8192]{1,0:T(8,128)(2,1)S(1)} %copy-done.3, bf16[16,8192]{1,0:T(8,128)(2,1)S(1)} %collective-permute-done.5.refs_2_, ...), custom_call_target="tpu_custom_call" | custom-call | flops 3221225472 | bytes 16777216 | tf_op jit(solution)/shard_map/attention/pallas_call | solution.py:151
  68.5 4.5 %project.2 = (bf16[128,4096]{1,0:T(8,128)(2,1)}, bf16[128,4096]{1,0:T(8,128)(2,1)S(1)}) custom-call(bf16[256,512]{1,0:T(8,128)(2,1)S(1)} %attention.1.m_ref, bf16[512,8192]{1,0:T(8,128)(2,1)} %bitcast.29), custom_call_target="tpu_custom_call" | custom-call | flops 1073741824 | bytes 6553600 | tf_op jit(solution)/shard_map/project/pallas_call | solution.py:197
  76.6 3.5 %student_proj_part.1 = (f32[8,16,1024]{2,1,0:T(8,128)S(1)}, bf16[8,16,1024]{2,1,0:T(8,128)(2,1)S(1)}, bf16[8,16,1024]{2,1,0:T(8,128)(2,1)S(1)}, bf16[8,16,1024]{2,1,0:T(8,128)(2,1)S(1)}) custom-call(s32[4]{0:T(128)S(1)} %pad_add_fusion.sc_ref, bf16[512,1024]{1,0:T(8,128)(2,1)} %bitcast.15.refs_0_, bf16[256,1024]{1,0:T(8,128)(2,1)} %refs_1_.1, ...), custom_call_target="tpu_custom_call" | custom-call | flops 1073741824 | bytes 4194304 | tf_op jit(solution)/shard_map/student_proj_part/pallas_call | solution.py:349
  80.1 3.6 %project.3 = (bf16[128,4096]{1,0:T(8,128)(2,1)S(1)}, bf16[128,4096]{1,0:T(8,128)(2,1)S(1)}) custom-call(bf16[256,512]{1,0:T(8,128)(2,1)S(1)} %attention.1.m_ref, bf16[512,8192]{1,0:T(8,128)(2,1)} %bitcast.30), custom_call_target="tpu_custom_call" | custom-call | flops 1073741824 | bytes 6553600 | tf_op jit(solution)/shard_map/project/pallas_call | solution.py:197
  90.3 2.4 %collective-permute-start.26 = (bf16[16,8192]{1,0:T(8,128)(2,1)}, bf16[16,8192]{1,0:T(8,128)(2,1)S(1)}, u32[]{:S(2)}, u32[]{:S(2)}) collective-permute-start(bf16[16,8192]{1,0:T(8,128)(2,1)} %get-tuple-element.66), channel_id=1, source_target_pairs={{0,2},{2,0},{1,3},{3,1},{4,6},{6,4},{5,7},{7,5},{8,10},{10,8},{9,1... | collective-permute-start | bytes 786440 | tf_op jit(solution)/shard_map/ppermute | solution.py:31
  93.4 3.9 %collective-permute-done.32.refs_2_ = bf16[8,16,1024]{2,1,0:T(8,128)(2,1)S(1)} collective-permute-done((bf16[8,16,1024]{2,1,0:T(8,128)(2,1)S(1)}, bf16[8,16,1024]{2,1,0:T(8,128)(2,1)S(1)}, u32[]{:S(2)}, u32[]{:S(2)}) %collective-permute-start.32) | collective-permute-done | bytes 262176 | tf_op jit(solution)/shard_map/ppermute | solution.py:31
  100.3 3.6 %all-to-all-start.1 = ((f32[8,16,1024]{2,1,0:T(8,128)}), f32[8,16,1024]{2,1,0:T(8,128)S(1)}, u32[]{:S(2)}, u32[]{:S(2)}) async-start(f32[8,16,1024]{2,1,0:T(8,128)} %sum_of.7), calls=%async_computation.1 | async-start | bytes 1048576 | tf_op jit(solution)/shard_map/all_to_all | solution.py:26
  107.5 2.5 %collective-permute-start.30 = (bf16[16,8192]{1,0:T(8,128)(2,1)S(1)}, bf16[16,8192]{1,0:T(8,128)(2,1)S(1)}, u32[]{:S(2)}, u32[]{:S(2)}) collective-permute-start(bf16[16,8192]{1,0:T(8,128)(2,1)S(1)} %sum_of.6), channel_id=1, source_target_pairs={{0,2},{2,0},{1,3},{3,1},{4,6},{6,4},{5,7},{7,5},{8,10},{10,8},{9,1... | collective-permute-start | bytes 786440 | tf_op jit(solution)/shard_map/ppermute | solution.py:31
  118.3 10.9 %all_to_all.20.refs_0_ = bf16[8,16,1152]{2,1,0:T(8,128)(2,1)S(1)} all-to-all(bf16[8,16,1152]{2,1,0:T(8,128)(2,1)S(1)} %get-tuple-element.81), channel_id=1, replica_groups=mesh['z'=4,'xl'=2,'y'=4,'xh'=2,'c'=2] {'z','xl'}, dimensions={0} | all-to-all | bytes 589824 | tf_op jit(solution)/shard_map/all_to_all | solution.py:26
  132.5 7.7 %collective-permute-done.36.refs_3_ = bf16[8,16,1152]{2,1,0:T(8,128)(2,1)S(1)} collective-permute-done((bf16[8,16,1152]{2,1,0:T(8,128)(2,1)S(1)}, bf16[8,16,1152]{2,1,0:T(8,128)(2,1)S(1)}, u32[]{:S(2)}, u32[]{:S(2)}) %collective-permute-start.36) | collective-permute-done | bytes 294944 | tf_op jit(solution)/shard_map/ppermute | solution.py:31
  140.9 6.8 %gradients.1 = (bf16[8,4,16,1024]{3,2,1,0:T(8,128)(2,1)}, f32[8,128]{1,0:T(8,128)S(1)}, bf16[256,1024]{1,0:T(8,128)(2,1)}, bf16[256,1024]{1,0:T(8,128)(2,1)S(1)}...) custom-call(s32[4]{0:T(128)S(1)} %pad_add_fusion.sc_ref, bf16[8,16,1152]{2,1,0:T(8,128)(2,1)S(1)} %all_to_all.20.refs_0_, ...), custom_call_target="tpu_custom_call" | custom-call | tf_op jit(solution)/shard_map/gradients/pallas_call | solution.py:404
  148.5 6.0 %collective-permute-start.39 = (bf16[256,1024]{1,0:T(8,128)(2,1)}, bf16[256,1024]{1,0:T(8,128)(2,1)}, u32[]{:S(2)}, u32[]{:S(2)}) collective-permute-start(bf16[256,1024]{1,0:T(8,128)(2,1)} %get-tuple-element.92), channel_id=1, source_target_pairs={{0,1},{1,0},{2,3},{3,2},{4,5},{5,4},{6,7},{7,6},{8,9},{9,8},{10,11... | collective-permute-start | bytes 1572872 | tf_op jit(solution)/shard_map/ppermute | solution.py:31
  154.5 3.6 %all-to-all-start.3 = ((bf16[8,4,16,1024]{3,2,1,0:T(8,128)(2,1)}), bf16[8,4,16,1024]{3,2,1,0:T(8,128)(2,1)S(1)}, u32[]{:S(2)}, u32[]{:S(2)}) async-start(bf16[8,4,16,1024]{3,2,1,0:T(8,128)(2,1)} %get-tuple-element.87), calls=%async_computation.3 | async-start | bytes 2097152 | tf_op jit(solution)/shard_map/all_to_all | solution.py:26
  164.7 9.2 %all-to-all-done.3.g_ref = bf16[8,4,16,1024]{3,2,1,0:T(8,128)(2,1)S(1)} async-done(((bf16[8,4,16,1024]{3,2,1,0:T(8,128)(2,1)}), bf16[8,4,16,1024]{3,2,1,0:T(8,128)(2,1)S(1)}, u32[]{:S(2)}, u32[]{:S(2)}) %all-to-all-start.3) | async-done | bytes 1048608 | tf_op jit(solution)/shard_map/all_to_all | solution.py:26
  176.2 7.6 %collective-permute-done.42 = f32[8,128]{1,0:T(8,128)S(1)} collective-permute-done((f32[8,128]{1,0:T(8,128)S(1)}, f32[8,128]{1,0:T(8,128)S(1)}, u32[]{:S(2)}, u32[]{:S(2)}) %collective-permute-start.42) | collective-permute-done | bytes 4128 | tf_op jit(solution)/shard_map/ppermute | solution.py:31
  (119 shorter events, 69.5 us)
Async XLA Ops:
  0.6 54.1 %collective-permute-start.16 = (bf16[2,64,8192]{2,1,0:T(8,128)(2,1)}, bf16[2,64,8192]{2,1,0:T(8,128)(2,1)}, u32[]{:S(2)}, u32[]{:S(2)}) collective-permute-start(bf16[2,64,8192]{2,1,0:T(8,128)(2,1)} %bitcast.33), channel_id=1, source_target_pairs={{0,1},{1,0},{2,3},{3,2},{4,5},{5,4},{6,7},{7,6},{8,9},{9,8},{10,11... | collective-permute-start | bytes 6291464 | tf_op jit(solution)/shard_map/ppermute | solution.py:31
  8.2 12.6 %collective-permute-start.8 = (bf16[16,8192]{1,0:T(8,128)(2,1)S(1)}, bf16[16,8192]{1,0:T(8,128)(2,1)S(1)}, u32[]{:S(2)}, u32[]{:S(2)}) collective-permute-start(bf16[16,8192]{1,0:T(8,128)(2,1)S(1)} %normalize.1.refs_8_), channel_id=1, source_target_pairs={{0,2},{2,0},{1,3},{3,1},{4,6},{6,4},{5,7},{7,5},{8,10},{10,8},{9,1... | collective-permute-start | bytes 786440 | tf_op jit(solution)/shard_map/ppermute | solution.py:31
  11.1 14.7 %collective-permute-start.6 = (bf16[16,8192]{1,0:T(8,128)(2,1)S(1)}, bf16[16,8192]{1,0:T(8,128)(2,1)S(1)}, u32[]{:S(2)}, u32[]{:S(2)}) collective-permute-start(bf16[16,8192]{1,0:T(8,128)(2,1)S(1)} %normalize.1.refs_8_), channel_id=1, source_target_pairs={{0,12},{4,8},{8,4},{12,0},{1,13},{5,9},{9,5},{13,1},{2,14},{6,10},... | collective-permute-start | bytes 786440 | tf_op jit(solution)/shard_map/ppermute | solution.py:31
  11.8 14.5 %collective-permute-start.4 = (bf16[16,8192]{1,0:T(8,128)(2,1)S(1)}, bf16[16,8192]{1,0:T(8,128)(2,1)S(1)}, u32[]{:S(2)}, u32[]{:S(2)}) collective-permute-start(bf16[16,8192]{1,0:T(8,128)(2,1)S(1)} %normalize.1.refs_8_), channel_id=1, source_target_pairs={{0,8},{4,12},{8,0},{12,4},{1,9},{5,13},{9,1},{13,5},{2,10},{6,14},... | collective-permute-start | bytes 786440 | tf_op jit(solution)/shard_map/ppermute | solution.py:31
  36.3 17.4 %collective-permute-start.15 = (bf16[16,8192]{1,0:T(8,128)(2,1)S(1)}, bf16[16,8192]{1,0:T(8,128)(2,1)}, u32[]{:S(2)}, u32[]{:S(2)}) collective-permute-start(bf16[16,8192]{1,0:T(8,128)(2,1)S(1)} %collective-permute-done.14.refs_15_), channel_id=1, source_target_pairs={{0,1},{1,0},{2,3},{3,2},{4,5},{5,4},{6,7},{7,6},{8,9},{9,8},{10,11... | collective-permute-start | bytes 786440 | tf_op jit(solution)/shard_map/ppermute | solution.py:31
  40.0 14.8 %collective-permute-start.11 = (bf16[16,8192]{1,0:T(8,128)(2,1)S(1)}, bf16[16,8192]{1,0:T(8,128)(2,1)}, u32[]{:S(2)}, u32[]{:S(2)}) collective-permute-start(bf16[16,8192]{1,0:T(8,128)(2,1)S(1)} %collective-permute-done.10.refs_13_), channel_id=1, source_target_pairs={{0,1},{1,0},{2,3},{3,2},{4,5},{5,4},{6,7},{7,6},{8,9},{9,8},{10,11... | collective-permute-start | bytes 786440 | tf_op jit(solution)/shard_map/ppermute | solution.py:31
  43.6 11.2 %collective-permute-start.13 = (bf16[16,8192]{1,0:T(8,128)(2,1)S(1)}, bf16[16,8192]{1,0:T(8,128)(2,1)}, u32[]{:S(2)}, u32[]{:S(2)}) collective-permute-start(bf16[16,8192]{1,0:T(8,128)(2,1)S(1)} %collective-permute-done.12.refs_14_), channel_id=1, source_target_pairs={{0,1},{1,0},{2,3},{3,2},{4,5},{5,4},{6,7},{7,6},{8,9},{9,8},{10,11... | collective-permute-start | bytes 786440 | tf_op jit(solution)/shard_map/ppermute | solution.py:31
  46.3 18.0 %collective-permute-start = (bf16[256,1024]{0,1:T(8,128)(2,1)}, bf16[256,1024]{0,1:T(8,128)(2,1)}, u32[]{:S(2)}, u32[]{:S(2)}) collective-permute-start(bf16[256,1024]{0,1:T(8,128)(2,1)} %copy.20), channel_id=1, source_target_pairs={{0,2},{2,0},{1,3},{3,1},{4,6},{6,4},{5,7},{7,5},{8,10},{10,8},{9,1... | collective-permute-start | bytes 1572872 | tf_op jit(solution)/shard_map/ppermute | solution.py:31
  47.6 26.6 %all-to-all-start = ((bf16[8,4,16,1024]{3,2,1,0:T(8,128)(2,1)}), bf16[8,4,16,1024]{3,2,1,0:T(8,128)(2,1)}, u32[]{:S(2)}, u32[]{:S(2)}) async-start(bf16[8,4,16,1024]{3,2,1,0:T(8,128)(2,1)} %broadcast_in_dim.9), calls=%async_computation | async-start | bytes 2097152 | tf_op jit(solution)/shard_map/all_to_all | solution.py:26
  64.3 11.3 %collective-permute-start.21 = (bf16[256,1024]{0,1:T(8,128)(2,1)}, bf16[256,1024]{0,1:T(8,128)(2,1)S(1)}, u32[]{:S(2)}, u32[]{:S(2)}) collective-permute-start(bf16[256,1024]{0,1:T(8,128)(2,1)} %collective-permute-done), channel_id=1, source_target_pairs={{0,1},{1,0},{2,3},{3,2},{4,5},{5,4},{6,7},{7,6},{8,9},{9,8},{10,11... | collective-permute-start | bytes 1572872 | tf_op jit(solution)/shard_map/ppermute | solution.py:31
  74.2 13.5 %collective-permute-start.22 = (bf16[128,4096]{1,0:T(8,128)(2,1)}, bf16[128,4096]{1,0:T(8,128)(2,1)S(1)}, u32[]{:S(2)}, u32[]{:S(2)}) collective-permute-start(bf16[128,4096]{1,0:T(8,128)(2,1)} %get-tuple-element.60), channel_id=1, source_target_pairs={{0,1},{1,0},{2,3},{3,2},{4,5},{5,4},{6,7},{7,6},{8,9},{9,8},{10,11... | collective-permute-start | bytes 3145736 | tf_op jit(solution)/shard_map/ppermute | solution.py:31
  83.9 13.4 %collective-permute-start.32 = (bf16[8,16,1024]{2,1,0:T(8,128)(2,1)S(1)}, bf16[8,16,1024]{2,1,0:T(8,128)(2,1)S(1)}, u32[]{:S(2)}, u32[]{:S(2)}) collective-permute-start(bf16[8,16,1024]{2,1,0:T(8,128)(2,1)S(1)} %get-tuple-element.72), channel_id=1, source_target_pairs={{0,8},{4,12},{8,0},{12,4},{1,9},{5,13},{9,1},{13,5},{2,10},{6,14},... | collective-permute-start | bytes 786440 | tf_op jit(solution)/shard_map/ppermute | solution.py:31
  85.7 13.7 %collective-permute-start.33 = (bf16[8,16,1024]{2,1,0:T(8,128)(2,1)S(1)}, bf16[8,16,1024]{2,1,0:T(8,128)(2,1)S(1)}, u32[]{:S(2)}, u32[]{:S(2)}) collective-permute-start(bf16[8,16,1024]{2,1,0:T(8,128)(2,1)S(1)} %get-tuple-element.73), channel_id=1, source_target_pairs={{0,12},{4,8},{8,4},{12,0},{1,13},{5,9},{9,5},{13,1},{2,14},{6,10},... | collective-permute-start | bytes 786440 | tf_op jit(solution)/shard_map/ppermute | solution.py:31
  90.3 15.8 %collective-permute-start.26 = (bf16[16,8192]{1,0:T(8,128)(2,1)}, bf16[16,8192]{1,0:T(8,128)(2,1)S(1)}, u32[]{:S(2)}, u32[]{:S(2)}) collective-permute-start(bf16[16,8192]{1,0:T(8,128)(2,1)} %get-tuple-element.66), channel_id=1, source_target_pairs={{0,2},{2,0},{1,3},{3,1},{4,6},{6,4},{5,7},{7,5},{8,10},{10,8},{9,1... | collective-permute-start | bytes 786440 | tf_op jit(solution)/shard_map/ppermute | solution.py:31
  92.8 14.6 %collective-permute-start.28 = (bf16[16,8192]{1,0:T(8,128)(2,1)}, bf16[16,8192]{1,0:T(8,128)(2,1)S(1)}, u32[]{:S(2)}, u32[]{:S(2)}) collective-permute-start(bf16[16,8192]{1,0:T(8,128)(2,1)} %get-tuple-element.68), channel_id=1, source_target_pairs={{0,4},{4,0},{8,12},{12,8},{1,5},{5,1},{9,13},{13,9},{2,6},{6,2},{1... | collective-permute-start | bytes 786440 | tf_op jit(solution)/shard_map/ppermute | solution.py:31
  92.8 14.6 %collective-permute-start.29 = (bf16[16,8192]{1,0:T(8,128)(2,1)}, bf16[16,8192]{1,0:T(8,128)(2,1)S(1)}, u32[]{:S(2)}, u32[]{:S(2)}) collective-permute-start(bf16[16,8192]{1,0:T(8,128)(2,1)} %get-tuple-element.69), channel_id=1, source_target_pairs={{0,12},{4,8},{8,4},{12,0},{1,13},{5,9},{9,5},{13,1},{2,14},{6,10},... | collective-permute-start | bytes 786440 | tf_op jit(solution)/shard_map/ppermute | solution.py:31
  100.3 14.0 %all-to-all-start.1 = ((f32[8,16,1024]{2,1,0:T(8,128)}), f32[8,16,1024]{2,1,0:T(8,128)S(1)}, u32[]{:S(2)}, u32[]{:S(2)}) async-start(f32[8,16,1024]{2,1,0:T(8,128)} %sum_of.7), calls=%async_computation.1 | async-start | bytes 1048576 | tf_op jit(solution)/shard_map/all_to_all | solution.py:26
  129.3 10.9 %collective-permute-start.36 = (bf16[8,16,1152]{2,1,0:T(8,128)(2,1)S(1)}, bf16[8,16,1152]{2,1,0:T(8,128)(2,1)S(1)}, u32[]{:S(2)}, u32[]{:S(2)}) collective-permute-start(bf16[8,16,1152]{2,1,0:T(8,128)(2,1)S(1)} %all_to_all.20.refs_0_), channel_id=1, source_target_pairs={{0,12},{4,8},{8,4},{12,0},{1,13},{5,9},{9,5},{13,1},{2,14},{6,10},... | collective-permute-start | bytes 884744 | tf_op jit(solution)/shard_map/ppermute | solution.py:31
  154.5 19.3 %all-to-all-start.3 = ((bf16[8,4,16,1024]{3,2,1,0:T(8,128)(2,1)}), bf16[8,4,16,1024]{3,2,1,0:T(8,128)(2,1)S(1)}, u32[]{:S(2)}, u32[]{:S(2)}) async-start(bf16[8,4,16,1024]{3,2,1,0:T(8,128)(2,1)} %get-tuple-element.87), calls=%async_computation.3 | async-start | bytes 2097152 | tf_op jit(solution)/shard_map/all_to_all | solution.py:26
  158.1 27.2 %collective-permute-start.38 = (bf16[256,1024]{1,0:T(8,128)(2,1)}, bf16[256,1024]{1,0:T(8,128)(2,1)}, u32[]{:S(2)}, u32[]{:S(2)}) collective-permute-start(bf16[256,1024]{1,0:T(8,128)(2,1)} %copy-done.5), channel_id=1, source_target_pairs={{0,1},{1,0},{2,3},{3,2},{4,5},{5,4},{6,7},{7,6},{8,9},{9,8},{10,11... | collective-permute-start | bytes 1572872 | tf_op jit(solution)/shard_map/ppermute | solution.py:31
  160.1 25.2 %collective-permute-start.40 = (bf16[256,1024]{1,0:T(8,128)(2,1)}, bf16[256,1024]{1,0:T(8,128)(2,1)S(1)}, u32[]{:S(2)}, u32[]{:S(2)}) collective-permute-start(bf16[256,1024]{1,0:T(8,128)(2,1)} %sum_of.8), channel_id=1, source_target_pairs={{0,2},{2,0},{1,3},{3,1},{4,6},{6,4},{5,7},{7,5},{8,10},{10,8},{9,1... | collective-permute-start | bytes 1572872 | tf_op jit(solution)/shard_map/ppermute | solution.py:31
  163.4 20.4 %collective-permute-start.42 = (f32[8,128]{1,0:T(8,128)S(1)}, f32[8,128]{1,0:T(8,128)S(1)}, u32[]{:S(2)}, u32[]{:S(2)}) collective-permute-start(f32[8,128]{1,0:T(8,128)S(1)} %add.22), channel_id=1, source_target_pairs={{0,2},{2,0},{1,3},{3,1},{4,6},{6,4},{5,7},{7,5},{8,10},{10,8},{9,1... | collective-permute-start | bytes 12296 | tf_op jit(solution)/shard_map/ppermute | solution.py:31
  174.0 13.4 %collective-permute-start.37 = (bf16[16,1024]{1,0:T(8,128)(2,1)S(1)}, bf16[16,1024]{1,0:T(8,128)(2,1)S(1)}, u32[]{:S(2)}, u32[]{:S(2)}) collective-permute-start(bf16[16,1024]{1,0:T(8,128)(2,1)S(1)} %get-tuple-element.88), channel_id=1, source_target_pairs={{0,12},{4,8},{8,4},{12,0},{1,13},{5,9},{9,5},{13,1},{2,14},{6,10},... | collective-permute-start | bytes 98312 | tf_op jit(solution)/shard_map/ppermute | solution.py:31
  176.1 12.4 %collective-permute-start.43 = (bf16[16,1024]{1,0:T(8,128)(2,1)S(1)}, bf16[16,1024]{1,0:T(8,128)(2,1)S(1)}, u32[]{:S(2)}, u32[]{:S(2)}) collective-permute-start(bf16[16,1024]{1,0:T(8,128)(2,1)S(1)} %get-tuple-element.96), channel_id=1, source_target_pairs={{0,4},{4,0},{8,12},{12,8},{1,5},{5,1},{9,13},{13,9},{2,6},{6,2},{1... | collective-permute-start | bytes 98312 | tf_op jit(solution)/shard_map/ppermute | solution.py:31
  (33 other events, 251.2 us)

commit v2 on v1

--- a/solution.py
+++ b/solution.py
@@ -52,7 +52,9 @@
     return copies
 
 
-def norm_kernel(x_ref, gain_ref, o_ref):
+def norm_kernel(x_far, gain_far, o_ref, x_ref, gain_ref, sems):
+    for copy in fetched((x_far, gain_far), (x_ref, gain_ref), sems):
+        copy.wait()
     x = f32(x_ref[...])
     mean_square = jnp.mean(x * x, axis=1, keepdims=True)
     o_ref[...] = (x * lax.rsqrt(mean_square + NORM_EPS) * gain_ref[...]).astype(jnp.bfloat16)
@@ -62,20 +64,27 @@
     return pl.pallas_call(
         norm_kernel,
         out_shape=jax.ShapeDtypeStruct(x.shape, jnp.bfloat16),
-        in_specs=[VM, VM],
+        in_specs=[FAR, FAR],
         out_specs=VM,
+        scratch_shapes=[
+            pltpu.VMEM(x.shape, x.dtype),
+            pltpu.VMEM(gain.shape, gain.dtype),
+            pltpu.SemaphoreType.DMA((2,)),
+        ],
         compiler_params=kernel_params(4),
-        cost_estimate=pl.CostEstimate(
-            flops=20 * x.size, bytes_accessed=320 * x.size, transcendentals=x.shape[0]
-        ),
         name="normalize",
-    )(x, gain)
+    )(far(x), far(gain))
 
 
 def attention_kernel(n_shards, chunk, sc_ref, *refs):
-    shard_refs = refs[:n_shards]
-    wq_hbm, kva_hbm, kvb_hbm, o_ref, q_acc, kv_acc, wq_ref, kva_ref, kvb_ref, sems = refs[n_shards:]
-    per, depth = shard_refs[0].shape
+    n_far = n_shards // 2
+    far_refs = refs[:n_far]
+    wq_hbm, kva_hbm, kvb_hbm, wo_hbm, o_ref, other_ref, own_ref = refs[n_shards : n_shards + 7]
+    q_acc, kv_acc, wq_ref, kva_ref, kvb_ref, wo_ref, held_ref, sems, out_sem, held_sems = refs[
+        n_shards + 7 :
+    ]
+    own_refs = refs[n_far:n_shards]
+    per, depth = own_refs[0].shape
     rows = n_shards * per
     half = rows // 2
     dh = kva_ref.shape[1]
@@ -87,11 +96,20 @@
             pltpu.make_async_copy(wq_hbm.at[cut, :], wq_ref.at[cut, :], sems.at[0, step]),
             pltpu.make_async_copy(kva_hbm.at[:, :, cut], kva_ref.at[:, :, cut], sems.at[1, step]),
             pltpu.make_async_copy(kvb_hbm.at[:, :, cut], kvb_ref.at[:, :, cut], sems.at[2, step]),
+            *(
+                pltpu.make_async_copy(
+                    r.at[:, cut], held_ref.at[i * per : (i + 1) * per, cut], held_sems.at[i, step]
+                )
+                for i, r in enumerate(far_refs)
+            ),
         )
 
     for step in range(steps):
         for copy in fetch(step):
             copy.start()
+    half_cols = own_ref.shape[1]
+    out_copy = pltpu.make_async_copy(wo_hbm.at[:, :half_cols], wo_ref, out_sem.at[0])
+    out_copy.start()
     q_acc[...] = jnp.zeros_like(q_acc)
     kv_acc[...] = jnp.zeros_like(kv_acc)
 
@@ -100,7 +118,7 @@
         for copy in fetch(step):
             copy.wait()
         cut = pl.ds(pl.multiple_of(step * chunk, chunk), chunk)
-        x = jnp.concatenate([r[:, cut] for r in shard_refs], axis=0)
+        x = jnp.concatenate([held_ref[:, cut], *(r[:, cut] for r in own_refs)], axis=0)
         wkv = jnp.concatenate(
             [kva_ref[0, :, cut], kvb_ref[0, :, cut], kva_ref[1, :, cut], kvb_ref[1, :, cut]],
             axis=0,
@@ -140,35 +158,46 @@
         weights = (expo / jnp.sum(expo, axis=1, keepdims=True)).astype(jnp.bfloat16)
         mixed = jnp.dot(weights, values, preferred_element_type=jnp.float32)
         o_ref[:, head] = mixed.astype(jnp.bfloat16)
-
-
-def attention(scalars, shards_in, wq, kv_mine, kv_other, chunk=1024):
+    out_copy.wait()
+    for cut in (slice(i, i + 512) for i in range(0, half_cols, 512)):
+        y = jnp.dot(o_ref[...], wo_ref[:, cut], preferred_element_type=jnp.float32)
+        other_ref[:, cut] = y[:half].astype(jnp.bfloat16)
+        own_ref[:, cut] = y[half:].astype(jnp.bfloat16)
+
+
+def attention(scalars, shards_in, wq, kv_mine, kv_other, wo, chunk=1024):
     per, depth = shards_in[0].shape
     n_shards = len(shards_in)
     rows = per * n_shards
     cols = wq.shape[1]
     dh = kv_mine.shape[1]
+    half_cols = wo.shape[1] // 2
+    part = jax.ShapeDtypeStruct((rows // 2, half_cols), jnp.bfloat16)
     return pl.pallas_call(
         functools.partial(attention_kernel, n_shards, chunk),
-        out_shape=jax.ShapeDtypeStruct((rows, cols), jnp.bfloat16),
-        in_specs=[SM] + [VM] * n_shards + [FAR] * 3,
-        out_specs=VM,
+        out_shape=(jax.ShapeDtypeStruct((rows, cols), jnp.bfloat16), part, part),
+        in_specs=[SM] + [FAR] * (n_shards // 2) + [VM] * (n_shards // 2) + [FAR] * 4,
+        out_specs=(VM,) * 3,
         scratch_shapes=[
             pltpu.VMEM((rows, cols), jnp.float32),
             pltpu.VMEM((rows, 4 * dh), jnp.float32),
             pltpu.VMEM(wq.shape, jnp.bfloat16),
             pltpu.VMEM(kv_mine.shape, jnp.bfloat16),
             pltpu.VMEM(kv_other.shape, jnp.bfloat16),
+            pltpu.VMEM((cols, half_cols), jnp.bfloat16),
+            pltpu.VMEM((rows // 2, depth), jnp.bfloat16),
             pltpu.SemaphoreType.DMA((3, depth // chunk)),
+            pltpu.SemaphoreType.DMA((1,)),
+            pltpu.SemaphoreType.DMA((n_shards // 2, depth // chunk)),
         ],
-        compiler_params=kernel_params(20),
+        compiler_params=kernel_params(28),
         cost_estimate=pl.CostEstimate(
             flops=2 * rows * depth * (cols + 4 * dh),
             bytes_accessed=2 * (rows * depth + depth * (cols + 4 * dh)),
             transcendentals=4 * rows * rows,
         ),
         name="attention",
-    )(scalars, *shards_in, far(wq), far(kv_mine), far(kv_other))
+    )(scalars, *map(far, shards_in[: n_shards // 2]), *shards_in[n_shards // 2 :], far(wq), far(kv_mine), far(kv_other), far(wo))
 
 
 def project_kernel(base, chunk, m_ref, w_hbm, other_ref, own_ref, w_ref, sems):
@@ -270,7 +299,7 @@
         new = (f32(x_ref[:, cols]) + total).astype(jnp.bfloat16)
         next_ref[:, cols] = new
         target = f32(new)
-        sp = sp_ref[j]
+        sp = f32(sp_ref[j])
         inner += jnp.sum(sp * target, axis=1, keepdims=True)
         own_sq += jnp.sum(sp * sp, axis=1, keepdims=True)
         target_sq += jnp.sum(target * target, axis=1, keepdims=True)
@@ -281,7 +310,7 @@
     away = inv_own * inv_target
     for j in range(blocks):
         cols = slice(j * width, (j + 1) * width)
-        slope = LOSS_WEIGHT * (toward * sp_ref[j] - f32(next_ref[:, cols]) * away)
+        slope = LOSS_WEIGHT * (toward * f32(sp_ref[j]) - f32(next_ref[:, cols]) * away)
         slope_ref[j, :, :width] = slope.astype(jnp.bfloat16)
     distance = jnp.broadcast_to(1.0 - cosine, (rows, CARRY))
     high = f32(distance.astype(jnp.bfloat16))
@@ -322,15 +351,16 @@
 
 
 def student_proj_kernel(n_sends, sc_ref, *refs):
-    distant, keep_ref, send_refs = refs[:5], refs[5], refs[6 : 6 + n_sends]
+    distant, last_ref, keep_ref, send_refs = refs[:4], refs[4], refs[5], refs[6 : 6 + n_sends]
     near, sems = refs[6 + n_sends : -1], refs[-1]
     copies = fetched(distant, near, sems)
-    tokens_ref, proj_refs = near[0], near[1:]
+    tokens_ref, proj_refs = near[0], (*near[1:], last_ref)
     size = proj_refs[0].shape[0]
     total = None
     copies[0].wait()
-    for cut, p, copy in zip(blocks_of(sc_ref, size), proj_refs, copies[1:]):
-        copy.wait()
+    for cut, p, copy in zip(blocks_of(sc_ref, size), proj_refs, (*copies[1:], None)):
+        if copy is not None:
+            copy.wait()
         y = jnp.dot(tokens_ref[:, cut], p[...], preferred_element_type=jnp.float32)
         total = y if total is None else total + y
     n_sec, rows, block = keep_ref.shape
@@ -345,11 +375,11 @@
     rows, block = n_tok // (n_sec * n_y), proj[0].shape[1]
     keep = jax.ShapeDtypeStruct((n_sec, rows, block), jnp.float32)
     send = jax.ShapeDtypeStruct((n_sec, rows, block), jnp.bfloat16)
-    inputs = (tokens, *proj)
+    inputs = (tokens, *proj[:3])
     return pl.pallas_call(
         functools.partial(student_proj_kernel, n_y - 1),
         out_shape=(keep,) + (send,) * (n_y - 1),
-        in_specs=[SM] + [FAR] * len(inputs),
+        in_specs=[SM] + [FAR] * len(inputs) + [VM],
         out_specs=(VM,) * n_y,
         scratch_shapes=[pltpu.VMEM(v.shape, v.dtype) for v in inputs]
         + [pltpu.SemaphoreType.DMA((len(inputs),))],
@@ -360,19 +390,36 @@
             transcendentals=0,
         ),
         name="student_proj_part",
-    )(scalars, *map(far, inputs))
+    )(scalars, *map(far, inputs), proj[3])
+
+
+def turn_kernel(n, *refs):
+    distant, outs, near, sems = refs[:n], refs[n : 2 * n], refs[2 * n : 3 * n], refs[-1]
+    copies = fetched(distant, near, sems)
+    for copy, v, out in zip(copies, near, outs):
+        copy.wait()
+        out[...] = v[...].T
+
+
+def turned(values):
+    return pl.pallas_call(
+        functools.partial(turn_kernel, len(values)),
+        out_shape=tuple(jax.ShapeDtypeStruct(v.shape[::-1], v.dtype) for v in values),
+        in_specs=[FAR] * len(values),
+        out_specs=(VM,) * len(values),
+        scratch_shapes=[pltpu.VMEM(v.shape, v.dtype) for v in values]
+        + [pltpu.SemaphoreType.DMA((len(values),))],
+        compiler_params=kernel_params(14),
+        name="turned",
+    )(*map(far, values))
 
 
 def gradients_kernel(n_y, sc_ref, *refs):
-    slope_refs, distant = refs[:n_y], refs[n_y : n_y + 5]
-    gs_ref, loss_ref, away_far, away_near, stay_far, stay_near = refs[n_y + 5 : n_y + 11]
-    all_ref, near, sems = refs[n_y + 11], refs[n_y + 12 : -1], refs[-1]
-    copies = fetched(distant, near, sems)
-    tokens_ref, proj_refs = near[0], near[1:]
+    slope_refs, tokens_ref, proj_refs = refs[:n_y], refs[n_y], refs[n_y + 1 : n_y + 5]
+    gs_ref, loss_ref, away_far, away_near, stay_far, stay_near, all_ref = refs[n_y + 5 :]
     slope = stacked(slope_refs, all_ref)
     width, size = proj_refs[0].shape
     core, xh = sc_ref[0], sc_ref[1]
-    copies[0].wait()
     for out, at_x, at_c in (
         (away_far, 1 - xh, 1 - core),
         (away_near, xh, 1 - core),
@@ -382,10 +429,12 @@
         cut = pl.ds(pl.multiple_of((at_x * 2 + at_c) * size, size), size)
         y = jnp.dot(tokens_ref[cut, :], slope, preferred_element_type=jnp.float32)
         out[...] = y.astype(out.dtype)
-    for cut, p, copy in zip(blocks_of(sc_ref, size), proj_refs, copies[1:]):
-        copy.wait()
+    for cut, p in zip(blocks_of(sc_ref, size), proj_refs):
         y = jnp.dot(slope, p[...], preferred_element_type=jnp.float32)
-        gs_ref[:, :, :, cut] = y.astype(jnp.bfloat16).reshape(*gs_ref.shape[:3], size)
+        n_z, n_xl, _, rows, _ = gs_ref.shape
+        y = y.astype(jnp.bfloat16).reshape(n_z * n_xl, n_y, rows, size)
+        for k in range(n_y):
+            gs_ref[:, :, sc_ref[2] ^ k, :, cut] = y[:, k].reshape(n_z, n_xl, rows, size)
     loss = None
     for r in slope_refs:
         part = jnp.sum(f32(r[:, :, width:]), axis=(0, 1), keepdims=True)
@@ -394,7 +443,7 @@
     loss_ref[...] = jnp.broadcast_to(loss, loss_ref.shape)
 
 
-def gradients(scalars, slope, tokens_t, proj_t):
+def gradients(scalars, slope, tokens_t, proj_t, n_z):
     n_y = len(slope)
     n_sec, rows = slope[0].shape[:2]
     width, size = proj_t[0].shape
@@ -404,63 +453,60 @@
     return pl.pallas_call(
         functools.partial(gradients_kernel, n_y),
         out_shape=(
-            jax.ShapeDtypeStruct((n_sec, n_y, rows, size * len(proj_t)), jnp.bfloat16),
+            jax.ShapeDtypeStruct(
+                (n_z, n_sec // n_z, n_y, rows, size * len(proj_t)), jnp.bfloat16
+            ),
             jax.ShapeDtypeStruct((8, 128), jnp.float32),
             low,
             low,
             high,
             high,
         ),
-        in_specs=[SM] + [VM] * n_y + [FAR] * len(inputs),
+        in_specs=[SM] + [VM] * (n_y + len(inputs)),
         out_specs=(VM,) * 6,
-        scratch_shapes=[pltpu.VMEM((n_sec, n_y, rows, width), jnp.bfloat16)]
-        + [pltpu.VMEM(v.shape, v.dtype) for v in inputs]
-        + [pltpu.SemaphoreType.DMA((len(inputs),))],
-        compiler_params=kernel_params(14),
+        scratch_shapes=[pltpu.VMEM((n_sec, n_y, rows, width), jnp.bfloat16)],
+        compiler_params=kernel_params(10),
         name="gradients",
-    )(scalars, *slope, *map(far, inputs))
-
-
-def section_sum_kernel(g_ref, *outs):
-    for k, out in enumerate(outs):
+    )(scalars, *slope, *inputs)
+
+
+def leading_sum_kernel(g_ref, o_ref):
+    total = f32(g_ref[0])
+    for s in range(1, g_ref.shape[0]):
+        total += f32(g_ref[s])
+    o_ref[...] = total.astype(o_ref.dtype)
+
+
+def leading_sum(g):
+    return pl.pallas_call(
+        leading_sum_kernel,
+        out_shape=jax.ShapeDtypeStruct(g.shape[1:], g.dtype),
+        in_specs=[VM],
+        out_specs=VM,
+        compiler_params=kernel_params(6),
+        name="leading_sum",
+    )(g)
+
+
+def place_kernel(g_ref, o_ref):
+    n_xl, n_y, _, feats = g_ref.shape
+    for k in range(n_y):
         total = f32(g_ref[0, k])
-        for s in range(1, g_ref.shape[0]):
+        for s in range(1, n_xl):
             total += f32(g_ref[s, k])
-        out[...] = total.astype(out.dtype)
-
-
-def section_sum(g):
+        o_ref[:, k * feats : (k + 1) * feats] = total
+
+
+def placed_feats(g):
     _, n_y, rows, feats = g.shape
-    first = jax.ShapeDtypeStruct((rows, feats), jnp.float32)
-    rest = jax.ShapeDtypeStruct((rows, feats), jnp.bfloat16)
-    return pl.pallas_call(
-        section_sum_kernel,
-        out_shape=(first,) + (rest,) * (n_y - 1),
+    return pl.pallas_call(
+        place_kernel,
+        out_shape=jax.ShapeDtypeStruct((rows, feats * n_y), jnp.float32),
         in_specs=[VM],
-        out_specs=(VM,) * n_y,
-        compiler_params=kernel_params(6),
-        name="section_sum",
-    )(g)
-
-
-def place_kernel(sc_ref, *refs):
-    o_ref = refs[-1]
-    feats = refs[0].shape[1]
-    for k, r in enumerate(refs[:-1]):
-        cut = pl.ds(pl.multiple_of((sc_ref[2] ^ k) * feats, feats), feats)
-        o_ref[:, cut] = f32(r[...])
-
-
-def placed_feats(scalars, pieces):
-    rows, feats = pieces[0].shape
-    return pl.pallas_call(
-        place_kernel,
-        out_shape=jax.ShapeDtypeStruct((rows, feats * len(pieces)), jnp.float32),
-        in_specs=[SM] + [VM] * len(pieces),
         out_specs=VM,
         compiler_params=kernel_params(4),
         name="placed_feats",
-    )(scalars, *pieces)
+    )(g)
 
 
 def tied(*values):
@@ -504,7 +550,7 @@
     across = swap(normed, "xh", 1)
     y2 = swap(normed, "y", 2)
     own = [normed, y1, y2, y3]
-    own += [across, swap(across, "y", 1), swap(y2, "xh", 1), swap(across, "y", 3)]
+    own += [across, swap(across, "y", 1), swap(across, "y", 2), swap(across, "y", 3)]
     other = [swap(v, "c", 1) for v in own]
     kv_mine = jnp.swapaxes(keys_values[0], 1, 2)
     kv_other = swap(kv_mine, "c", 1)
@@ -514,15 +560,15 @@
     n_tok = n_sec * n_y * rows
     tokens = tokens.reshape(n_tok, feats)
 
-    mixed = attention(scalars, other + own, query_weight[0], kv_mine, kv_other)
+    mixed, to_other, kept = attention(
+        scalars, other + own, query_weight[0], kv_mine, kv_other, output_weight[0]
+    )
 
     proj[2], mixed = tied(proj[2], mixed)
     proj.append(swap(proj[2], "c", 1))
     half = width // 2
-    to_other, kept = project(mixed, output_weight[0], 0, half)
     sides = [(kept, to_other, swap(to_other, "c", 1))]
 
-    tokens, _ = tied(tokens, kept)
     keep, *sends = student_proj_part(scalars, tokens, proj, n_sec, n_y)
     mixed, keep = tied(mixed, keep)
     got = [swap(sends[k - 1], "y", k) for k in range(1, n_y)]
@@ -531,38 +577,39 @@
 
     pieces = add_pieces([s[0] for s in sides], [s[2] for s in sides], 2 * n_y)
     near, away = list(pieces[:n_y]), list(pieces[n_y:])
-    late = tied(pieces[0], tokens, *proj)
-    tokens_t = late[1].T
-    proj_t = [p.T for p in late[2:]]
     relayed = swap(away[2], "xh", 1)
     away = sum_of((away[0], swap(away[1], "y", 1), swap(away[3], "y", 3)), jnp.bfloat16)
     away = swap(away, "xh", 1)
     relayed = swap(sum_of((near[2], relayed), jnp.bfloat16), "y", 2)
     parts = (near[0], swap(near[1], "y", 1), swap(near[3], "y", 3), relayed, away)
 
-    sp = sum_of((keep, *got), jnp.float32)
+    sp = sum_of((keep, *got), jnp.bfloat16)
     sp = exchange(sp, SEC)
-    sp, tokens_t, *proj_t = tied(sp, tokens_t, *proj_t)
     teacher_next, slope = slopes(parts, x, sp)
 
     slope = exchange(slope, SEC)
+    slope, tokens = tied(slope, tokens)
     slope = to_columns(slope, n_y)
+    tokens_t, *proj_t = turned((tokens, *proj))
     grad_s, loss, away_far, away_near, stay_far, stay_near = gradients(
-        scalars, slope, tokens_t, proj_t
+        scalars, slope, tokens_t, proj_t, lax.axis_size("z")
     )
-    grad_s = exchange(grad_s, SEC)
+    grad_s = exchange(grad_s, "z")
     loss = loss + swap(loss, "c", 1)
     away_far = swap(away_far, "c", 1)
     away_near = swap(away_near, "c", 1)
     loss = loss + swap(loss, "xh", 1)
     across = swap(sum_of((stay_far, away_far), jnp.bfloat16), "xh", 1)
-    grad_projector = sum_of((stay_near, away_near, across), jnp.float32)
-    pieces = section_sum(grad_s)
-    pieces = [pieces[0]] + [swap(pieces[k], "y", k) for k in range(1, n_y)]
-    pieces[3], grad_projector, loss = tied(pieces[3], grad_projector, loss)
-    grad_student = placed_feats(scalars, pieces)
-    loss = loss[0, 0] / (n_sec * n_tp * rows)
-    return (teacher_next[None], loss, grad_student[None], grad_projector)
+    nearly = sum_of((stay_near, away_near), jnp.float32)
+    loss = loss[:1, :1] / (n_sec * n_tp * rows)
+    grad_s, loss, nearly = tied(grad_s, loss, nearly)
+    grad_s = leading_sum(grad_s)
+    shape = grad_s.shape
+    grad_s = exchange(grad_s.reshape(-1, *shape[2:]), ("xl", "y")).reshape(shape)
+    grad_projector = sum_of((nearly, across), jnp.float32)
+    grad_s, grad_projector = tied(grad_s, grad_projector)
+    grad_student = placed_feats(grad_s)
+    return (teacher_next[None], loss[0, 0], grad_student[None], grad_projector)
 
 
 def solution(mesh):

time: 192 us -> 189 us (0.984)
  local copies, waits for them, and re-layouts: 18.8 us -> 4.98 us
  waiting for transfers between devices: 52.4 us -> 65 us
  blocking collectives: 10.9 us -> 17.7 us
  starting transfers between devices: 69.6 us -> 63.2 us
  Pallas kernels: 35.9 us -> 33.6 us
    ppermute x45 -> x42, waiting for transfers between devices: 42 us -> 53.7 us  [swap(): return lax.ppermute(value, axis, [(i, i ^ apart) for i in range(count)])]
    all_to_all x1 -> x2, blocking collectives: 10.9 us -> 17.7 us  [exchange(): return lax.all_to_all(pieces, axes, split_axis=0, concat_axis=0, tiled=True)]
    optimization_barrier x3 -> x0, local copies, waits for them, and re-layouts: 6.39 us -> none  [tied(): return lax.optimization_barrier(values)]
    ppermute x45 -> x42, starting transfers between devices: 56.5 us -> 50.2 us  [swap(): return lax.ppermute(value, axis, [(i, i ^ apart) for i in range(count)])]
    pallas_call x2 -> x1, Pallas kernels: 8.08 us -> 3.63 us  [project(): pl.pallas_call(functools.partial(project_kernel, base, chunk), out_shape=...]
    unnamed x19 -> x22, local copies, waits for them, and re-layouts: 6.91 us -> 2.54 us
    pallas_call x1 -> x2, Pallas kernels: 0.14 us -> 3.19 us  [the longest x1 2.36 us: turned(): pl.pallas_call(functools.partial(turn_kernel, len(values)), out_shape=tup...]
    ppermute x2 -> x0, local copies, waits for them, and re-layouts: 3.05 us -> none  [swap(): return lax.ppermute(value, axis, [(i, i ^ apart) for i in range(count)])]
  transfers between devices with their start and end apart: 48 -> 45, of which waited for: 15 -> 17; matrix products, arithmetic and copies ran while one was open for 7% -> 1% of each run, Pallas kernels for 14% -> 15%
where the time goes in v2:
time: 189 us; the launch traced here: 188 us
  waiting for transfers between devices  65 us (34%)
  starting transfers between devices  63.2 us (33%)
  Pallas kernels  33.6 us (18%)
  blocking collectives  17.7 us (9%)
  local copies, waits for them, and re-layouts  4.98 us (3%)
  between operations  3.35 us (2%)
    ppermute x42, waiting for transfers between devices, swap(): return lax.ppermute(value, axis, [(i, i ^ apart) for i in range(count)])  53.7 us
    ppermute x42, starting transfers between devices, swap(): return lax.ppermute(value, axis, [(i, i ^ apart) for i in range(count)])  50.2 us
    all_to_all x2, blocking collectives, exchange(): return lax.all_to_all(pieces, axes, split_axis=0, concat_axis=0, tiled=True)  17.7 us
    all_to_all x3, starting transfers between devices, exchange(): return lax.all_to_all(pieces, axes, split_axis=0, concat_axis=0, tiled=True)  13 us
    pallas_call x1, Pallas kernels, attention(): pl.pallas_call(functools.partial(attention_kernel, n_shards, chunk), out_...  11.5 us
    all_to_all x3, waiting for transfers between devices, exchange(): return lax.all_to_all(pieces, axes, split_axis=0, concat_axis=0, tiled=True)  11.3 us
    pallas_call x6, Pallas kernels, sum_of(): pl.pallas_call(sum_kernel, out_shape=jax.ShapeDtypeStruct(arrays[0].shape...  4.46 us
    pallas_call x1, Pallas kernels, gradients(): pl.pallas_call(functools.partial(gradients_kernel, n_y), out_shape=(jax.S...  4 us
  transfers between devices with their start and end apart: 45, of which 17 were waited for; matrix products, arithmetic and copies ran while one was open for 1% of the time, Pallas kernels for 15%

profile of v2, /device:TPU:1, one launch (start us, length us, event | category | flops | bytes accessed | tf_op | source)
XLA Modules:
  0.0 187.9 jit_solution(13646431963034420518)
XLA Ops:
  8.2 2.8 %collective-permute-start.7 = (bf16[16,8192]{1,0:T(8,128)(2,1)S(1)}, bf16[16,8192]{1,0:T(8,128)(2,1)S(1)}, u32[]{:S(2)}, u32[]{:S(2)}) collective-permute-start(bf16[16,8192]{1,0:T(8,128)(2,1)S(1)} %normalize.1.refs_8_), channel_id=1, source_target_pairs={{0,2},{2,0},{1,3},{3,1},{4,6},{6,4},{5,7},{7,5},{8,10},{10,8},{9,1... | collective-permute-start | bytes 786440 | tf_op jit(solution)/shard_map/ppermute | solution.py:31
  12.2 2.7 %collective-permute-start.19 = (bf16[16,1024]{1,0:T(8,128)(2,1)S(1)}, bf16[16,1024]{1,0:T(8,128)(2,1)S(1)}, u32[]{:S(2)}, u32[]{:S(2)}) collective-permute-start(bf16[16,1024]{1,0:T(8,128)(2,1)S(1)} %get-tuple-element.90), channel_id=1, source_target_pairs={{0,12},{4,8},{8,4},{12,0},{1,13},{5,9},{9,5},{13,1},{2,14},{6,10},... | collective-permute-start | bytes 98312 | tf_op jit(solution)/shard_map/ppermute | solution.py:31
  18.9 3.2 %collective-permute-start = (bf16[16,8192]{1,0:T(8,128)(2,1)S(1)}, bf16[16,8192]{1,0:T(8,128)(2,1)S(1)}, u32[]{:S(2)}, u32[]{:S(2)}) collective-permute-start(bf16[16,8192]{1,0:T(8,128)(2,1)S(1)} %normalize.1.refs_8_), channel_id=1, source_target_pairs={{0,1},{1,0},{2,3},{3,2},{4,5},{5,4},{6,7},{7,6},{8,9},{9,8},{10,11... | collective-permute-start | bytes 786440 | tf_op jit(solution)/shard_map/ppermute | solution.py:31
  25.3 5.0 %collective-permute-done.5.refs_11_ = bf16[16,8192]{1,0:T(8,128)(2,1)S(1)} collective-permute-done((bf16[16,8192]{1,0:T(8,128)(2,1)S(1)}, bf16[16,8192]{1,0:T(8,128)(2,1)S(1)}, u32[]{:S(2)}, u32[]{:S(2)}) %collective-permute-start.5) | collective-permute-done | bytes 262176 | tf_op jit(solution)/shard_map/ppermute | solution.py:31
  36.4 5.0 %collective-permute-done.13.refs_15_ = bf16[16,8192]{1,0:T(8,128)(2,1)S(1)} collective-permute-done((bf16[16,8192]{1,0:T(8,128)(2,1)S(1)}, bf16[16,8192]{1,0:T(8,128)(2,1)S(1)}, u32[]{:S(2)}, u32[]{:S(2)}) %collective-permute-start.13) | collective-permute-done | bytes 262176 | tf_op jit(solution)/shard_map/ppermute | solution.py:31
  45.9 6.0 %all-to-all-start = ((bf16[8,4,16,1024]{3,2,1,0:T(8,128)(2,1)}), bf16[8,4,16,1024]{3,2,1,0:T(8,128)(2,1)}, u32[]{:S(2)}, u32[]{:S(2)}) async-start(bf16[8,4,16,1024]{3,2,1,0:T(8,128)(2,1)} %broadcast_in_dim.9), calls=%async_computation | async-start | bytes 2097152 | tf_op jit(solution)/shard_map/all_to_all | solution.py:26
  53.5 11.5 %attention.1 = (bf16[256,512]{1,0:T(8,128)(2,1)S(1)}, bf16[128,4096]{1,0:T(8,128)(2,1)}, bf16[128,4096]{1,0:T(8,128)(2,1)S(1)}) custom-call(s32[4]{0:T(128)S(1)} %pad_add_fusion.sc_ref, bf16[16,8192]{1,0:T(8,128)(2,1)} %copy-done.3, bf16[16,8192]{1,0:T(8,128)(2,1)} %copy-done.5, bf16[16,8192]{1,0:T(8,128)(2,1)} %copy-done.6, bf16[16,8192]{1,0:T(8,128)(2,1)} %copy-done.7, ...), custom_call_target="tpu_custom_call" | custom-call | flops 3221225472 | bytes 16777216 | tf_op jit(solution)/shard_map/attention/pallas_call | solution.py:176
  65.6 7.4 %all-to-all-done = bf16[8,4,16,1024]{3,2,1,0:T(8,128)(2,1)} async-done(((bf16[8,4,16,1024]{3,2,1,0:T(8,128)(2,1)}), bf16[8,4,16,1024]{3,2,1,0:T(8,128)(2,1)}, u32[]{:S(2)}, u32[]{:S(2)}) %all-to-all-start) | async-done | bytes 1048608 | tf_op jit(solution)/shard_map/all_to_all | solution.py:26
  73.0 3.4 %student_proj_part.1 = (f32[8,16,1024]{2,1,0:T(8,128)S(1)}, bf16[8,16,1024]{2,1,0:T(8,128)(2,1)S(1)}, bf16[8,16,1024]{2,1,0:T(8,128)(2,1)S(1)}, bf16[8,16,1024]{2,1,0:T(8,128)(2,1)S(1)}) custom-call(s32[4]{0:T(128)S(1)} %pad_add_fusion.sc_ref, bf16[512,1024]{1,0:T(8,128)(2,1)} %bitcast.15.refs_0_, bf16[256,1024]{1,0:T(8,128)(2,1)} %refs_1_.3, ...), custom_call_target="tpu_custom_call" | custom-call | flops 1073741824 | bytes 4194304 | tf_op jit(solution)/shard_map/student_proj_part/pallas_call | solution.py:379
  76.5 3.6 %project.1 = (bf16[128,4096]{1,0:T(8,128)(2,1)S(1)}, bf16[128,4096]{1,0:T(8,128)(2,1)S(1)}) custom-call(bf16[256,512]{1,0:T(8,128)(2,1)S(1)} %get-tuple-element.52.m_ref, bf16[512,8192]{1,0:T(8,128)(2,1)} %bitcast.28), custom_call_target="tpu_custom_call" | custom-call | flops 1073741824 | bytes 6553600 | tf_op jit(solution)/shard_map/project/pallas_call | solution.py:226
  86.6 2.7 %collective-permute-start.29 = (bf16[16,8192]{1,0:T(8,128)(2,1)S(1)}, bf16[16,8192]{1,0:T(8,128)(2,1)S(1)}, u32[]{:S(2)}, u32[]{:S(2)}) collective-permute-start(bf16[16,8192]{1,0:T(8,128)(2,1)S(1)} %get-tuple-element.63), channel_id=1, source_target_pairs={{0,12},{4,8},{8,4},{12,0},{1,13},{5,9},{9,5},{13,1},{2,14},{6,10},... | collective-permute-start | bytes 786440 | tf_op jit(solution)/shard_map/ppermute | solution.py:31
  93.1 2.7 %collective-permute-start.33 = (bf16[8,16,1024]{2,1,0:T(8,128)(2,1)S(1)}, bf16[8,16,1024]{2,1,0:T(8,128)(2,1)S(1)}, u32[]{:S(2)}, u32[]{:S(2)}) collective-permute-start(bf16[8,16,1024]{2,1,0:T(8,128)(2,1)S(1)} %get-tuple-element.67), channel_id=1, source_target_pairs={{0,12},{4,8},{8,4},{12,0},{1,13},{5,9},{9,5},{13,1},{2,14},{6,10},... | collective-permute-start | bytes 786440 | tf_op jit(solution)/shard_map/ppermute | solution.py:31
  99.9 7.6 %collective-permute-done.32.refs_2_ = bf16[8,16,1024]{2,1,0:T(8,128)(2,1)S(1)} collective-permute-done((bf16[8,16,1024]{2,1,0:T(8,128)(2,1)S(1)}, bf16[8,16,1024]{2,1,0:T(8,128)(2,1)S(1)}, u32[]{:S(2)}, u32[]{:S(2)}) %collective-permute-start.32) | collective-permute-done | bytes 262176 | tf_op jit(solution)/shard_map/ppermute | solution.py:31
  107.7 8.8 %all_to_all.25.refs_6_ = bf16[8,16,1024]{2,1,0:T(8,128)(2,1)S(1)} all-to-all(bf16[8,16,1024]{2,1,0:T(8,128)(2,1)S(1)} %sum_of.8), channel_id=1, replica_groups=mesh['z'=4,'xl'=2,'y'=4,'xh'=2,'c'=2] {'z','xl'}, dimensions={0} | all-to-all | bytes 524288 | tf_op jit(solution)/shard_map/all_to_all | solution.py:26
  119.8 8.9 %all_to_all.26.refs_0_ = bf16[8,16,1152]{2,1,0:T(8,128)(2,1)S(1)} all-to-all(bf16[8,16,1152]{2,1,0:T(8,128)(2,1)S(1)} %get-tuple-element.69), channel_id=1, replica_groups=mesh['z'=4,'xl'=2,'y'=4,'xh'=2,'c'=2] {'z','xl'}, dimensions={0} | all-to-all | bytes 589824 | tf_op jit(solution)/shard_map/all_to_all | solution.py:26
  128.6 3.0 %collective-permute-start.35 = (bf16[8,16,1152]{2,1,0:T(8,128)(2,1)S(1)}, bf16[8,16,1152]{2,1,0:T(8,128)(2,1)S(1)}, u32[]{:S(2)}, u32[]{:S(2)}) collective-permute-start(bf16[8,16,1152]{2,1,0:T(8,128)(2,1)S(1)} %all_to_all.26.refs_0_), channel_id=1, source_target_pairs={{0,8},{4,12},{8,0},{12,4},{1,9},{5,13},{9,1},{13,5},{2,10},{6,14},... | collective-permute-start | bytes 884744 | tf_op jit(solution)/shard_map/ppermute | solution.py:31
  134.9 6.3 %collective-permute-done.35.refs_2_ = bf16[8,16,1152]{2,1,0:T(8,128)(2,1)S(1)} collective-permute-done((bf16[8,16,1152]{2,1,0:T(8,128)(2,1)S(1)}, bf16[8,16,1152]{2,1,0:T(8,128)(2,1)S(1)}, u32[]{:S(2)}, u32[]{:S(2)}) %collective-permute-start.35) | collective-permute-done | bytes 294944 | tf_op jit(solution)/shard_map/ppermute | solution.py:31
  141.1 4.9 %collective-permute-done.36.refs_3_ = bf16[8,16,1152]{2,1,0:T(8,128)(2,1)S(1)} collective-permute-done((bf16[8,16,1152]{2,1,0:T(8,128)(2,1)S(1)}, bf16[8,16,1152]{2,1,0:T(8,128)(2,1)S(1)}, u32[]{:S(2)}, u32[]{:S(2)}) %collective-permute-start.36) | collective-permute-done | bytes 294944 | tf_op jit(solution)/shard_map/ppermute | solution.py:31
  146.1 4.0 %gradients.1 = (bf16[4,2,4,16,1024]{4,3,2,1,0:T(8,128)(2,1)}, f32[8,128]{1,0:T(8,128)S(1)}, bf16[256,1024]{1,0:T(8,128)(2,1)}, bf16[256,1024]{1,0:T(8,128)(2,1)S...) custom-call(s32[4]{0:T(128)S(1)} %pad_add_fusion.sc_ref, bf16[8,16,1152]{2,1,0:T(8,128)(2,1)S(1)} %all_to_all.26.refs_0_, ...), custom_call_target="tpu_custom_call" | custom-call | tf_op jit(solution)/shard_map/gradients/pallas_call | solution.py:453
  153.4 3.5 %all-to-all-start.3 = ((bf16[4,2,4,16,1024]{4,3,2,1,0:T(8,128)(2,1)}), bf16[4,2,4,16,1024]{4,3,2,1,0:T(8,128)(2,1)S(1)}, u32[]{:S(2)}, u32[]{:S(2)}) async-start(bf16[4,2,4,16,1024]{4,3,2,1,0:T(8,128)(2,1)} %get-tuple-element.77), calls=%async_computation.3 | async-start | bytes 2097152 | tf_op jit(solution)/shard_map/all_to_all | solution.py:26
  159.0 3.3 %collective-permute-start.41 = (bf16[256,1024]{1,0:T(8,128)(2,1)}, bf16[256,1024]{1,0:T(8,128)(2,1)}, u32[]{:S(2)}, u32[]{:S(2)}) collective-permute-start(bf16[256,1024]{1,0:T(8,128)(2,1)} %sum_of.10), channel_id=1, source_target_pairs={{0,2},{2,0},{1,3},{3,1},{4,6},{6,4},{5,7},{7,5},{8,10},{10,8},{9,1... | collective-permute-start | bytes 1572872 | tf_op jit(solution)/shard_map/ppermute | solution.py:31
  163.9 10.6 %collective-permute-done.38 = f32[8,128]{1,0:T(8,128)S(1)} collective-permute-done((f32[8,128]{1,0:T(8,128)S(1)}, f32[8,128]{1,0:T(8,128)S(1)}, u32[]{:S(2)}, u32[]{:S(2)}) %collective-permute-start.38) | collective-permute-done | bytes 4128 | tf_op jit(solution)/shard_map/ppermute | solution.py:31
  176.6 3.4 %all-to-all-start.4 = ((bf16[8,16,1024]{2,1,0:T(8,128)(2,1)}), bf16[8,16,1024]{2,1,0:T(8,128)(2,1)S(1)}, u32[]{:S(2)}, u32[]{:S(2)}) async-start(bf16[8,16,1024]{2,1,0:T(8,128)(2,1)} %bitcast.18), calls=%async_computation.4 | async-start | bytes 524288 | tf_op jit(solution)/shard_map/all_to_all | solution.py:26
  182.2 3.9 %all-to-all-done.4 = bf16[8,16,1024]{2,1,0:T(8,128)(2,1)S(1)} async-done(((bf16[8,16,1024]{2,1,0:T(8,128)(2,1)}), bf16[8,16,1024]{2,1,0:T(8,128)(2,1)S(1)}, u32[]{:S(2)}, u32[]{:S(2)}) %all-to-all-start.4) | async-done | bytes 262176 | tf_op jit(solution)/shard_map/all_to_all | solution.py:26
  (113 shorter events, 60.1 us)
Async XLA Ops:
  0.6 52.1 %collective-permute-start.15 = (bf16[2,64,8192]{2,1,0:T(8,128)(2,1)}, bf16[2,64,8192]{2,1,0:T(8,128)(2,1)}, u32[]{:S(2)}, u32[]{:S(2)}) collective-permute-start(bf16[2,64,8192]{2,1,0:T(8,128)(2,1)} %bitcast.30), channel_id=1, source_target_pairs={{0,1},{1,0},{2,3},{3,2},{4,5},{5,4},{6,7},{7,6},{8,9},{9,8},{10,11... | collective-permute-start | bytes 6291464 | tf_op jit(solution)/shard_map/ppermute | solution.py:31
  11.1 11.1 %collective-permute-start.1 = (bf16[16,8192]{1,0:T(8,128)(2,1)S(1)}, bf16[16,8192]{1,0:T(8,128)(2,1)S(1)}, u32[]{:S(2)}, u32[]{:S(2)}) collective-permute-start(bf16[16,8192]{1,0:T(8,128)(2,1)S(1)} %normalize.1.refs_8_), channel_id=1, source_target_pairs={{0,4},{4,0},{8,12},{12,8},{1,5},{5,1},{9,13},{13,9},{2,6},{6,2},{1... | collective-permute-start | bytes 786440 | tf_op jit(solution)/shard_map/ppermute | solution.py:31
  11.1 12.3 %collective-permute-start.3 = (bf16[16,8192]{1,0:T(8,128)(2,1)S(1)}, bf16[16,8192]{1,0:T(8,128)(2,1)S(1)}, u32[]{:S(2)}, u32[]{:S(2)}) collective-permute-start(bf16[16,8192]{1,0:T(8,128)(2,1)S(1)} %normalize.1.refs_8_), channel_id=1, source_target_pairs={{0,8},{4,12},{8,0},{12,4},{1,9},{5,13},{9,1},{13,5},{2,10},{6,14},... | collective-permute-start | bytes 786440 | tf_op jit(solution)/shard_map/ppermute | solution.py:31
  16.5 13.9 %collective-permute-start.5 = (bf16[16,8192]{1,0:T(8,128)(2,1)S(1)}, bf16[16,8192]{1,0:T(8,128)(2,1)S(1)}, u32[]{:S(2)}, u32[]{:S(2)}) collective-permute-start(bf16[16,8192]{1,0:T(8,128)(2,1)S(1)} %normalize.1.refs_8_), channel_id=1, source_target_pairs={{0,12},{4,8},{8,4},{12,0},{1,13},{5,9},{9,5},{13,1},{2,14},{6,10},... | collective-permute-start | bytes 786440 | tf_op jit(solution)/shard_map/ppermute | solution.py:31
  18.9 13.7 %collective-permute-start = (bf16[16,8192]{1,0:T(8,128)(2,1)S(1)}, bf16[16,8192]{1,0:T(8,128)(2,1)S(1)}, u32[]{:S(2)}, u32[]{:S(2)}) collective-permute-start(bf16[16,8192]{1,0:T(8,128)(2,1)S(1)} %normalize.1.refs_8_), channel_id=1, source_target_pairs={{0,1},{1,0},{2,3},{3,2},{4,5},{5,4},{6,7},{7,6},{8,9},{9,8},{10,11... | collective-permute-start | bytes 786440 | tf_op jit(solution)/shard_map/ppermute | solution.py:31
  22.1 11.6 %collective-permute-start.9 = (bf16[16,8192]{1,0:T(8,128)(2,1)S(1)}, bf16[16,8192]{1,0:T(8,128)(2,1)S(1)}, u32[]{:S(2)}, u32[]{:S(2)}) collective-permute-start(bf16[16,8192]{1,0:T(8,128)(2,1)S(1)} %collective-permute-done.7.refs_12_), channel_id=1, source_target_pairs={{0,4},{4,0},{8,12},{12,8},{1,5},{5,1},{9,13},{13,9},{2,6},{6,2},{1... | collective-permute-start | bytes 786440 | tf_op jit(solution)/shard_map/ppermute | solution.py:31
  23.3 12.2 %collective-permute-start.11 = (bf16[16,8192]{1,0:T(8,128)(2,1)S(1)}, bf16[16,8192]{1,0:T(8,128)(2,1)S(1)}, u32[]{:S(2)}, u32[]{:S(2)}) collective-permute-start(bf16[16,8192]{1,0:T(8,128)(2,1)S(1)} %collective-permute-done.7.refs_12_), channel_id=1, source_target_pairs={{0,8},{4,12},{8,0},{12,4},{1,9},{5,13},{9,1},{13,5},{2,10},{6,14},... | collective-permute-start | bytes 786440 | tf_op jit(solution)/shard_map/ppermute | solution.py:31
  30.4 11.1 %collective-permute-start.13 = (bf16[16,8192]{1,0:T(8,128)(2,1)S(1)}, bf16[16,8192]{1,0:T(8,128)(2,1)S(1)}, u32[]{:S(2)}, u32[]{:S(2)}) collective-permute-start(bf16[16,8192]{1,0:T(8,128)(2,1)S(1)} %collective-permute-done.7.refs_12_), channel_id=1, source_target_pairs={{0,12},{4,8},{8,4},{12,0},{1,13},{5,9},{9,5},{13,1},{2,14},{6,10},... | collective-permute-start | bytes 786440 | tf_op jit(solution)/shard_map/ppermute | solution.py:31
  42.0 10.7 %collective-permute-start.12 = (bf16[16,8192]{1,0:T(8,128)(2,1)S(1)}, bf16[16,8192]{1,0:T(8,128)(2,1)S(1)}, u32[]{:S(2)}, u32[]{:S(2)}) collective-permute-start(bf16[16,8192]{1,0:T(8,128)(2,1)S(1)} %collective-permute-done.11.refs_14_), channel_id=1, source_target_pairs={{0,1},{1,0},{2,3},{3,2},{4,5},{5,4},{6,7},{7,6},{8,9},{9,8},{10,11... | collective-permute-start | bytes 786440 | tf_op jit(solution)/shard_map/ppermute | solution.py:31
  44.6 20.5 %collective-permute-start.16 = (bf16[256,1024]{1,0:T(8,128)(2,1)}, bf16[256,1024]{1,0:T(8,128)(2,1)}, u32[]{:S(2)}, u32[]{:S(2)}) collective-permute-start(bf16[256,1024]{1,0:T(8,128)(2,1)} %refs_1_.3), channel_id=1, source_target_pairs={{0,2},{2,0},{1,3},{3,1},{4,6},{6,4},{5,7},{7,5},{8,10},{10,8},{9,1... | collective-permute-start | bytes 1572872 | tf_op jit(solution)/shard_map/ppermute | solution.py:31
  45.9 27.1 %all-to-all-start = ((bf16[8,4,16,1024]{3,2,1,0:T(8,128)(2,1)}), bf16[8,4,16,1024]{3,2,1,0:T(8,128)(2,1)}, u32[]{:S(2)}, u32[]{:S(2)}) async-start(bf16[8,4,16,1024]{3,2,1,0:T(8,128)(2,1)} %broadcast_in_dim.9), calls=%async_computation | async-start | bytes 2097152 | tf_op jit(solution)/shard_map/all_to_all | solution.py:26
  52.0 13.6 %collective-permute-start.20 = (bf16[256,1024]{1,0:T(8,128)(2,1)}, bf16[256,1024]{1,0:T(8,128)(2,1)}, u32[]{:S(2)}, u32[]{:S(2)}) collective-permute-start(bf16[256,1024]{1,0:T(8,128)(2,1)} %refs_1_.3), channel_id=1, source_target_pairs={{0,1},{1,0},{2,3},{3,2},{4,5},{5,4},{6,7},{7,6},{8,9},{9,8},{10,11... | collective-permute-start | bytes 1572872 | tf_op jit(solution)/shard_map/ppermute | solution.py:31
  65.1 16.2 %collective-permute-start.22 = (bf16[128,4096]{1,0:T(8,128)(2,1)}, bf16[128,4096]{1,0:T(8,128)(2,1)S(1)}, u32[]{:S(2)}, u32[]{:S(2)}) collective-permute-start(bf16[128,4096]{1,0:T(8,128)(2,1)} %get-tuple-element.54), channel_id=1, source_target_pairs={{0,1},{1,0},{2,3},{3,2},{4,5},{5,4},{6,7},{7,6},{8,9},{9,8},{10,11... | collective-permute-start | bytes 3145736 | tf_op jit(solution)/shard_map/ppermute | solution.py:31
  90.2 17.3 %collective-permute-start.32 = (bf16[8,16,1024]{2,1,0:T(8,128)(2,1)S(1)}, bf16[8,16,1024]{2,1,0:T(8,128)(2,1)S(1)}, u32[]{:S(2)}, u32[]{:S(2)}) collective-permute-start(bf16[8,16,1024]{2,1,0:T(8,128)(2,1)S(1)} %get-tuple-element.66), channel_id=1, source_target_pairs={{0,8},{4,12},{8,0},{12,4},{1,9},{5,13},{9,1},{13,5},{2,10},{6,14},... | collective-permute-start | bytes 786440 | tf_op jit(solution)/shard_map/ppermute | solution.py:31
  93.1 14.4 %collective-permute-start.33 = (bf16[8,16,1024]{2,1,0:T(8,128)(2,1)S(1)}, bf16[8,16,1024]{2,1,0:T(8,128)(2,1)S(1)}, u32[]{:S(2)}, u32[]{:S(2)}) collective-permute-start(bf16[8,16,1024]{2,1,0:T(8,128)(2,1)S(1)} %get-tuple-element.67), channel_id=1, source_target_pairs={{0,12},{4,8},{8,4},{12,0},{1,13},{5,9},{9,5},{13,1},{2,14},{6,10},... | collective-permute-start | bytes 786440 | tf_op jit(solution)/shard_map/ppermute | solution.py:31
  96.0 20.5 %collective-permute-start.24 = (bf16[16,8192]{1,0:T(8,128)(2,1)S(1)}, bf16[16,8192]{1,0:T(8,128)(2,1)S(1)}, u32[]{:S(2)}, u32[]{:S(2)}) collective-permute-start(bf16[16,8192]{1,0:T(8,128)(2,1)S(1)} %get-tuple-element.57), channel_id=1, source_target_pairs={{0,4},{4,0},{8,12},{12,8},{1,5},{5,1},{9,13},{13,9},{2,6},{6,2},{1... | collective-permute-start | bytes 786440 | tf_op jit(solution)/shard_map/ppermute | solution.py:31
  96.1 21.0 %collective-permute-start.25 = (bf16[16,8192]{1,0:T(8,128)(2,1)S(1)}, bf16[16,8192]{1,0:T(8,128)(2,1)S(1)}, u32[]{:S(2)}, u32[]{:S(2)}) collective-permute-start(bf16[16,8192]{1,0:T(8,128)(2,1)S(1)} %get-tuple-element.58), channel_id=1, source_target_pairs={{0,12},{4,8},{8,4},{12,0},{1,13},{5,9},{9,5},{13,1},{2,14},{6,10},... | collective-permute-start | bytes 786440 | tf_op jit(solution)/shard_map/ppermute | solution.py:31
  99.4 17.6 %collective-permute-start.30 = (bf16[16,8192]{1,0:T(8,128)(2,1)S(1)}, bf16[16,8192]{1,0:T(8,128)(2,1)S(1)}, u32[]{:S(2)}, u32[]{:S(2)}) collective-permute-start(bf16[16,8192]{1,0:T(8,128)(2,1)S(1)} %sum_of.7), channel_id=1, source_target_pairs={{0,2},{2,0},{1,3},{3,1},{4,6},{6,4},{5,7},{7,5},{8,10},{10,8},{9,1... | collective-permute-start | bytes 786440 | tf_op jit(solution)/shard_map/ppermute | solution.py:31
  107.5 11.2 %collective-permute-start.27 = (bf16[16,8192]{1,0:T(8,128)(2,1)S(1)}, bf16[16,8192]{1,0:T(8,128)(2,1)S(1)}, u32[]{:S(2)}, u32[]{:S(2)}) collective-permute-start(bf16[16,8192]{1,0:T(8,128)(2,1)S(1)} %sum_of.6), channel_id=1, source_target_pairs={{0,8},{4,12},{8,0},{12,4},{1,9},{5,13},{9,1},{13,5},{2,10},{6,14},... | collective-permute-start | bytes 786440 | tf_op jit(solution)/shard_map/ppermute | solution.py:31
  128.6 12.5 %collective-permute-start.35 = (bf16[8,16,1152]{2,1,0:T(8,128)(2,1)S(1)}, bf16[8,16,1152]{2,1,0:T(8,128)(2,1)S(1)}, u32[]{:S(2)}, u32[]{:S(2)}) collective-permute-start(bf16[8,16,1152]{2,1,0:T(8,128)(2,1)S(1)} %all_to_all.26.refs_0_), channel_id=1, source_target_pairs={{0,8},{4,12},{8,0},{12,4},{1,9},{5,13},{9,1},{13,5},{2,10},{6,14},... | collective-permute-start | bytes 884744 | tf_op jit(solution)/shard_map/ppermute | solution.py:31
  131.6 14.4 %collective-permute-start.36 = (bf16[8,16,1152]{2,1,0:T(8,128)(2,1)S(1)}, bf16[8,16,1152]{2,1,0:T(8,128)(2,1)S(1)}, u32[]{:S(2)}, u32[]{:S(2)}) collective-permute-start(bf16[8,16,1152]{2,1,0:T(8,128)(2,1)S(1)} %all_to_all.26.refs_0_), channel_id=1, source_target_pairs={{0,12},{4,8},{8,4},{12,0},{1,13},{5,9},{9,5},{13,1},{2,14},{6,10},... | collective-permute-start | bytes 884744 | tf_op jit(solution)/shard_map/ppermute | solution.py:31
  153.4 22.4 %all-to-all-start.3 = ((bf16[4,2,4,16,1024]{4,3,2,1,0:T(8,128)(2,1)}), bf16[4,2,4,16,1024]{4,3,2,1,0:T(8,128)(2,1)S(1)}, u32[]{:S(2)}, u32[]{:S(2)}) async-start(bf16[4,2,4,16,1024]{4,3,2,1,0:T(8,128)(2,1)} %get-tuple-element.77), calls=%async_computation.3 | async-start | bytes 2097152 | tf_op jit(solution)/shard_map/all_to_all | solution.py:26
  156.9 18.7 %collective-permute-start.39 = (bf16[256,1024]{1,0:T(8,128)(2,1)}, bf16[256,1024]{1,0:T(8,128)(2,1)S(1)}, u32[]{:S(2)}, u32[]{:S(2)}) collective-permute-start(bf16[256,1024]{1,0:T(8,128)(2,1)} %copy-done.2), channel_id=1, source_target_pairs={{0,1},{1,0},{2,3},{3,2},{4,5},{5,4},{6,7},{7,6},{8,9},{9,8},{10,11... | collective-permute-start | bytes 1572872 | tf_op jit(solution)/shard_map/ppermute | solution.py:31
  159.0 21.0 %collective-permute-start.41 = (bf16[256,1024]{1,0:T(8,128)(2,1)}, bf16[256,1024]{1,0:T(8,128)(2,1)}, u32[]{:S(2)}, u32[]{:S(2)}) collective-permute-start(bf16[256,1024]{1,0:T(8,128)(2,1)} %sum_of.10), channel_id=1, source_target_pairs={{0,2},{2,0},{1,3},{3,1},{4,6},{6,4},{5,7},{7,5},{8,10},{10,8},{9,1... | collective-permute-start | bytes 1572872 | tf_op jit(solution)/shard_map/ppermute | solution.py:31
  (32 other events, 238.1 us)

commit v3 on v2

--- a/solution.py
+++ b/solution.py
@@ -416,7 +416,8 @@
 
 def gradients_kernel(n_y, sc_ref, *refs):
     slope_refs, tokens_ref, proj_refs = refs[:n_y], refs[n_y], refs[n_y + 1 : n_y + 5]
-    gs_ref, loss_ref, away_far, away_near, stay_far, stay_near, all_ref = refs[n_y + 5 :]
+    loss_ref, away_far, away_near, stay_far, stay_near = refs[n_y + 5 : n_y + 10]
+    piece_refs, all_ref, gs_ref = refs[n_y + 10 : -2], refs[-2], refs[-1]
     slope = stacked(slope_refs, all_ref)
     width, size = proj_refs[0].shape
     core, xh = sc_ref[0], sc_ref[1]
@@ -435,6 +436,8 @@
         y = y.astype(jnp.bfloat16).reshape(n_z * n_xl, n_y, rows, size)
         for k in range(n_y):
             gs_ref[:, :, sc_ref[2] ^ k, :, cut] = y[:, k].reshape(n_z, n_xl, rows, size)
+    for k, out in enumerate(piece_refs):
+        out[...] = gs_ref[sc_ref[4] ^ k]
     loss = None
     for r in slope_refs:
         part = jnp.sum(f32(r[:, :, width:]), axis=(0, 1), keepdims=True)
@@ -449,43 +452,28 @@
     width, size = proj_t[0].shape
     low = jax.ShapeDtypeStruct((size, width), jnp.bfloat16)
     high = jax.ShapeDtypeStruct((size, width), jnp.float32)
+    shape = (n_z, n_sec // n_z, n_y, rows, size * len(proj_t))
+    piece = jax.ShapeDtypeStruct(shape[1:], jnp.bfloat16)
     inputs = (tokens_t, *proj_t)
     return pl.pallas_call(
         functools.partial(gradients_kernel, n_y),
         out_shape=(
-            jax.ShapeDtypeStruct(
-                (n_z, n_sec // n_z, n_y, rows, size * len(proj_t)), jnp.bfloat16
-            ),
             jax.ShapeDtypeStruct((8, 128), jnp.float32),
             low,
             low,
             high,
             high,
+            *(piece,) * n_z,
         ),
         in_specs=[SM] + [VM] * (n_y + len(inputs)),
-        out_specs=(VM,) * 6,
-        scratch_shapes=[pltpu.VMEM((n_sec, n_y, rows, width), jnp.bfloat16)],
-        compiler_params=kernel_params(10),
+        out_specs=(VM,) * (5 + n_z),
+        scratch_shapes=[
+            pltpu.VMEM((n_sec, n_y, rows, width), jnp.bfloat16),
+            pltpu.VMEM(shape, jnp.bfloat16),
+        ],
+        compiler_params=kernel_params(12),
         name="gradients",
     )(scalars, *slope, *inputs)
-
-
-def leading_sum_kernel(g_ref, o_ref):
-    total = f32(g_ref[0])
-    for s in range(1, g_ref.shape[0]):
-        total += f32(g_ref[s])
-    o_ref[...] = total.astype(o_ref.dtype)
-
-
-def leading_sum(g):
-    return pl.pallas_call(
-        leading_sum_kernel,
-        out_shape=jax.ShapeDtypeStruct(g.shape[1:], g.dtype),
-        in_specs=[VM],
-        out_specs=VM,
-        compiler_params=kernel_params(6),
-        name="leading_sum",
-    )(g)
 
 
 def place_kernel(g_ref, o_ref):
@@ -535,7 +523,8 @@
     n_tp = lax.axis_size(TP)
     x = teacher_rows[0]
     rows, width = x.shape
-    scalars = jnp.stack([core, xh, y, doc_start[0]])
+    z = lax.axis_index("z").astype(jnp.int32)
+    scalars = jnp.stack([core, xh, y, doc_start[0], z])
 
     feats = student_rows.shape[2] // n_y
     picked = [
@@ -591,10 +580,11 @@
     slope, tokens = tied(slope, tokens)
     slope = to_columns(slope, n_y)
     tokens_t, *proj_t = turned((tokens, *proj))
-    grad_s, loss, away_far, away_near, stay_far, stay_near = gradients(
+    loss, away_far, away_near, stay_far, stay_near, *grad_s = gradients(
         scalars, slope, tokens_t, proj_t, lax.axis_size("z")
     )
-    grad_s = exchange(grad_s, "z")
+    for k in range(1, len(grad_s)):
+        grad_s[k] = swap(grad_s[k], "z", k)
     loss = loss + swap(loss, "c", 1)
     away_far = swap(away_far, "c", 1)
     away_near = swap(away_near, "c", 1)
@@ -602,8 +592,8 @@
     across = swap(sum_of((stay_far, away_far), jnp.bfloat16), "xh", 1)
     nearly = sum_of((stay_near, away_near), jnp.float32)
     loss = loss[:1, :1] / (n_sec * n_tp * rows)
-    grad_s, loss, nearly = tied(grad_s, loss, nearly)
-    grad_s = leading_sum(grad_s)
+    grad_s[2], nearly = tied(grad_s[2], nearly)
+    grad_s = sum_of(grad_s, jnp.bfloat16)
     shape = grad_s.shape
     grad_s = exchange(grad_s.reshape(-1, *shape[2:]), ("xl", "y")).reshape(shape)
     grad_projector = sum_of((nearly, across), jnp.float32)

time: 189 us -> 185 us (0.979)
  Pallas kernels: 33.6 us -> 29.8 us
  waiting for transfers between devices: 65 us -> 67.9 us
  local copies, waits for them, and re-layouts: 4.98 us -> 3.09 us
    ppermute x42 -> x45, waiting for transfers between devices: 53.7 us -> 61.1 us  [swap(): return lax.ppermute(value, axis, [(i, i ^ apart) for i in range(count)])]
    all_to_all x3 -> x2, waiting for transfers between devices: 11.3 us -> 6.78 us  [exchange(): return lax.all_to_all(pieces, axes, split_axis=0, concat_axis=0, tiled=True)]
    all_to_all x3 -> x2, starting transfers between devices: 13 us -> 8.91 us  [exchange(): return lax.all_to_all(pieces, axes, split_axis=0, concat_axis=0, tiled=True)]
    ppermute x42 -> x45, starting transfers between devices: 50.2 us -> 53.8 us  [swap(): return lax.ppermute(value, axis, [(i, i ^ apart) for i in range(count)])]
    pallas_call x6 -> x7, Pallas kernels: 4.46 us -> 2.43 us  [sum_of(): pl.pallas_call(sum_kernel, out_shape=jax.ShapeDtypeStruct(arrays[0].shape...]
    unnamed x22 -> x16, local copies, waits for them, and re-layouts: 2.54 us -> 0.57 us
  transfers between devices with their start and end apart: 45 -> 47, of which waited for: 17 -> 21; matrix products, arithmetic and copies ran while one was open for 1% -> 1% of each run, Pallas kernels for 15% -> 13%
where the time goes in v3:
time: 185 us
  waiting for transfers between devices  67.9 us (37%)
  starting transfers between devices  62.8 us (34%)
  Pallas kernels  29.8 us (16%)
  blocking collectives  17.7 us (10%)
  between operations  3.3 us (2%)
  local copies, waits for them, and re-layouts  3.09 us (2%)
    ppermute x45, waiting for transfers between devices, swap(): return lax.ppermute(value, axis, [(i, i ^ apart) for i in range(count)])  61.1 us
    ppermute x45, starting transfers between devices, swap(): return lax.ppermute(value, axis, [(i, i ^ apart) for i in range(count)])  53.8 us
    all_to_all x2, blocking collectives, exchange(): return lax.all_to_all(pieces, axes, split_axis=0, concat_axis=0, tiled=True)  17.7 us
    pallas_call x1, Pallas kernels, attention(): pl.pallas_call(functools.partial(attention_kernel, n_shards, chunk), out_...  11.5 us
    all_to_all x2, starting transfers between devices, exchange(): return lax.all_to_all(pieces, axes, split_axis=0, concat_axis=0, tiled=True)  8.91 us
    all_to_all x2, waiting for transfers between devices, exchange(): return lax.all_to_all(pieces, axes, split_axis=0, concat_axis=0, tiled=True)  6.78 us
  transfers between devices with their start and end apart: 47, of which 21 were waited for; matrix products, arithmetic and copies ran while one was open for 1% of the time, Pallas kernels for 13%

profile of v3, /device:TPU:1, one launch (start us, length us, event | category | flops | bytes accessed | tf_op | source)
XLA Modules:
  0.0 184.6 jit_solution(5713979163022040738)
XLA Ops:
  8.2 2.8 %collective-permute-start.7 = (bf16[16,8192]{1,0:T(8,128)(2,1)S(1)}, bf16[16,8192]{1,0:T(8,128)(2,1)S(1)}, u32[]{:S(2)}, u32[]{:S(2)}) collective-permute-start(bf16[16,8192]{1,0:T(8,128)(2,1)S(1)} %normalize.1.refs_8_), channel_id=1, source_target_pairs={{0,2},{2,0},{1,3},{3,1},{4,6},{6,4},{5,7},{7,5},{8,10},{10,8},{9,1... | collective-permute-start | bytes 786440 | tf_op jit(solution)/shard_map/ppermute | solution.py:31
  12.2 2.7 %collective-permute-start.19 = (bf16[16,1024]{1,0:T(8,128)(2,1)S(1)}, bf16[16,1024]{1,0:T(8,128)(2,1)S(1)}, u32[]{:S(2)}, u32[]{:S(2)}) collective-permute-start(bf16[16,1024]{1,0:T(8,128)(2,1)S(1)} %get-tuple-element.94), channel_id=1, source_target_pairs={{0,12},{4,8},{8,4},{12,0},{1,13},{5,9},{9,5},{13,1},{2,14},{6,10},... | collective-permute-start | bytes 98312 | tf_op jit(solution)/shard_map/ppermute | solution.py:31
  18.9 3.2 %collective-permute-start = (bf16[16,8192]{1,0:T(8,128)(2,1)S(1)}, bf16[16,8192]{1,0:T(8,128)(2,1)S(1)}, u32[]{:S(2)}, u32[]{:S(2)}) collective-permute-start(bf16[16,8192]{1,0:T(8,128)(2,1)S(1)} %normalize.1.refs_8_), channel_id=1, source_target_pairs={{0,1},{1,0},{2,3},{3,2},{4,5},{5,4},{6,7},{7,6},{8,9},{9,8},{10,11... | collective-permute-start | bytes 786440 | tf_op jit(solution)/shard_map/ppermute | solution.py:31
  25.3 5.0 %collective-permute-done.5.refs_11_ = bf16[16,8192]{1,0:T(8,128)(2,1)S(1)} collective-permute-done((bf16[16,8192]{1,0:T(8,128)(2,1)S(1)}, bf16[16,8192]{1,0:T(8,128)(2,1)S(1)}, u32[]{:S(2)}, u32[]{:S(2)}) %collective-permute-start.5) | collective-permute-done | bytes 262176 | tf_op jit(solution)/shard_map/ppermute | solution.py:31
  36.4 5.0 %collective-permute-done.13.refs_15_ = bf16[16,8192]{1,0:T(8,128)(2,1)S(1)} collective-permute-done((bf16[16,8192]{1,0:T(8,128)(2,1)S(1)}, bf16[16,8192]{1,0:T(8,128)(2,1)S(1)}, u32[]{:S(2)}, u32[]{:S(2)}) %collective-permute-start.13) | collective-permute-done | bytes 262176 | tf_op jit(solution)/shard_map/ppermute | solution.py:31
  44.9 5.5 %all-to-all-start = ((bf16[8,4,16,1024]{3,2,1,0:T(8,128)(2,1)}), bf16[8,4,16,1024]{3,2,1,0:T(8,128)(2,1)}, u32[]{:S(2)}, u32[]{:S(2)}) async-start(bf16[8,4,16,1024]{3,2,1,0:T(8,128)(2,1)} %broadcast_in_dim.9), calls=%async_computation | async-start | bytes 2097152 | tf_op jit(solution)/shard_map/all_to_all | solution.py:26
  52.2 11.5 %attention.1 = (bf16[256,512]{1,0:T(8,128)(2,1)S(1)}, bf16[128,4096]{1,0:T(8,128)(2,1)}, bf16[128,4096]{1,0:T(8,128)(2,1)S(1)}) custom-call(s32[5]{0:T(128)S(1)} %stack.32.sc_ref, bf16[16,8192]{1,0:T(8,128)(2,1)} %copy-done.2, bf16[16,8192]{1,0:T(8,128)(2,1)} %copy-done.4, bf16[16,8192]{1,0:T(8,128)(2,1)} %copy-done.5, bf16[16,8192]{1,0:T(8,128)(2,1)} %copy-done.6, ...), custom_call_target="tpu_custom_call" | custom-call | flops 3221225472 | bytes 16777216 | tf_op jit(solution)/shard_map/attention/pallas_call | solution.py:176
  64.4 6.8 %all-to-all-done = bf16[8,4,16,1024]{3,2,1,0:T(8,128)(2,1)} async-done(((bf16[8,4,16,1024]{3,2,1,0:T(8,128)(2,1)}), bf16[8,4,16,1024]{3,2,1,0:T(8,128)(2,1)}, u32[]{:S(2)}, u32[]{:S(2)}) %all-to-all-start) | async-done | bytes 1048608 | tf_op jit(solution)/shard_map/all_to_all | solution.py:26
  71.2 3.4 %student_proj_part.1 = (f32[8,16,1024]{2,1,0:T(8,128)S(1)}, bf16[8,16,1024]{2,1,0:T(8,128)(2,1)S(1)}, bf16[8,16,1024]{2,1,0:T(8,128)(2,1)S(1)}, bf16[8,16,1024]{2,1,0:T(8,128)(2,1)S(1)}) custom-call(s32[5]{0:T(128)S(1)} %stack.32.sc_ref, bf16[512,1024]{1,0:T(8,128)(2,1)} %bitcast.16.refs_0_, bf16[256,1024]{1,0:T(8,128)(2,1)} %refs_1_.3, ...), custom_call_target="tpu_custom_call" | custom-call | flops 1073741824 | bytes 4194304 | tf_op jit(solution)/shard_map/student_proj_part/pallas_call | solution.py:379
  74.6 3.6 %project.1 = (bf16[128,4096]{1,0:T(8,128)(2,1)S(1)}, bf16[128,4096]{1,0:T(8,128)(2,1)S(1)}) custom-call(bf16[256,512]{1,0:T(8,128)(2,1)S(1)} %get-tuple-element.54.m_ref, bf16[512,8192]{1,0:T(8,128)(2,1)} %bitcast.29), custom_call_target="tpu_custom_call" | custom-call | flops 1073741824 | bytes 6553600 | tf_op jit(solution)/shard_map/project/pallas_call | solution.py:226
  85.0 2.7 %collective-permute-start.29 = (bf16[16,8192]{1,0:T(8,128)(2,1)S(1)}, bf16[16,8192]{1,0:T(8,128)(2,1)S(1)}, u32[]{:S(2)}, u32[]{:S(2)}) collective-permute-start(bf16[16,8192]{1,0:T(8,128)(2,1)S(1)} %get-tuple-element.65), channel_id=1, source_target_pairs={{0,12},{4,8},{8,4},{12,0},{1,13},{5,9},{9,5},{13,1},{2,14},{6,10},... | collective-permute-start | bytes 786440 | tf_op jit(solution)/shard_map/ppermute | solution.py:31
  91.6 2.7 %collective-permute-start.33 = (bf16[8,16,1024]{2,1,0:T(8,128)(2,1)S(1)}, bf16[8,16,1024]{2,1,0:T(8,128)(2,1)S(1)}, u32[]{:S(2)}, u32[]{:S(2)}) collective-permute-start(bf16[8,16,1024]{2,1,0:T(8,128)(2,1)S(1)} %get-tuple-element.69), channel_id=1, source_target_pairs={{0,12},{4,8},{8,4},{12,0},{1,13},{5,9},{9,5},{13,1},{2,14},{6,10},... | collective-permute-start | bytes 786440 | tf_op jit(solution)/shard_map/ppermute | solution.py:31
  98.4 7.6 %collective-permute-done.32.refs_2_ = bf16[8,16,1024]{2,1,0:T(8,128)(2,1)S(1)} collective-permute-done((bf16[8,16,1024]{2,1,0:T(8,128)(2,1)S(1)}, bf16[8,16,1024]{2,1,0:T(8,128)(2,1)S(1)}, u32[]{:S(2)}, u32[]{:S(2)}) %collective-permute-start.32) | collective-permute-done | bytes 262176 | tf_op jit(solution)/shard_map/ppermute | solution.py:31
  106.1 8.8 %all_to_all.20.refs_6_ = bf16[8,16,1024]{2,1,0:T(8,128)(2,1)S(1)} all-to-all(bf16[8,16,1024]{2,1,0:T(8,128)(2,1)S(1)} %sum_of.9), channel_id=1, replica_groups=mesh['z'=4,'xl'=2,'y'=4,'xh'=2,'c'=2] {'z','xl'}, dimensions={0} | all-to-all | bytes 524288 | tf_op jit(solution)/shard_map/all_to_all | solution.py:26
  118.2 8.9 %all_to_all.21.refs_0_ = bf16[8,16,1152]{2,1,0:T(8,128)(2,1)S(1)} all-to-all(bf16[8,16,1152]{2,1,0:T(8,128)(2,1)S(1)} %get-tuple-element.71), channel_id=1, replica_groups=mesh['z'=4,'xl'=2,'y'=4,'xh'=2,'c'=2] {'z','xl'}, dimensions={0} | all-to-all | bytes 589824 | tf_op jit(solution)/shard_map/all_to_all | solution.py:26
  127.1 3.0 %collective-permute-start.35 = (bf16[8,16,1152]{2,1,0:T(8,128)(2,1)S(1)}, bf16[8,16,1152]{2,1,0:T(8,128)(2,1)S(1)}, u32[]{:S(2)}, u32[]{:S(2)}) collective-permute-start(bf16[8,16,1152]{2,1,0:T(8,128)(2,1)S(1)} %all_to_all.21.refs_0_), channel_id=1, source_target_pairs={{0,8},{4,12},{8,0},{12,4},{1,9},{5,13},{9,1},{13,5},{2,10},{6,14},... | collective-permute-start | bytes 884744 | tf_op jit(solution)/shard_map/ppermute | solution.py:31
  133.3 6.3 %collective-permute-done.35.refs_2_ = bf16[8,16,1152]{2,1,0:T(8,128)(2,1)S(1)} collective-permute-done((bf16[8,16,1152]{2,1,0:T(8,128)(2,1)S(1)}, bf16[8,16,1152]{2,1,0:T(8,128)(2,1)S(1)}, u32[]{:S(2)}, u32[]{:S(2)}) %collective-permute-start.35) | collective-permute-done | bytes 294944 | tf_op jit(solution)/shard_map/ppermute | solution.py:31
  139.6 4.9 %collective-permute-done.36.refs_3_ = bf16[8,16,1152]{2,1,0:T(8,128)(2,1)S(1)} collective-permute-done((bf16[8,16,1152]{2,1,0:T(8,128)(2,1)S(1)}, bf16[8,16,1152]{2,1,0:T(8,128)(2,1)S(1)}, u32[]{:S(2)}, u32[]{:S(2)}) %collective-permute-start.36) | collective-permute-done | bytes 294944 | tf_op jit(solution)/shard_map/ppermute | solution.py:31
  144.5 3.1 %gradients.1 = (f32[8,128]{1,0:T(8,128)S(1)}, bf16[256,1024]{1,0:T(8,128)(2,1)S(1)}, bf16[256,1024]{1,0:T(8,128)(2,1)S(1)}, f32[256,1024]{1,0:T(8,128)S(1)}, f32...) custom-call(s32[5]{0:T(128)S(1)} %stack.32.sc_ref, ...), custom_call_target="tpu_custom_call" | custom-call | tf_op jit(solution)/shard_map/gradients/pallas_call | solution.py:458
  151.9 3.3 %collective-permute-start.44 = (bf16[256,1024]{1,0:T(8,128)(2,1)S(1)}, bf16[256,1024]{1,0:T(8,128)(2,1)S(1)}, u32[]{:S(2)}, u32[]{:S(2)}) collective-permute-start(bf16[256,1024]{1,0:T(8,128)(2,1)S(1)} %sum_of.12), channel_id=1, source_target_pairs={{0,2},{2,0},{1,3},{3,1},{4,6},{6,4},{5,7},{7,5},{8,10},{10,8},{9,1... | collective-permute-start | bytes 1572872 | tf_op jit(solution)/shard_map/ppermute | solution.py:31
  158.6 5.4 %collective-permute-done.40.refs_2_ = bf16[2,4,16,1024]{3,2,1,0:T(8,128)(2,1)S(1)} collective-permute-done((bf16[2,4,16,1024]{3,2,1,0:T(8,128)(2,1)S(1)}, bf16[2,4,16,1024]{3,2,1,0:T(8,128)(2,1)S(1)}, u32[]{:S(2)}, u32[]{:S(2)}) %collective-permute-start.40) | collective-permute-done | bytes 262176 | tf_op jit(solution)/shard_map/ppermute | solution.py:31
  164.0 4.2 %collective-permute-done.39.refs_1_ = bf16[2,4,16,1024]{3,2,1,0:T(8,128)(2,1)S(1)} collective-permute-done((bf16[2,4,16,1024]{3,2,1,0:T(8,128)(2,1)S(1)}, bf16[2,4,16,1024]{3,2,1,0:T(8,128)(2,1)S(1)}, u32[]{:S(2)}, u32[]{:S(2)}) %collective-permute-start.39) | collective-permute-done | bytes 262176 | tf_op jit(solution)/shard_map/ppermute | solution.py:31
  171.4 3.4 %all-to-all-start.3 = ((bf16[8,16,1024]{2,1,0:T(8,128)(2,1)}), bf16[8,16,1024]{2,1,0:T(8,128)(2,1)S(1)}, u32[]{:S(2)}, u32[]{:S(2)}) async-start(bf16[8,16,1024]{2,1,0:T(8,128)(2,1)} %bitcast.19), calls=%async_computation.3 | async-start | bytes 524288 | tf_op jit(solution)/shard_map/all_to_all | solution.py:26
  176.3 4.1 %collective-permute-done.38 = f32[8,128]{1,0:T(8,128)S(1)} collective-permute-done((f32[8,128]{1,0:T(8,128)S(1)}, f32[8,128]{1,0:T(8,128)S(1)}, u32[]{:S(2)}, u32[]{:S(2)}) %collective-permute-start.38) | collective-permute-done | bytes 4128 | tf_op jit(solution)/shard_map/ppermute | solution.py:31
  (111 shorter events, 63.1 us)
Async XLA Ops:
  0.6 51.6 %collective-permute-start.15 = (bf16[2,64,8192]{2,1,0:T(8,128)(2,1)}, bf16[2,64,8192]{2,1,0:T(8,128)(2,1)}, u32[]{:S(2)}, u32[]{:S(2)}) collective-permute-start(bf16[2,64,8192]{2,1,0:T(8,128)(2,1)} %bitcast.31), channel_id=1, source_target_pairs={{0,1},{1,0},{2,3},{3,2},{4,5},{5,4},{6,7},{7,6},{8,9},{9,8},{10,11... | collective-permute-start | bytes 6291464 | tf_op jit(solution)/shard_map/ppermute | solution.py:31
  11.1 11.1 %collective-permute-start.1 = (bf16[16,8192]{1,0:T(8,128)(2,1)S(1)}, bf16[16,8192]{1,0:T(8,128)(2,1)S(1)}, u32[]{:S(2)}, u32[]{:S(2)}) collective-permute-start(bf16[16,8192]{1,0:T(8,128)(2,1)S(1)} %normalize.1.refs_8_), channel_id=1, source_target_pairs={{0,4},{4,0},{8,12},{12,8},{1,5},{5,1},{9,13},{13,9},{2,6},{6,2},{1... | collective-permute-start | bytes 786440 | tf_op jit(solution)/shard_map/ppermute | solution.py:31
  11.1 12.3 %collective-permute-start.3 = (bf16[16,8192]{1,0:T(8,128)(2,1)S(1)}, bf16[16,8192]{1,0:T(8,128)(2,1)S(1)}, u32[]{:S(2)}, u32[]{:S(2)}) collective-permute-start(bf16[16,8192]{1,0:T(8,128)(2,1)S(1)} %normalize.1.refs_8_), channel_id=1, source_target_pairs={{0,8},{4,12},{8,0},{12,4},{1,9},{5,13},{9,1},{13,5},{2,10},{6,14},... | collective-permute-start | bytes 786440 | tf_op jit(solution)/shard_map/ppermute | solution.py:31
  16.5 13.9 %collective-permute-start.5 = (bf16[16,8192]{1,0:T(8,128)(2,1)S(1)}, bf16[16,8192]{1,0:T(8,128)(2,1)S(1)}, u32[]{:S(2)}, u32[]{:S(2)}) collective-permute-start(bf16[16,8192]{1,0:T(8,128)(2,1)S(1)} %normalize.1.refs_8_), channel_id=1, source_target_pairs={{0,12},{4,8},{8,4},{12,0},{1,13},{5,9},{9,5},{13,1},{2,14},{6,10},... | collective-permute-start | bytes 786440 | tf_op jit(solution)/shard_map/ppermute | solution.py:31
  18.9 13.7 %collective-permute-start = (bf16[16,8192]{1,0:T(8,128)(2,1)S(1)}, bf16[16,8192]{1,0:T(8,128)(2,1)S(1)}, u32[]{:S(2)}, u32[]{:S(2)}) collective-permute-start(bf16[16,8192]{1,0:T(8,128)(2,1)S(1)} %normalize.1.refs_8_), channel_id=1, source_target_pairs={{0,1},{1,0},{2,3},{3,2},{4,5},{5,4},{6,7},{7,6},{8,9},{9,8},{10,11... | collective-permute-start | bytes 786440 | tf_op jit(solution)/shard_map/ppermute | solution.py:31
  22.1 11.6 %collective-permute-start.9 = (bf16[16,8192]{1,0:T(8,128)(2,1)S(1)}, bf16[16,8192]{1,0:T(8,128)(2,1)S(1)}, u32[]{:S(2)}, u32[]{:S(2)}) collective-permute-start(bf16[16,8192]{1,0:T(8,128)(2,1)S(1)} %collective-permute-done.7.refs_12_), channel_id=1, source_target_pairs={{0,4},{4,0},{8,12},{12,8},{1,5},{5,1},{9,13},{13,9},{2,6},{6,2},{1... | collective-permute-start | bytes 786440 | tf_op jit(solution)/shard_map/ppermute | solution.py:31
  23.3 12.2 %collective-permute-start.11 = (bf16[16,8192]{1,0:T(8,128)(2,1)S(1)}, bf16[16,8192]{1,0:T(8,128)(2,1)S(1)}, u32[]{:S(2)}, u32[]{:S(2)}) collective-permute-start(bf16[16,8192]{1,0:T(8,128)(2,1)S(1)} %collective-permute-done.7.refs_12_), channel_id=1, source_target_pairs={{0,8},{4,12},{8,0},{12,4},{1,9},{5,13},{9,1},{13,5},{2,10},{6,14},... | collective-permute-start | bytes 786440 | tf_op jit(solution)/shard_map/ppermute | solution.py:31
  30.4 11.1 %collective-permute-start.13 = (bf16[16,8192]{1,0:T(8,128)(2,1)S(1)}, bf16[16,8192]{1,0:T(8,128)(2,1)S(1)}, u32[]{:S(2)}, u32[]{:S(2)}) collective-permute-start(bf16[16,8192]{1,0:T(8,128)(2,1)S(1)} %collective-permute-done.7.refs_12_), channel_id=1, source_target_pairs={{0,12},{4,8},{8,4},{12,0},{1,13},{5,9},{9,5},{13,1},{2,14},{6,10},... | collective-permute-start | bytes 786440 | tf_op jit(solution)/shard_map/ppermute | solution.py:31
  43.1 20.6 %collective-permute-start.16 = (bf16[256,1024]{1,0:T(8,128)(2,1)}, bf16[256,1024]{1,0:T(8,128)(2,1)}, u32[]{:S(2)}, u32[]{:S(2)}) collective-permute-start(bf16[256,1024]{1,0:T(8,128)(2,1)} %refs_1_.3), channel_id=1, source_target_pairs={{0,2},{2,0},{1,3},{3,1},{4,6},{6,4},{5,7},{7,5},{8,10},{10,8},{9,1... | collective-permute-start | bytes 1572872 | tf_op jit(solution)/shard_map/ppermute | solution.py:31
  44.9 26.3 %all-to-all-start = ((bf16[8,4,16,1024]{3,2,1,0:T(8,128)(2,1)}), bf16[8,4,16,1024]{3,2,1,0:T(8,128)(2,1)}, u32[]{:S(2)}, u32[]{:S(2)}) async-start(bf16[8,4,16,1024]{3,2,1,0:T(8,128)(2,1)} %broadcast_in_dim.9), calls=%async_computation | async-start | bytes 2097152 | tf_op jit(solution)/shard_map/all_to_all | solution.py:26
  51.2 13.3 %collective-permute-start.20 = (bf16[256,1024]{1,0:T(8,128)(2,1)}, bf16[256,1024]{1,0:T(8,128)(2,1)}, u32[]{:S(2)}, u32[]{:S(2)}) collective-permute-start(bf16[256,1024]{1,0:T(8,128)(2,1)} %refs_1_.3), channel_id=1, source_target_pairs={{0,1},{1,0},{2,3},{3,2},{4,5},{5,4},{6,7},{7,6},{8,9},{9,8},{10,11... | collective-permute-start | bytes 1572872 | tf_op jit(solution)/shard_map/ppermute | solution.py:31
  64.3 15.4 %collective-permute-start.22 = (bf16[128,4096]{1,0:T(8,128)(2,1)}, bf16[128,4096]{1,0:T(8,128)(2,1)S(1)}, u32[]{:S(2)}, u32[]{:S(2)}) collective-permute-start(bf16[128,4096]{1,0:T(8,128)(2,1)} %get-tuple-element.56), channel_id=1, source_target_pairs={{0,1},{1,0},{2,3},{3,2},{4,5},{5,4},{6,7},{7,6},{8,9},{9,8},{10,11... | collective-permute-start | bytes 3145736 | tf_op jit(solution)/shard_map/ppermute | solution.py:31
  88.6 17.3 %collective-permute-start.32 = (bf16[8,16,1024]{2,1,0:T(8,128)(2,1)S(1)}, bf16[8,16,1024]{2,1,0:T(8,128)(2,1)S(1)}, u32[]{:S(2)}, u32[]{:S(2)}) collective-permute-start(bf16[8,16,1024]{2,1,0:T(8,128)(2,1)S(1)} %get-tuple-element.68), channel_id=1, source_target_pairs={{0,8},{4,12},{8,0},{12,4},{1,9},{5,13},{9,1},{13,5},{2,10},{6,14},... | collective-permute-start | bytes 786440 | tf_op jit(solution)/shard_map/ppermute | solution.py:31
  91.6 14.4 %collective-permute-start.33 = (bf16[8,16,1024]{2,1,0:T(8,128)(2,1)S(1)}, bf16[8,16,1024]{2,1,0:T(8,128)(2,1)S(1)}, u32[]{:S(2)}, u32[]{:S(2)}) collective-permute-start(bf16[8,16,1024]{2,1,0:T(8,128)(2,1)S(1)} %get-tuple-element.69), channel_id=1, source_target_pairs={{0,12},{4,8},{8,4},{12,0},{1,13},{5,9},{9,5},{13,1},{2,14},{6,10},... | collective-permute-start | bytes 786440 | tf_op jit(solution)/shard_map/ppermute | solution.py:31
  94.4 20.6 %collective-permute-start.24 = (bf16[16,8192]{1,0:T(8,128)(2,1)S(1)}, bf16[16,8192]{1,0:T(8,128)(2,1)S(1)}, u32[]{:S(2)}, u32[]{:S(2)}) collective-permute-start(bf16[16,8192]{1,0:T(8,128)(2,1)S(1)} %get-tuple-element.59), channel_id=1, source_target_pairs={{0,4},{4,0},{8,12},{12,8},{1,5},{5,1},{9,13},{13,9},{2,6},{6,2},{1... | collective-permute-start | bytes 786440 | tf_op jit(solution)/shard_map/ppermute | solution.py:31
  94.5 21.0 %collective-permute-start.25 = (bf16[16,8192]{1,0:T(8,128)(2,1)S(1)}, bf16[16,8192]{1,0:T(8,128)(2,1)S(1)}, u32[]{:S(2)}, u32[]{:S(2)}) collective-permute-start(bf16[16,8192]{1,0:T(8,128)(2,1)S(1)} %get-tuple-element.60), channel_id=1, source_target_pairs={{0,12},{4,8},{8,4},{12,0},{1,13},{5,9},{9,5},{13,1},{2,14},{6,10},... | collective-permute-start | bytes 786440 | tf_op jit(solution)/shard_map/ppermute | solution.py:31
  97.9 17.6 %collective-permute-start.30 = (bf16[16,8192]{1,0:T(8,128)(2,1)S(1)}, bf16[16,8192]{1,0:T(8,128)(2,1)S(1)}, u32[]{:S(2)}, u32[]{:S(2)}) collective-permute-start(bf16[16,8192]{1,0:T(8,128)(2,1)S(1)} %sum_of.8), channel_id=1, source_target_pairs={{0,2},{2,0},{1,3},{3,1},{4,6},{6,4},{5,7},{7,5},{8,10},{10,8},{9,1... | collective-permute-start | bytes 786440 | tf_op jit(solution)/shard_map/ppermute | solution.py:31
  106.0 11.2 %collective-permute-start.27 = (bf16[16,8192]{1,0:T(8,128)(2,1)S(1)}, bf16[16,8192]{1,0:T(8,128)(2,1)S(1)}, u32[]{:S(2)}, u32[]{:S(2)}) collective-permute-start(bf16[16,8192]{1,0:T(8,128)(2,1)S(1)} %sum_of.7), channel_id=1, source_target_pairs={{0,8},{4,12},{8,0},{12,4},{1,9},{5,13},{9,1},{13,5},{2,10},{6,14},... | collective-permute-start | bytes 786440 | tf_op jit(solution)/shard_map/ppermute | solution.py:31
  127.1 12.5 %collective-permute-start.35 = (bf16[8,16,1152]{2,1,0:T(8,128)(2,1)S(1)}, bf16[8,16,1152]{2,1,0:T(8,128)(2,1)S(1)}, u32[]{:S(2)}, u32[]{:S(2)}) collective-permute-start(bf16[8,16,1152]{2,1,0:T(8,128)(2,1)S(1)} %all_to_all.21.refs_0_), channel_id=1, source_target_pairs={{0,8},{4,12},{8,0},{12,4},{1,9},{5,13},{9,1},{13,5},{2,10},{6,14},... | collective-permute-start | bytes 884744 | tf_op jit(solution)/shard_map/ppermute | solution.py:31
  130.1 14.4 %collective-permute-start.36 = (bf16[8,16,1152]{2,1,0:T(8,128)(2,1)S(1)}, bf16[8,16,1152]{2,1,0:T(8,128)(2,1)S(1)}, u32[]{:S(2)}, u32[]{:S(2)}) collective-permute-start(bf16[8,16,1152]{2,1,0:T(8,128)(2,1)S(1)} %all_to_all.21.refs_0_), channel_id=1, source_target_pairs={{0,12},{4,8},{8,4},{12,0},{1,13},{5,9},{9,5},{13,1},{2,14},{6,10},... | collective-permute-start | bytes 884744 | tf_op jit(solution)/shard_map/ppermute | solution.py:31
  151.9 29.7 %collective-permute-start.44 = (bf16[256,1024]{1,0:T(8,128)(2,1)S(1)}, bf16[256,1024]{1,0:T(8,128)(2,1)S(1)}, u32[]{:S(2)}, u32[]{:S(2)}) collective-permute-start(bf16[256,1024]{1,0:T(8,128)(2,1)S(1)} %sum_of.12), channel_id=1, source_target_pairs={{0,2},{2,0},{1,3},{3,1},{4,6},{6,4},{5,7},{7,5},{8,10},{10,8},{9,1... | collective-permute-start | bytes 1572872 | tf_op jit(solution)/shard_map/ppermute | solution.py:31
  156.2 11.9 %collective-permute-start.39 = (bf16[2,4,16,1024]{3,2,1,0:T(8,128)(2,1)S(1)}, bf16[2,4,16,1024]{3,2,1,0:T(8,128)(2,1)S(1)}, u32[]{:S(2)}, u32[]{:S(2)}) collective-permute-start(bf16[2,4,16,1024]{3,2,1,0:T(8,128)(2,1)S(1)} %get-tuple-element.81), channel_id=1, source_target_pairs={{0,32},{32,0},{64,96},{96,64},{1,33},{33,1},{65,97},{97,65},{2,34}... | collective-permute-start | bytes 786440 | tf_op jit(solution)/shard_map/ppermute | solution.py:31
  156.8 13.8 %collective-permute-start.42 = (bf16[2,4,16,1024]{3,2,1,0:T(8,128)(2,1)S(1)}, bf16[2,4,16,1024]{3,2,1,0:T(8,128)(2,1)S(1)}, u32[]{:S(2)}, u32[]{:S(2)}) collective-permute-start(bf16[2,4,16,1024]{3,2,1,0:T(8,128)(2,1)S(1)} %get-tuple-element.86), channel_id=1, source_target_pairs={{0,96},{32,64},{64,32},{96,0},{1,97},{33,65},{65,33},{97,1},{2,98}... | collective-permute-start | bytes 786440 | tf_op jit(solution)/shard_map/ppermute | solution.py:31
  171.4 11.3 %all-to-all-start.3 = ((bf16[8,16,1024]{2,1,0:T(8,128)(2,1)}), bf16[8,16,1024]{2,1,0:T(8,128)(2,1)S(1)}, u32[]{:S(2)}, u32[]{:S(2)}) async-start(bf16[8,16,1024]{2,1,0:T(8,128)(2,1)} %bitcast.19), calls=%async_computation.3 | async-start | bytes 524288 | tf_op jit(solution)/shard_map/all_to_all | solution.py:26
  (31 other events, 264.9 us)

commit v4 on v3

--- a/solution.py
+++ b/solution.py
@@ -79,7 +79,7 @@
 def attention_kernel(n_shards, chunk, sc_ref, *refs):
     n_far = n_shards // 2
     far_refs = refs[:n_far]
-    wq_hbm, kva_hbm, kvb_hbm, wo_hbm, o_ref, other_ref, own_ref = refs[n_shards : n_shards + 7]
+    wq_hbm, kva_hbm, kvb_hbm, wo_hbm, other_ref, own_ref, o_ref = refs[n_shards : n_shards + 7]
     q_acc, kv_acc, wq_ref, kva_ref, kvb_ref, wo_ref, held_ref, sems, out_sem, held_sems = refs[
         n_shards + 7 :
     ]
@@ -107,8 +107,8 @@
     for step in range(steps):
         for copy in fetch(step):
             copy.start()
-    half_cols = own_ref.shape[1]
-    out_copy = pltpu.make_async_copy(wo_hbm.at[:, :half_cols], wo_ref, out_sem.at[0])
+    out_cols = own_ref.shape[1]
+    out_copy = pltpu.make_async_copy(wo_hbm, wo_ref, out_sem.at[0])
     out_copy.start()
     q_acc[...] = jnp.zeros_like(q_acc)
     kv_acc[...] = jnp.zeros_like(kv_acc)
@@ -159,7 +159,7 @@
         mixed = jnp.dot(weights, values, preferred_element_type=jnp.float32)
         o_ref[:, head] = mixed.astype(jnp.bfloat16)
     out_copy.wait()
-    for cut in (slice(i, i + 512) for i in range(0, half_cols, 512)):
+    for cut in (slice(i, i + 512) for i in range(0, out_cols, 512)):
         y = jnp.dot(o_ref[...], wo_ref[:, cut], preferred_element_type=jnp.float32)
         other_ref[:, cut] = y[:half].astype(jnp.bfloat16)
         own_ref[:, cut] = y[half:].astype(jnp.bfloat16)
@@ -171,26 +171,26 @@
     rows = per * n_shards
     cols = wq.shape[1]
     dh = kv_mine.shape[1]
-    half_cols = wo.shape[1] // 2
-    part = jax.ShapeDtypeStruct((rows // 2, half_cols), jnp.bfloat16)
+    part = jax.ShapeDtypeStruct((rows // 2, wo.shape[1]), jnp.bfloat16)
     return pl.pallas_call(
         functools.partial(attention_kernel, n_shards, chunk),
-        out_shape=(jax.ShapeDtypeStruct((rows, cols), jnp.bfloat16), part, part),
+        out_shape=(part, part),
         in_specs=[SM] + [FAR] * (n_shards // 2) + [VM] * (n_shards // 2) + [FAR] * 4,
-        out_specs=(VM,) * 3,
+        out_specs=(VM,) * 2,
         scratch_shapes=[
+            pltpu.VMEM((rows, cols), jnp.bfloat16),
             pltpu.VMEM((rows, cols), jnp.float32),
             pltpu.VMEM((rows, 4 * dh), jnp.float32),
             pltpu.VMEM(wq.shape, jnp.bfloat16),
             pltpu.VMEM(kv_mine.shape, jnp.bfloat16),
             pltpu.VMEM(kv_other.shape, jnp.bfloat16),
-            pltpu.VMEM((cols, half_cols), jnp.bfloat16),
+            pltpu.VMEM(wo.shape, jnp.bfloat16),
             pltpu.VMEM((rows // 2, depth), jnp.bfloat16),
             pltpu.SemaphoreType.DMA((3, depth // chunk)),
             pltpu.SemaphoreType.DMA((1,)),
             pltpu.SemaphoreType.DMA((n_shards // 2, depth // chunk)),
         ],
-        compiler_params=kernel_params(28),
+        compiler_params=kernel_params(32),
         cost_estimate=pl.CostEstimate(
             flops=2 * rows * depth * (cols + 4 * dh),
             bytes_accessed=2 * (rows * depth + depth * (cols + 4 * dh)),
@@ -198,48 +198,6 @@
         ),
         name="attention",
     )(scalars, *map(far, shards_in[: n_shards // 2]), *shards_in[n_shards // 2 :], far(wq), far(kv_mine), far(kv_other), far(wo))
-
-
-def project_kernel(base, chunk, m_ref, w_hbm, other_ref, own_ref, w_ref, sems):
-    half, cols = other_ref.shape
-    copies = []
-    for step in range(cols // chunk):
-        copies.append(
-            pltpu.make_async_copy(
-                w_hbm.at[:, base + step * chunk : base + (step + 1) * chunk],
-                w_ref.at[:, step * chunk : (step + 1) * chunk],
-                sems.at[step],
-            )
-        )
-        copies[-1].start()
-    for step, copy in enumerate(copies):
-        copy.wait()
-        cut = slice(step * chunk, (step + 1) * chunk)
-        y = jnp.dot(m_ref[...], w_ref[:, cut], preferred_element_type=jnp.float32)
-        other_ref[:, cut] = y[:half].astype(jnp.bfloat16)
-        own_ref[:, cut] = y[half:].astype(jnp.bfloat16)
-
-
-def project(mixed, w, base, cols, chunk=512):
-    rows, depth = mixed.shape
-    out = jax.ShapeDtypeStruct((rows // 2, cols), jnp.bfloat16)
-    return pl.pallas_call(
-        functools.partial(project_kernel, base, chunk),
-        out_shape=(out, out),
-        in_specs=[VM, FAR],
-        out_specs=(VM, VM),
-        scratch_shapes=[
-            pltpu.VMEM((depth, cols), jnp.bfloat16),
-            pltpu.SemaphoreType.DMA((cols // chunk,)),
-        ],
-        compiler_params=kernel_params(12),
-        cost_estimate=pl.CostEstimate(
-            flops=2 * rows * depth * cols,
-            bytes_accessed=2 * (rows * depth + depth * cols + rows * cols),
-            transcendentals=0,
-        ),
-        name="project",
-    )(mixed, far(w))
 
 
 def add_kernel(n, *refs):
@@ -522,7 +480,7 @@
     n_y = lax.axis_size("y")
     n_tp = lax.axis_size(TP)
     x = teacher_rows[0]
-    rows, width = x.shape
+    rows, _ = x.shape
     z = lax.axis_index("z").astype(jnp.int32)
     scalars = jnp.stack([core, xh, y, doc_start[0], z])
 
@@ -549,22 +507,17 @@
     n_tok = n_sec * n_y * rows
     tokens = tokens.reshape(n_tok, feats)
 
-    mixed, to_other, kept = attention(
+    proj.append(swap(proj[2], "c", 1))
+    to_other, kept = attention(
         scalars, other + own, query_weight[0], kv_mine, kv_other, output_weight[0]
     )
-
-    proj[2], mixed = tied(proj[2], mixed)
-    proj.append(swap(proj[2], "c", 1))
-    half = width // 2
-    sides = [(kept, to_other, swap(to_other, "c", 1))]
-
+    arrived = swap(to_other, "c", 1)
+
+    tokens, kept = tied(tokens, kept)
     keep, *sends = student_proj_part(scalars, tokens, proj, n_sec, n_y)
-    mixed, keep = tied(mixed, keep)
     got = [swap(sends[k - 1], "y", k) for k in range(1, n_y)]
-    to_other, kept = project(mixed, output_weight[0], half, half)
-    sides.append((kept, to_other, swap(to_other, "c", 1)))
-
-    pieces = add_pieces([s[0] for s in sides], [s[2] for s in sides], 2 * n_y)
+
+    pieces = add_pieces([kept], [arrived], 2 * n_y)
     near, away = list(pieces[:n_y]), list(pieces[n_y:])
     relayed = swap(away[2], "xh", 1)
     away = sum_of((away[0], swap(away[1], "y", 1), swap(away[3], "y", 3)), jnp.bfloat16)

time: 185 us -> 193 us (1.043)
  starting transfers between devices: 62.8 us -> 67 us
  local copies, waits for them, and re-layouts: 3.09 us -> 7.25 us
    unnamed x16 -> x28, local copies, waits for them, and re-layouts: 0.57 us -> 5.54 us
    ppermute x45 -> x44, starting transfers between devices: 53.8 us -> 58 us  [swap(): return lax.ppermute(value, axis, [(i, i ^ apart) for i in range(count)])]
    pallas_call x1 -> x0, Pallas kernels: 3.6 us -> none  [project(): pl.pallas_call(functools.partial(project_kernel, base, chunk), out_shape=...]
    all_to_all x2, waiting for transfers between devices: 6.78 us -> 9.68 us  [exchange(): return lax.all_to_all(pieces, axes, split_axis=0, concat_axis=0, tiled=True)]
    ppermute x45 -> x44, waiting for transfers between devices: 61.1 us -> 58.5 us  [swap(): return lax.ppermute(value, axis, [(i, i ^ apart) for i in range(count)])]
  transfers between devices with their start and end apart: 47 -> 46, of which waited for: 21 -> 22; matrix products, arithmetic and copies ran while one was open for 1% -> 1% of each run, Pallas kernels for 13% -> 6%
where the time goes in v4:
time: 193 us; the launch traced here: 192 us
  waiting for transfers between devices  68.1 us (35%)
  starting transfers between devices  67 us (35%)
  Pallas kernels  29.2 us (15%)
  blocking collectives  17.4 us (9%)
  local copies, waits for them, and re-layouts  7.25 us (4%)
  between operations  3.28 us (2%)
    ppermute x44, waiting for transfers between devices, swap(): return lax.ppermute(value, axis, [(i, i ^ apart) for i in range(count)])  58.5 us
    ppermute x44, starting transfers between devices, swap(): return lax.ppermute(value, axis, [(i, i ^ apart) for i in range(count)])  58 us
    all_to_all x2, blocking collectives, exchange(): return lax.all_to_all(pieces, axes, split_axis=0, concat_axis=0, tiled=True)  17.4 us
    pallas_call x1, Pallas kernels, attention(): pl.pallas_call(functools.partial(attention_kernel, n_shards, chunk), out_...  12.9 us
    all_to_all x2, waiting for transfers between devices, exchange(): return lax.all_to_all(pieces, axes, split_axis=0, concat_axis=0, tiled=True)  9.68 us
    all_to_all x2, starting transfers between devices, exchange(): return lax.all_to_all(pieces, axes, split_axis=0, concat_axis=0, tiled=True)  9.01 us
    unnamed x28, local copies, waits for them, and re-layouts  5.54 us
  transfers between devices with their start and end apart: 46, of which 22 were waited for; matrix products, arithmetic and copies ran while one was open for 1% of the time, Pallas kernels for 6%

profile of v4, /device:TPU:1, one launch (start us, length us, event | category | flops | bytes accessed | tf_op | source)
XLA Modules:
  0.0 192.3 jit_solution(3373234756966412591)
XLA Ops:
  3.3 2.9 %collective-permute-start.10 = (bf16[16,8192]{1,0:T(8,128)(2,1)S(1)}, bf16[16,8192]{1,0:T(8,128)(2,1)S(1)}, u32[]{:S(2)}, u32[]{:S(2)}) collective-permute-start(bf16[16,8192]{1,0:T(8,128)(2,1)S(1)} %normalize.1.refs_8_), channel_id=1, source_target_pairs={{0,2},{2,0},{1,3},{3,1},{4,6},{6,4},{5,7},{7,5},{8,10},{10,8},{9,1... | collective-permute-start | bytes 786440 | tf_op jit(solution)/shard_map/ppermute | solution.py:31
  7.5 2.6 %collective-permute-start.6 = (bf16[16,8192]{1,0:T(8,128)(2,1)S(1)}, bf16[16,8192]{1,0:T(8,128)(2,1)S(1)}, u32[]{:S(2)}, u32[]{:S(2)}) collective-permute-start(bf16[16,8192]{1,0:T(8,128)(2,1)S(1)} %normalize.1.refs_8_), channel_id=1, source_target_pairs={{0,8},{4,12},{8,0},{12,4},{1,9},{5,13},{9,1},{13,5},{2,10},{6,14},... | collective-permute-start | bytes 786440 | tf_op jit(solution)/shard_map/ppermute | solution.py:31
  15.1 6.8 %collective-permute-done.6.refs_10_ = bf16[16,8192]{1,0:T(8,128)(2,1)S(1)} collective-permute-done((bf16[16,8192]{1,0:T(8,128)(2,1)S(1)}, bf16[16,8192]{1,0:T(8,128)(2,1)S(1)}, u32[]{:S(2)}, u32[]{:S(2)}) %collective-permute-start.6) | collective-permute-done | bytes 262176 | tf_op jit(solution)/shard_map/ppermute | solution.py:31
  27.0 6.2 %collective-permute-done.14.refs_14_ = bf16[16,8192]{1,0:T(8,128)(2,1)S(1)} collective-permute-done((bf16[16,8192]{1,0:T(8,128)(2,1)S(1)}, bf16[16,8192]{1,0:T(8,128)(2,1)S(1)}, u32[]{:S(2)}, u32[]{:S(2)}) %collective-permute-start.14) | collective-permute-done | bytes 262176 | tf_op jit(solution)/shard_map/ppermute | solution.py:31
  34.4 3.9 %collective-permute-done.16.refs_15_ = bf16[16,8192]{1,0:T(8,128)(2,1)S(1)} collective-permute-done((bf16[16,8192]{1,0:T(8,128)(2,1)S(1)}, bf16[16,8192]{1,0:T(8,128)(2,1)S(1)}, u32[]{:S(2)}, u32[]{:S(2)}) %collective-permute-start.16) | collective-permute-done | bytes 262176 | tf_op jit(solution)/shard_map/ppermute | solution.py:31
  46.4 12.9 %attention.1 = (bf16[128,8192]{1,0:T(8,128)(2,1)}, bf16[128,8192]{1,0:T(8,128)(2,1)S(1)}) custom-call(s32[5]{0:T(128)S(1)} %stack.36.sc_ref, bf16[16,8192]{1,0:T(8,128)(2,1)} %copy-done.8, bf16[16,8192]{1,0:T(8,128)(2,1)} %copy-done.10, bf16[16,8192]{1,0:T(8,128)(2,1)} %copy-done.11, bf16[16,8192]{1,0:T(8,128)(2,1)} %copy-done.12, ...), custom_call_target="tpu_custom_call" | custom-call | flops 3221225472 | bytes 16777216 | tf_op jit(solution)/shard_map/attention/pallas_call | solution.py:175
  61.1 2.6 %collective-permute-start.2 = (bf16[16,1024]{1,0:T(8,128)(2,1)S(1)}, bf16[16,1024]{1,0:T(8,128)(2,1)S(1)}, u32[]{:S(2)}, u32[]{:S(2)}) collective-permute-start(bf16[16,1024]{1,0:T(8,128)(2,1)S(1)} %get-tuple-element.84), channel_id=1, source_target_pairs={{0,12},{4,8},{8,4},{12,0},{1,13},{5,9},{9,5},{13,1},{2,14},{6,10},... | collective-permute-start | bytes 98312 | tf_op jit(solution)/shard_map/ppermute | solution.py:31
  66.3 5.1 %all-to-all-start = ((bf16[8,4,16,1024]{3,2,1,0:T(8,128)(2,1)}), bf16[8,4,16,1024]{3,2,1,0:T(8,128)(2,1)}, u32[]{:S(2)}, u32[]{:S(2)}) async-start(bf16[8,4,16,1024]{3,2,1,0:T(8,128)(2,1)} %broadcast_in_dim.9), calls=%async_computation | async-start | bytes 2097152 | tf_op jit(solution)/shard_map/all_to_all | solution.py:26
  73.4 4.7 %collective-permute-done.28.refs_3_ = bf16[256,1024]{1,0:T(8,128)(2,1)} collective-permute-done((bf16[256,1024]{1,0:T(8,128)(2,1)}, bf16[256,1024]{1,0:T(8,128)(2,1)}, u32[]{:S(2)}, u32[]{:S(2)}) %collective-permute-start.28) | collective-permute-done | bytes 524320 | tf_op jit(solution)/shard_map/ppermute | solution.py:31
  78.1 3.2 %collective-permute-start.29 = (bf16[256,1024]{1,0:T(8,128)(2,1)}, bf16[256,1024]{1,0:T(8,128)(2,1)S(1)}, u32[]{:S(2)}, u32[]{:S(2)}) collective-permute-start(bf16[256,1024]{1,0:T(8,128)(2,1)} %collective-permute-done.28.refs_3_), channel_id=1, source_target_pairs={{0,1},{1,0},{2,3},{3,2},{4,5},{5,4},{6,7},{7,6},{8,9},{9,8},{10,11... | collective-permute-start | bytes 1572872 | tf_op jit(solution)/shard_map/ppermute | solution.py:31
  81.3 9.7 %all-to-all-done = bf16[8,4,16,1024]{3,2,1,0:T(8,128)(2,1)} async-done(((bf16[8,4,16,1024]{3,2,1,0:T(8,128)(2,1)}), bf16[8,4,16,1024]{3,2,1,0:T(8,128)(2,1)}, u32[]{:S(2)}, u32[]{:S(2)}) %all-to-all-start) | async-done | bytes 1048608 | tf_op jit(solution)/shard_map/all_to_all | solution.py:26
  95.9 3.4 %student_proj_part.1 = (f32[8,16,1024]{2,1,0:T(8,128)S(1)}, bf16[8,16,1024]{2,1,0:T(8,128)(2,1)S(1)}, bf16[8,16,1024]{2,1,0:T(8,128)(2,1)S(1)}, bf16[8,16,1024]{2,1,0:T(8,128)(2,1)S(1)}) custom-call(s32[5]{0:T(128)S(1)} %stack.36.sc_ref, bf16[512,1024]{1,0:T(8,128)(2,1)} %bitcast.7.refs_0_, bf16[256,1024]{1,0:T(8,128)(2,1)} %refs_1_.3, ...), custom_call_target="tpu_custom_call" | custom-call | flops 1073741824 | bytes 4194304 | tf_op jit(solution)/shard_map/student_proj_part/pallas_call | solution.py:337
  108.2 3.8 %collective-permute-done.31.refs_2_ = bf16[8,16,1024]{2,1,0:T(8,128)(2,1)S(1)} collective-permute-done((bf16[8,16,1024]{2,1,0:T(8,128)(2,1)S(1)}, bf16[8,16,1024]{2,1,0:T(8,128)(2,1)S(1)}, u32[]{:S(2)}, u32[]{:S(2)}) %collective-permute-start.31) | collective-permute-done | bytes 262176 | tf_op jit(solution)/shard_map/ppermute | solution.py:31
  114.3 8.5 %all_to_all.20.refs_6_ = bf16[8,16,1024]{2,1,0:T(8,128)(2,1)S(1)} all-to-all(bf16[8,16,1024]{2,1,0:T(8,128)(2,1)S(1)} %sum_of.9), channel_id=1, replica_groups=mesh['z'=4,'xl'=2,'y'=4,'xh'=2,'c'=2] {'z','xl'}, dimensions={0} | all-to-all | bytes 524288 | tf_op jit(solution)/shard_map/all_to_all | solution.py:26
  122.9 4.7 %collective-permute-done.21.refs_2_ = bf16[16,8192]{1,0:T(8,128)(2,1)S(1)} collective-permute-done((bf16[16,8192]{1,0:T(8,128)(2,1)S(1)}, bf16[16,8192]{1,0:T(8,128)(2,1)S(1)}, u32[]{:S(2)}, u32[]{:S(2)}) %collective-permute-start.21) | collective-permute-done | bytes 262176 | tf_op jit(solution)/shard_map/ppermute | solution.py:31
  128.6 8.9 %all_to_all.21.refs_0_ = bf16[8,16,1152]{2,1,0:T(8,128)(2,1)S(1)} all-to-all(bf16[8,16,1152]{2,1,0:T(8,128)(2,1)S(1)} %get-tuple-element.61), channel_id=1, replica_groups=mesh['z'=4,'xl'=2,'y'=4,'xh'=2,'c'=2] {'z','xl'}, dimensions={0} | all-to-all | bytes 589824 | tf_op jit(solution)/shard_map/all_to_all | solution.py:26
  138.1 3.3 %collective-permute-start.35 = (bf16[8,16,1152]{2,1,0:T(8,128)(2,1)S(1)}, bf16[8,16,1152]{2,1,0:T(8,128)(2,1)S(1)}, u32[]{:S(2)}, u32[]{:S(2)}) collective-permute-start(bf16[8,16,1152]{2,1,0:T(8,128)(2,1)S(1)} %all_to_all.21.refs_0_), channel_id=1, source_target_pairs={{0,12},{4,8},{8,4},{12,0},{1,13},{5,9},{9,5},{13,1},{2,14},{6,10},... | collective-permute-start | bytes 884744 | tf_op jit(solution)/shard_map/ppermute | solution.py:31
  145.4 3.1 %collective-permute-done.35.refs_3_ = bf16[8,16,1152]{2,1,0:T(8,128)(2,1)S(1)} collective-permute-done((bf16[8,16,1152]{2,1,0:T(8,128)(2,1)S(1)}, bf16[8,16,1152]{2,1,0:T(8,128)(2,1)S(1)}, u32[]{:S(2)}, u32[]{:S(2)}) %collective-permute-start.35) | collective-permute-done | bytes 294944 | tf_op jit(solution)/shard_map/ppermute | solution.py:31
  148.5 3.1 %gradients.1 = (f32[8,128]{1,0:T(8,128)S(1)}, bf16[256,1024]{1,0:T(8,128)(2,1)S(1)}, bf16[256,1024]{1,0:T(8,128)(2,1)S(1)}, f32[256,1024]{1,0:T(8,128)S(1)}, f32...) custom-call(s32[5]{0:T(128)S(1)} %stack.36.sc_ref, ...), custom_call_target="tpu_custom_call" | custom-call | tf_op jit(solution)/shard_map/gradients/pallas_call | solution.py:416
  151.6 7.6 %collective-permute-start.42 = (bf16[256,1024]{1,0:T(8,128)(2,1)S(1)}, bf16[256,1024]{1,0:T(8,128)(2,1)S(1)}, u32[]{:S(2)}, u32[]{:S(2)}) collective-permute-start(bf16[256,1024]{1,0:T(8,128)(2,1)S(1)} %get-tuple-element.79), channel_id=1, source_target_pairs={{0,1},{1,0},{2,3},{3,2},{4,5},{5,4},{6,7},{7,6},{8,9},{9,8},{10,11... | collective-permute-start | bytes 1572872 | tf_op jit(solution)/shard_map/ppermute | solution.py:31
  164.9 5.4 %collective-permute-done.39.refs_2_ = bf16[2,4,16,1024]{3,2,1,0:T(8,128)(2,1)S(1)} collective-permute-done((bf16[2,4,16,1024]{3,2,1,0:T(8,128)(2,1)S(1)}, bf16[2,4,16,1024]{3,2,1,0:T(8,128)(2,1)S(1)}, u32[]{:S(2)}, u32[]{:S(2)}) %collective-permute-start.39) | collective-permute-done | bytes 262176 | tf_op jit(solution)/shard_map/ppermute | solution.py:31
  170.3 4.1 %collective-permute-done.38.refs_1_ = bf16[2,4,16,1024]{3,2,1,0:T(8,128)(2,1)S(1)} collective-permute-done((bf16[2,4,16,1024]{3,2,1,0:T(8,128)(2,1)S(1)}, bf16[2,4,16,1024]{3,2,1,0:T(8,128)(2,1)S(1)}, u32[]{:S(2)}, u32[]{:S(2)}) %collective-permute-start.38) | collective-permute-done | bytes 262176 | tf_op jit(solution)/shard_map/ppermute | solution.py:31
  177.7 4.0 %all-to-all-start.3 = ((bf16[8,16,1024]{2,1,0:T(8,128)(2,1)}), bf16[8,16,1024]{2,1,0:T(8,128)(2,1)S(1)}, u32[]{:S(2)}, u32[]{:S(2)}) async-start(bf16[8,16,1024]{2,1,0:T(8,128)(2,1)} %bitcast.19), calls=%async_computation.3 | async-start | bytes 524288 | tf_op jit(solution)/shard_map/all_to_all | solution.py:26
  183.2 3.2 %collective-permute-start.37 = (f32[8,128]{1,0:T(8,128)S(1)}, f32[8,128]{1,0:T(8,128)S(1)}, u32[]{:S(2)}, u32[]{:S(2)}) collective-permute-start(f32[8,128]{1,0:T(8,128)S(1)} %add.22), channel_id=1, source_target_pairs={{0,2},{2,0},{1,3},{3,1},{4,6},{6,4},{5,7},{7,5},{8,10},{10,8},{9,1... | collective-permute-start | bytes 12296 | tf_op jit(solution)/shard_map/ppermute | solution.py:31
  (120 shorter events, 65.3 us)
Async XLA Ops:
  0.6 42.3 %collective-permute-start.18 = (bf16[2,64,8192]{2,1,0:T(8,128)(2,1)}, bf16[2,64,8192]{2,1,0:T(8,128)(2,1)}, u32[]{:S(2)}, u32[]{:S(2)}) collective-permute-start(bf16[2,64,8192]{2,1,0:T(8,128)(2,1)} %bitcast.30), channel_id=1, source_target_pairs={{0,1},{1,0},{2,3},{3,2},{4,5},{5,4},{6,7},{7,6},{8,9},{9,8},{10,11... | collective-permute-start | bytes 6291464 | tf_op jit(solution)/shard_map/ppermute | solution.py:31
  7.5 14.4 %collective-permute-start.6 = (bf16[16,8192]{1,0:T(8,128)(2,1)S(1)}, bf16[16,8192]{1,0:T(8,128)(2,1)S(1)}, u32[]{:S(2)}, u32[]{:S(2)}) collective-permute-start(bf16[16,8192]{1,0:T(8,128)(2,1)S(1)} %normalize.1.refs_8_), channel_id=1, source_target_pairs={{0,8},{4,12},{8,0},{12,4},{1,9},{5,13},{9,1},{13,5},{2,10},{6,14},... | collective-permute-start | bytes 786440 | tf_op jit(solution)/shard_map/ppermute | solution.py:31
  10.2 13.8 %collective-permute-start.8 = (bf16[16,8192]{1,0:T(8,128)(2,1)S(1)}, bf16[16,8192]{1,0:T(8,128)(2,1)S(1)}, u32[]{:S(2)}, u32[]{:S(2)}) collective-permute-start(bf16[16,8192]{1,0:T(8,128)(2,1)S(1)} %normalize.1.refs_8_), channel_id=1, source_target_pairs={{0,12},{4,8},{8,4},{12,0},{1,13},{5,9},{9,5},{13,1},{2,14},{6,10},... | collective-permute-start | bytes 786440 | tf_op jit(solution)/shard_map/ppermute | solution.py:31
  12.7 11.4 %collective-permute-start.3 = (bf16[16,8192]{1,0:T(8,128)(2,1)S(1)}, bf16[16,8192]{1,0:T(8,128)(2,1)S(1)}, u32[]{:S(2)}, u32[]{:S(2)}) collective-permute-start(bf16[16,8192]{1,0:T(8,128)(2,1)S(1)} %normalize.1.refs_8_), channel_id=1, source_target_pairs={{0,1},{1,0},{2,3},{3,2},{4,5},{5,4},{6,7},{7,6},{8,9},{9,8},{10,11... | collective-permute-start | bytes 786440 | tf_op jit(solution)/shard_map/ppermute | solution.py:31
  13.8 12.9 %collective-permute-start.12 = (bf16[16,8192]{1,0:T(8,128)(2,1)S(1)}, bf16[16,8192]{1,0:T(8,128)(2,1)S(1)}, u32[]{:S(2)}, u32[]{:S(2)}) collective-permute-start(bf16[16,8192]{1,0:T(8,128)(2,1)S(1)} %collective-permute-done.10.refs_12_), channel_id=1, source_target_pairs={{0,4},{4,0},{8,12},{12,8},{1,5},{5,1},{9,13},{13,9},{2,6},{6,2},{1... | collective-permute-start | bytes 786440 | tf_op jit(solution)/shard_map/ppermute | solution.py:31
  21.9 11.3 %collective-permute-start.14 = (bf16[16,8192]{1,0:T(8,128)(2,1)S(1)}, bf16[16,8192]{1,0:T(8,128)(2,1)S(1)}, u32[]{:S(2)}, u32[]{:S(2)}) collective-permute-start(bf16[16,8192]{1,0:T(8,128)(2,1)S(1)} %collective-permute-done.10.refs_12_), channel_id=1, source_target_pairs={{0,8},{4,12},{8,0},{12,4},{1,9},{5,13},{9,1},{13,5},{2,10},{6,14},... | collective-permute-start | bytes 786440 | tf_op jit(solution)/shard_map/ppermute | solution.py:31
  24.0 14.3 %collective-permute-start.16 = (bf16[16,8192]{1,0:T(8,128)(2,1)S(1)}, bf16[16,8192]{1,0:T(8,128)(2,1)S(1)}, u32[]{:S(2)}, u32[]{:S(2)}) collective-permute-start(bf16[16,8192]{1,0:T(8,128)(2,1)S(1)} %collective-permute-done.10.refs_12_), channel_id=1, source_target_pairs={{0,12},{4,8},{8,4},{12,0},{1,13},{5,9},{9,5},{13,1},{2,14},{6,10},... | collective-permute-start | bytes 786440 | tf_op jit(solution)/shard_map/ppermute | solution.py:31
  24.2 15.2 %collective-permute-start.11 = (bf16[16,8192]{1,0:T(8,128)(2,1)S(1)}, bf16[16,8192]{1,0:T(8,128)(2,1)S(1)}, u32[]{:S(2)}, u32[]{:S(2)}) collective-permute-start(bf16[16,8192]{1,0:T(8,128)(2,1)S(1)} %collective-permute-done.10.refs_12_), channel_id=1, source_target_pairs={{0,1},{1,0},{2,3},{3,2},{4,5},{5,4},{6,7},{7,6},{8,9},{9,8},{10,11... | collective-permute-start | bytes 786440 | tf_op jit(solution)/shard_map/ppermute | solution.py:31
  26.7 13.5 %collective-permute-start.5 = (bf16[16,8192]{1,0:T(8,128)(2,1)S(1)}, bf16[16,8192]{1,0:T(8,128)(2,1)S(1)}, u32[]{:S(2)}, u32[]{:S(2)}) collective-permute-start(bf16[16,8192]{1,0:T(8,128)(2,1)S(1)} %collective-permute-done.4.refs_9_), channel_id=1, source_target_pairs={{0,1},{1,0},{2,3},{3,2},{4,5},{5,4},{6,7},{7,6},{8,9},{9,8},{10,11... | collective-permute-start | bytes 786440 | tf_op jit(solution)/shard_map/ppermute | solution.py:31
  59.3 31.7 %collective-permute-start.19 = (bf16[128,8192]{1,0:T(8,128)(2,1)}, bf16[128,8192]{1,0:T(8,128)(2,1)}, u32[]{:S(2)}, u32[]{:S(2)}) collective-permute-start(bf16[128,8192]{1,0:T(8,128)(2,1)} %get-tuple-element.46), channel_id=1, source_target_pairs={{0,1},{1,0},{2,3},{3,2},{4,5},{5,4},{6,7},{7,6},{8,9},{9,8},{10,11... | collective-permute-start | bytes 6291464 | tf_op jit(solution)/shard_map/ppermute | solution.py:31
  63.8 14.4 %collective-permute-start.28 = (bf16[256,1024]{1,0:T(8,128)(2,1)}, bf16[256,1024]{1,0:T(8,128)(2,1)}, u32[]{:S(2)}, u32[]{:S(2)}) collective-permute-start(bf16[256,1024]{1,0:T(8,128)(2,1)} %refs_1_.3), channel_id=1, source_target_pairs={{0,2},{2,0},{1,3},{3,1},{4,6},{6,4},{5,7},{7,5},{8,10},{10,8},{9,1... | collective-permute-start | bytes 1572872 | tf_op jit(solution)/shard_map/ppermute | solution.py:31
  66.3 24.7 %all-to-all-start = ((bf16[8,4,16,1024]{3,2,1,0:T(8,128)(2,1)}), bf16[8,4,16,1024]{3,2,1,0:T(8,128)(2,1)}, u32[]{:S(2)}, u32[]{:S(2)}) async-start(bf16[8,4,16,1024]{3,2,1,0:T(8,128)(2,1)} %broadcast_in_dim.9), calls=%async_computation | async-start | bytes 2097152 | tf_op jit(solution)/shard_map/all_to_all | solution.py:26
  71.4 24.5 %collective-permute-start.27 = (bf16[256,1024]{1,0:T(8,128)(2,1)}, bf16[256,1024]{1,0:T(8,128)(2,1)}, u32[]{:S(2)}, u32[]{:S(2)}) collective-permute-start(bf16[256,1024]{1,0:T(8,128)(2,1)} %refs_1_.3), channel_id=1, source_target_pairs={{0,1},{1,0},{2,3},{3,2},{4,5},{5,4},{6,7},{7,6},{8,9},{9,8},{10,11... | collective-permute-start | bytes 1572872 | tf_op jit(solution)/shard_map/ppermute | solution.py:31
  78.1 17.7 %collective-permute-start.29 = (bf16[256,1024]{1,0:T(8,128)(2,1)}, bf16[256,1024]{1,0:T(8,128)(2,1)S(1)}, u32[]{:S(2)}, u32[]{:S(2)}) collective-permute-start(bf16[256,1024]{1,0:T(8,128)(2,1)} %collective-permute-done.28.refs_3_), channel_id=1, source_target_pairs={{0,1},{1,0},{2,3},{3,2},{4,5},{5,4},{6,7},{7,6},{8,9},{9,8},{10,11... | collective-permute-start | bytes 1572872 | tf_op jit(solution)/shard_map/ppermute | solution.py:31
  100.6 11.4 %collective-permute-start.31 = (bf16[8,16,1024]{2,1,0:T(8,128)(2,1)S(1)}, bf16[8,16,1024]{2,1,0:T(8,128)(2,1)S(1)}, u32[]{:S(2)}, u32[]{:S(2)}) collective-permute-start(bf16[8,16,1024]{2,1,0:T(8,128)(2,1)S(1)} %get-tuple-element.58), channel_id=1, source_target_pairs={{0,8},{4,12},{8,0},{12,4},{1,9},{5,13},{9,1},{13,5},{2,10},{6,14},... | collective-permute-start | bytes 786440 | tf_op jit(solution)/shard_map/ppermute | solution.py:31
  103.0 11.2 %collective-permute-start.32 = (bf16[8,16,1024]{2,1,0:T(8,128)(2,1)S(1)}, bf16[8,16,1024]{2,1,0:T(8,128)(2,1)S(1)}, u32[]{:S(2)}, u32[]{:S(2)}) collective-permute-start(bf16[8,16,1024]{2,1,0:T(8,128)(2,1)S(1)} %get-tuple-element.59), channel_id=1, source_target_pairs={{0,12},{4,8},{8,4},{12,0},{1,13},{5,9},{9,5},{13,1},{2,14},{6,10},... | collective-permute-start | bytes 786440 | tf_op jit(solution)/shard_map/ppermute | solution.py:31
  103.3 19.6 %collective-permute-start.20 = (bf16[16,8192]{1,0:T(8,128)(2,1)S(1)}, bf16[16,8192]{1,0:T(8,128)(2,1)S(1)}, u32[]{:S(2)}, u32[]{:S(2)}) collective-permute-start(bf16[16,8192]{1,0:T(8,128)(2,1)S(1)} %get-tuple-element.48), channel_id=1, source_target_pairs={{0,4},{4,0},{8,12},{12,8},{1,5},{5,1},{9,13},{13,9},{2,6},{6,2},{1... | collective-permute-start | bytes 786440 | tf_op jit(solution)/shard_map/ppermute | solution.py:31
  103.4 24.2 %collective-permute-start.21 = (bf16[16,8192]{1,0:T(8,128)(2,1)S(1)}, bf16[16,8192]{1,0:T(8,128)(2,1)S(1)}, u32[]{:S(2)}, u32[]{:S(2)}) collective-permute-start(bf16[16,8192]{1,0:T(8,128)(2,1)S(1)} %get-tuple-element.49), channel_id=1, source_target_pairs={{0,12},{4,8},{8,4},{12,0},{1,13},{5,9},{9,5},{13,1},{2,14},{6,10},... | collective-permute-start | bytes 786440 | tf_op jit(solution)/shard_map/ppermute | solution.py:31
  107.7 19.9 %collective-permute-start.26 = (bf16[16,8192]{1,0:T(8,128)(2,1)S(1)}, bf16[16,8192]{1,0:T(8,128)(2,1)S(1)}, u32[]{:S(2)}, u32[]{:S(2)}) collective-permute-start(bf16[16,8192]{1,0:T(8,128)(2,1)S(1)} %sum_of.8), channel_id=1, source_target_pairs={{0,2},{2,0},{1,3},{3,1},{4,6},{6,4},{5,7},{7,5},{8,10},{10,8},{9,1... | collective-permute-start | bytes 786440 | tf_op jit(solution)/shard_map/ppermute | solution.py:31
  112.0 15.6 %collective-permute-start.23 = (bf16[16,8192]{1,0:T(8,128)(2,1)S(1)}, bf16[16,8192]{1,0:T(8,128)(2,1)S(1)}, u32[]{:S(2)}, u32[]{:S(2)}) collective-permute-start(bf16[16,8192]{1,0:T(8,128)(2,1)S(1)} %sum_of.7), channel_id=1, source_target_pairs={{0,8},{4,12},{8,0},{12,4},{1,9},{5,13},{9,1},{13,5},{2,10},{6,14},... | collective-permute-start | bytes 786440 | tf_op jit(solution)/shard_map/ppermute | solution.py:31
  160.9 28.4 %collective-permute-start.43 = (bf16[256,1024]{1,0:T(8,128)(2,1)S(1)}, bf16[256,1024]{1,0:T(8,128)(2,1)S(1)}, u32[]{:S(2)}, u32[]{:S(2)}) collective-permute-start(bf16[256,1024]{1,0:T(8,128)(2,1)S(1)} %sum_of.12), channel_id=1, source_target_pairs={{0,2},{2,0},{1,3},{3,1},{4,6},{6,4},{5,7},{7,5},{8,10},{10,8},{9,1... | collective-permute-start | bytes 1572872 | tf_op jit(solution)/shard_map/ppermute | solution.py:31
  162.4 11.9 %collective-permute-start.38 = (bf16[2,4,16,1024]{3,2,1,0:T(8,128)(2,1)S(1)}, bf16[2,4,16,1024]{3,2,1,0:T(8,128)(2,1)S(1)}, u32[]{:S(2)}, u32[]{:S(2)}) collective-permute-start(bf16[2,4,16,1024]{3,2,1,0:T(8,128)(2,1)S(1)} %get-tuple-element.71), channel_id=1, source_target_pairs={{0,32},{32,0},{64,96},{96,64},{1,33},{33,1},{65,97},{97,65},{2,34}... | collective-permute-start | bytes 786440 | tf_op jit(solution)/shard_map/ppermute | solution.py:31
  163.0 13.9 %collective-permute-start.41 = (bf16[2,4,16,1024]{3,2,1,0:T(8,128)(2,1)S(1)}, bf16[2,4,16,1024]{3,2,1,0:T(8,128)(2,1)S(1)}, u32[]{:S(2)}, u32[]{:S(2)}) collective-permute-start(bf16[2,4,16,1024]{3,2,1,0:T(8,128)(2,1)S(1)} %get-tuple-element.76), channel_id=1, source_target_pairs={{0,96},{32,64},{64,32},{96,0},{1,97},{33,65},{65,33},{97,1},{2,98}... | collective-permute-start | bytes 786440 | tf_op jit(solution)/shard_map/ppermute | solution.py:31
  177.7 12.7 %all-to-all-start.3 = ((bf16[8,16,1024]{2,1,0:T(8,128)(2,1)}), bf16[8,16,1024]{2,1,0:T(8,128)(2,1)S(1)}, u32[]{:S(2)}, u32[]{:S(2)}) async-start(bf16[8,16,1024]{2,1,0:T(8,128)(2,1)} %bitcast.19), calls=%async_computation.3 | async-start | bytes 524288 | tf_op jit(solution)/shard_map/all_to_all | solution.py:26
  (36 other events, 220.2 us)
